TPU v7x, 32 devices: a whole 2x2x4 slice. The times are simulated.
32 devices in a mesh: seq: 2 (over y), blk: 16 (over z, x, core).
Axes of the slice: x: 2, y: 2, z: 4, core: 2. Of those that a mesh axis runs over, the one named last changes fastest.
Arguments:
- residual: bfloat16 [16, 256, 1024], P('blk', 'seq'), may hold values from -6 to 6
- segments: int32 [4096], replicated, may hold values from 0 to 15, never falling along the last dimension, each value on 1 to 512 neighbouring positions
- routes: int32 [16, 256, 8], P('blk', 'seq'), may hold values from 0 to 15, all different within a row; in each aligned block of 128 rows (0 to 127, 128 to 255, ..., all dimensions but the last counted through in order) at most 96 rows name the same one
- w_query: bfloat16 [1024, 1024], P(('seq', 'blk')), may hold values from -0.1875 to 0.1875
- w_key: bfloat16 [1024, 512], P(('seq', 'blk')), may hold values from -0.1875 to 0.1875
- w_value: bfloat16 [1024, 512], P(('seq', 'blk')), may hold values from -0.1875 to 0.1875
- w_out: bfloat16 [1024, 1024], P(None, ('seq', 'blk')), may hold values from -0.75 to 0.75
- w_router: bfloat16 [1024, 16], P(('seq', 'blk')), may hold values from -0.09375 to 0.09375
- attn_gain: bfloat16 [1024], P(('seq', 'blk')), may hold values from 0.5 to 1.5
- moe_gain: bfloat16 [1024], P(('seq', 'blk')), may hold values from 0.5 to 1.5
- w_gate: bfloat16 [16, 1024, 512], P('blk', 'seq'), may hold values from -0.1875 to 0.1875
- w_up: bfloat16 [16, 1024, 512], P('blk', 'seq'), may hold values from -0.1875 to 0.1875
- w_down: bfloat16 [16, 512, 1024], P('blk', 'seq'), may hold values from -1 to 1
- cotangent: bfloat16 [16, 256, 1024], P('blk', 'seq'), may hold values from -6 to 6
Outputs:
- block_out: bfloat16 [16, 256, 1024], P('blk', 'seq')
- grad_input: float32 [16, 256, 1024], P('blk', 'seq')
- grad_query: float32 [1024, 1024], P(('seq', 'blk'))
- grad_key: float32 [1024, 512], P(('seq', 'blk'))
- grad_value: float32 [1024, 512], P(('seq', 'blk'))
- grad_out: float32 [1024, 1024], P(None, ('seq', 'blk'))
- grad_router: float32 [1024, 16], P(('seq', 'blk'))
- grad_attn_gain: float32 [1024], P(('seq', 'blk'))
- grad_moe_gain: float32 [1024], P(('seq', 'blk'))
- grad_gate: float32 [16, 1024, 512], P('blk', 'seq')
- grad_up: float32 [16, 1024, 512], P('blk', 'seq')
- grad_down: float32 [16, 512, 1024], P('blk', 'seq')
Inputs may be any that keep to these rules, and one draw needn't show every extreme that they name: `routes`: among the 128 consecutive tokens of one device no expert is named by more than 96 tokens, a bound that some block reaches. `segments`: document numbers never fall along the sequence; each document has 1 to 512 tokens and one has exactly 512.
All inputs are finite; a program needn't handle non-finite values.
Results may differ from a plain program's by a relative error of at most 0.02.
Values may be sent and summed in bfloat16 or wider, within the bound.
No kernel may reach another device: no remote copies, remote signals or barrier semaphores. Data moves between devices by JAX's collectives and lax.ppermute only.
A program may use at most 128 MiB of HBM per device.

v0:
```python
import math

import jax
import jax.numpy as jnp
from jax import lax
from jax.sharding import PartitionSpec as P

HEADS = 16
KV_HEADS = 8
HEAD_DIM = 64
TOP = 8


highest = lax.Precision.HIGHEST
epsilon = 1e-06
neg_large = -1e30


def shifted(value, axis, steps):
    count = lax.axis_size(axis)
    leading, last = (max(0, -steps), min(count, count - steps))
    return lax.ppermute(value, axis, [(source, source + steps) for source in range(leading, last)])


def passed_along(value, axis, by):
    devices = lax.axis_size(axis)
    return lax.ppermute(value, axis, [(i, (i + by) % devices) for i in range(devices)])


def rope_tables(positions, width):
    half_dim = width // 2
    inverse = jnp.exp(jnp.arange(half_dim, dtype=jnp.float32) * (-2.0 * math.log(10000.0) / width))
    angles = positions.astype(jnp.float32)[:, None] * inverse[None, :]
    return (jnp.cos(angles), jnp.sin(angles))


def rotate(vector, cos_part, sin_part):
    half_dim = vector.shape[-1] // 2
    first_half = vector[..., :half_dim]
    second = vector[..., half_dim:]
    cos_b = cos_part[:, None, :]
    sin_b = sin_part[:, None, :]
    return jnp.concatenate(
        [first_half * cos_b - second * sin_b, second * cos_b + first_half * sin_b], axis=-1
    )


def rotate_back(gradient, cos_part, sin_part):
    half_dim = gradient.shape[-1] // 2
    first_half = gradient[..., :half_dim]
    second = gradient[..., half_dim:]
    cos_b = cos_part[:, None, :]
    sin_b = sin_part[:, None, :]
    return jnp.concatenate(
        [first_half * cos_b + second * sin_b, second * cos_b - first_half * sin_b], axis=-1
    )


def norm_parts(stream, gain):
    inverse = lax.rsqrt(jnp.mean(stream * stream, axis=-1, keepdims=True) + epsilon)
    normed = stream * inverse
    return (normed * gain, normed, inverse)


def norm_back(grad_after, normed, inverse, gain):
    scaled = grad_after * gain
    grad_before = inverse * (scaled - normed * jnp.mean(scaled * normed, axis=-1, keepdims=True))
    return (grad_before, jnp.sum(grad_after * normed, axis=0))


def per_device(
    residual,
    segments,
    routes,
    w_query,
    w_key,
    w_value,
    w_out,
    w_router,
    attn_gain,
    moe_gain,
    w_gate,
    w_up,
    w_down,
    cotangent,
):
    seq_count = lax.axis_size("seq")
    blk_count = lax.axis_size("blk")
    seq_index = lax.axis_index("seq")
    blk_index = lax.axis_index("blk")
    tok_count = residual.shape[1]
    row_count = tok_count * seq_count
    group_size = HEADS // KV_HEADS
    q_local = HEADS // seq_count
    kv_local = KV_HEADS // seq_count
    kv_cols = kv_local * 2 * HEAD_DIM
    score_scale = HEAD_DIM ** (-0.5)
    turns = blk_count - 1
    query_full, key_full, value_full, out_full, router_full, gain_one, gain_two = (
        lax.all_gather(w_query, ("seq", "blk"), axis=0, tiled=True),
        lax.all_gather(w_key, ("seq", "blk"), axis=0, tiled=True),
        lax.all_gather(w_value, ("seq", "blk"), axis=0, tiled=True),
        lax.all_gather(w_out, ("seq", "blk"), axis=1, tiled=True),
        lax.all_gather(w_router, ("seq", "blk"), axis=0, tiled=True),
        lax.all_gather(attn_gain, ("seq", "blk"), axis=0, tiled=True),
        lax.all_gather(moe_gain, ("seq", "blk"), axis=0, tiled=True),
    )
    gate_full, up_full, down_full = (
        lax.all_gather(w_gate, "seq", axis=1, tiled=True),
        lax.all_gather(w_up, "seq", axis=1, tiled=True),
        lax.all_gather(w_down, "seq", axis=1, tiled=True),
    )
    gate_full = gate_full[0]
    up_full = up_full[0]
    down_full = down_full[0]
    gain_one = gain_one.astype(jnp.float32)
    gain_two = gain_two.astype(jnp.float32)
    stream = residual[0].astype(jnp.float32)
    normed_one, unit_one, inv_one = norm_parts(stream, gain_one)
    normed_attn = normed_one.astype(jnp.bfloat16)
    positions = (
        blk_index * row_count + seq_index * tok_count + jnp.arange(tok_count, dtype=jnp.int32)
    )
    cos_part, sin_part = rope_tables(positions, HEAD_DIM)
    q_pre = jnp.dot(normed_attn, query_full, preferred_element_type=jnp.float32).reshape(
        tok_count, HEADS, HEAD_DIM
    )
    k_pre = jnp.dot(normed_attn, key_full, preferred_element_type=jnp.float32).reshape(
        tok_count, KV_HEADS, HEAD_DIM
    )
    v_tok = (
        jnp.dot(normed_attn, value_full, preferred_element_type=jnp.float32)
        .astype(jnp.bfloat16)
        .reshape(tok_count, KV_HEADS, HEAD_DIM)
    )
    q_tok = (
        rotate(q_pre, cos_part, sin_part).astype(jnp.bfloat16).reshape(tok_count, HEADS * HEAD_DIM)
    )
    k_tok = rotate(k_pre, cos_part, sin_part).astype(jnp.bfloat16)
    kv_tok = jnp.stack([k_tok, v_tok], axis=2).reshape(tok_count, KV_HEADS * 2 * HEAD_DIM)
    q_rows, kv_own = (
        lax.all_to_all(q_tok, "seq", split_axis=1, concat_axis=0, tiled=True),
        lax.all_to_all(kv_tok, "seq", split_axis=1, concat_axis=0, tiled=True),
    )
    q_rows = q_rows.reshape(row_count, kv_local, group_size, HEAD_DIM)
    row_ids = jnp.arange(row_count, dtype=jnp.int32)
    seg_blocks = segments.reshape(blk_count, row_count)
    seg_query = lax.dynamic_index_in_dim(seg_blocks, blk_index, 0, keepdims=False)

    def scores_for(kv_block, source):
        split_kv = kv_block.reshape(row_count, kv_local, 2, HEAD_DIM)
        key_part = split_kv[:, :, 0]
        value_part = split_kv[:, :, 1]
        raw_scores = (
            jnp.einsum("qhgd,khd->qhgk", q_rows, key_part, preferred_element_type=jnp.float32)
            * score_scale
        )
        seg_key = lax.dynamic_index_in_dim(seg_blocks, source, 0, keepdims=False)
        visible = (
            (source * row_count + row_ids)[None, :] <= (blk_index * row_count + row_ids)[:, None]
        ) & (seg_key[None, :] == seg_query[:, None])
        return (raw_scores, visible[:, None, None, :], key_part, value_part)

    def forward_step(soft_state, kv_block, source):

        def forward_work(current):
            running_max, running_sum, weighted = current
            raw_scores, visible, key_part, value_part = scores_for(kv_block, source)
            masked = jnp.where(visible, raw_scores, neg_large)
            new_max = jnp.maximum(running_max, jnp.max(masked, axis=-1))
            weights = jnp.where(visible, jnp.exp(masked - new_max[..., None]), 0.0)
            shrink = jnp.exp(running_max - new_max)
            running_sum = running_sum * shrink + jnp.sum(weights, axis=-1)
            weighted = weighted * shrink[..., None] + jnp.einsum(
                "qhgk,khd->qhgd",
                weights.astype(jnp.bfloat16),
                value_part,
                preferred_element_type=jnp.float32,
            )
            return (new_max, running_sum, weighted)

        return lax.cond(source <= blk_index, forward_work, lambda unchanged: unchanged, soft_state)

    soft_state = (
        jnp.full((row_count, kv_local, group_size), neg_large, jnp.float32),
        jnp.zeros((row_count, kv_local, group_size), jnp.float32),
        jnp.zeros((row_count, kv_local, group_size, HEAD_DIM), jnp.float32),
    )
    kept_blocks = jnp.zeros((1, 1), jnp.bfloat16)

    def cycle_turn(turn_index, carry):
        state_now, kv_block, kept_now = carry
        source = (blk_index - turn_index) % blk_count
        state_now = forward_step(state_now, kv_block, source)
        kv_block = shifted(kv_block, "blk", 1)
        return (state_now, kv_block, kept_now)

    soft_state, last_block, kept_blocks = lax.fori_loop(
        0, turns, cycle_turn, (soft_state, kv_own, kept_blocks)
    )
    last_source = (blk_index - turns) % blk_count
    soft_state = forward_step(soft_state, last_block, last_source)
    running_max, running_sum, weighted = soft_state
    row_lse = running_max + jnp.log(running_sum)
    mixed_rows = (weighted / running_sum[..., None]).astype(jnp.bfloat16)
    mixed_tok = lax.all_to_all(
        mixed_rows.reshape(row_count, q_local * HEAD_DIM),
        "seq",
        split_axis=0,
        concat_axis=1,
        tiled=True,
    )
    middle = stream + jnp.dot(mixed_tok, out_full, preferred_element_type=jnp.float32)
    normed_two, unit_two, inv_two = norm_parts(middle, gain_two)
    normed_moe = normed_two.astype(jnp.bfloat16)
    expert_count = router_full.shape[1]
    capacity = 3 * tok_count * TOP // (2 * expert_count)
    chosen = (
        routes[0][:, :, None] == jnp.arange(expert_count, dtype=jnp.int32)[None, None, :]
    ).astype(jnp.float32)
    member = jnp.sum(chosen, axis=1)
    token_ids = jnp.arange(tok_count, dtype=jnp.int32)
    earlier = (token_ids[:, None] > token_ids[None, :]).astype(jnp.float32)
    slot_rank = jnp.dot(earlier, member, precision=highest)
    slot_hit = member.T[:, None, :] * (
        slot_rank.T[:, None, :] == jnp.arange(capacity, dtype=jnp.float32)[None, :, None]
    ).astype(jnp.float32)
    dispatch = slot_hit.astype(jnp.bfloat16)
    logits = jnp.dot(normed_moe, router_full, preferred_element_type=jnp.float32)
    picked = jnp.einsum("tke,te->tk", chosen, logits, precision=highest)
    gate_prob = jax.nn.softmax(picked, axis=-1)
    gate_table = jnp.einsum("tk,tke->te", gate_prob, chosen, precision=highest)
    gate_slot = jnp.einsum("ect,te->ec", slot_hit, gate_table, precision=highest)
    outgoing = jnp.einsum(
        "ect,td->ecd", dispatch, normed_moe, preferred_element_type=jnp.float32
    ).astype(jnp.bfloat16)
    received = lax.all_to_all(outgoing, "blk", split_axis=0, concat_axis=0, tiled=True)
    gate_pre = jnp.einsum("scd,df->scf", received, gate_full, preferred_element_type=jnp.float32)
    up_pre = jnp.einsum("scd,df->scf", received, up_full, preferred_element_type=jnp.float32)
    hidden = (jax.nn.silu(gate_pre) * up_pre).astype(jnp.bfloat16)
    result = jnp.einsum(
        "scf,fd->scd", hidden, down_full, preferred_element_type=jnp.float32
    ).astype(jnp.bfloat16)
    returned = lax.all_to_all(result, "blk", split_axis=0, concat_axis=0, tiled=True)
    returned, received, gate_pre, up_pre = (returned, received, gate_pre, up_pre)
    per_expert = jnp.einsum("ect,ecd->ted", dispatch, returned, preferred_element_type=jnp.float32)
    final = middle + jnp.sum(gate_table[:, :, None] * per_expert, axis=1)
    block_out = final.astype(jnp.bfloat16)[None]
    grad_final = cotangent[0].astype(jnp.float32)
    grad_table = jnp.sum(per_expert * grad_final[:, None, :], axis=-1)
    routed_grad = jnp.einsum(
        "ect,td->ecd", dispatch, cotangent[0], preferred_element_type=jnp.float32
    )
    grad_slots = (gate_slot[:, :, None] * routed_grad).astype(jnp.bfloat16)
    grad_received = lax.all_to_all(grad_slots, "blk", split_axis=0, concat_axis=0, tiled=True)
    sigmoid = jax.nn.sigmoid(gate_pre)
    activated = gate_pre * sigmoid
    hidden = (activated * up_pre).astype(jnp.bfloat16)
    grad_down = jnp.einsum("scf,scd->fd", hidden, grad_received, preferred_element_type=jnp.float32)
    grad_hidden = jnp.einsum(
        "scd,fd->scf", grad_received, down_full, preferred_element_type=jnp.float32
    )
    grad_gate_pre = (grad_hidden * up_pre * sigmoid * (1.0 + gate_pre * (1.0 - sigmoid))).astype(
        jnp.bfloat16
    )
    grad_up_pre = (grad_hidden * activated).astype(jnp.bfloat16)
    grad_gate = jnp.einsum(
        "scd,scf->df", received, grad_gate_pre, preferred_element_type=jnp.float32
    )
    grad_up = jnp.einsum("scd,scf->df", received, grad_up_pre, preferred_element_type=jnp.float32)
    grad_inputs = (
        jnp.einsum("scf,df->scd", grad_gate_pre, gate_full, preferred_element_type=jnp.float32)
        + jnp.einsum("scf,df->scd", grad_up_pre, up_full, preferred_element_type=jnp.float32)
    ).astype(jnp.bfloat16)
    grad_back = lax.all_to_all(grad_inputs, "blk", split_axis=0, concat_axis=0, tiled=True)
    grad_normed_moe = jnp.einsum(
        "ect,ecd->td", dispatch, grad_back, preferred_element_type=jnp.float32
    )
    grad_picked = jnp.einsum("te,tke->tk", grad_table, chosen, precision=highest)
    grad_pick = gate_prob * (grad_picked - jnp.sum(gate_prob * grad_picked, axis=-1, keepdims=True))
    grad_logits = jnp.einsum("tk,tke->te", grad_pick, chosen, precision=highest)
    router_wide = router_full.astype(jnp.float32)
    grad_normed_moe = grad_normed_moe + jnp.dot(grad_logits, router_wide.T, precision=highest)
    grad_router = jnp.dot(normed_moe.astype(jnp.float32).T, grad_logits, precision=highest)
    grad_middle_part, grad_gain_two = norm_back(grad_normed_moe, unit_two, inv_two, gain_two)
    grad_middle = grad_final + grad_middle_part
    grad_branch = grad_middle.astype(jnp.bfloat16)
    grad_out = jnp.dot(mixed_tok.T, grad_branch, preferred_element_type=jnp.float32)
    grad_mixed_tok = jnp.dot(grad_branch, out_full.T, preferred_element_type=jnp.float32).astype(
        jnp.bfloat16
    )
    grad_mixed = lax.all_to_all(
        grad_mixed_tok, "seq", split_axis=1, concat_axis=0, tiled=True
    ).reshape(row_count, kv_local, group_size, HEAD_DIM)
    row_delta = jnp.sum(grad_mixed.astype(jnp.float32) * mixed_rows.astype(jnp.float32), axis=-1)

    def back_step(grad_pair, kv_block, source):

        def back_work(current):
            grad_queries, grad_kv = current
            raw_scores, visible, key_part, value_part = scores_for(kv_block, source)
            probability = jnp.exp(jnp.where(visible, raw_scores - row_lse[..., None], neg_large))
            grad_values = jnp.einsum(
                "qhgk,qhgd->khd",
                probability.astype(jnp.bfloat16),
                grad_mixed,
                preferred_element_type=jnp.float32,
            )
            grad_probs = jnp.einsum(
                "qhgd,khd->qhgk", grad_mixed, value_part, preferred_element_type=jnp.float32
            )
            grad_scores = (probability * (grad_probs - row_delta[..., None])).astype(jnp.bfloat16)
            grad_queries = (
                grad_queries
                + jnp.einsum(
                    "qhgk,khd->qhgd", grad_scores, key_part, preferred_element_type=jnp.float32
                )
                * score_scale
            )
            grad_keys = (
                jnp.einsum(
                    "qhgk,qhgd->khd", grad_scores, q_rows, preferred_element_type=jnp.float32
                )
                * score_scale
            )
            grad_kv = grad_kv + jnp.stack([grad_keys, grad_values], axis=2).reshape(
                row_count, kv_cols
            )
            return (grad_queries, grad_kv)

        return lax.cond(source <= blk_index, back_work, lambda unchanged: unchanged, grad_pair)

    def send_back(moving):
        return (
            passed_along(moving[0], "blk", 1),
            passed_along(moving[1].astype(jnp.bfloat16), "blk", 1).astype(jnp.float32),
        )

    grad_pair = (
        jnp.zeros((row_count, kv_local, group_size, HEAD_DIM), jnp.float32),
        jnp.zeros((row_count, kv_cols), jnp.float32),
    )

    def back_turn(turn_index, carry):
        pair_now, kv_block = carry
        source = (blk_index - turn_index) % blk_count
        grad_queries, grad_kv = back_step(pair_now, kv_block, source)
        kv_next, grad_next = send_back((kv_block, grad_kv))
        return ((grad_queries, grad_next), kv_next)

    grad_pair, final_block = lax.fori_loop(0, turns, back_turn, (grad_pair, kv_own))
    grad_queries, grad_kv = back_step(grad_pair, final_block, last_source)
    grad_kv = passed_along(grad_kv.astype(jnp.bfloat16), "blk", -turns).astype(grad_kv.dtype)
    grad_q_tok, grad_kv_tok = (
        lax.all_to_all(
            grad_queries.astype(jnp.bfloat16).reshape(row_count, q_local * HEAD_DIM),
            "seq",
            split_axis=0,
            concat_axis=1,
            tiled=True,
        ),
        lax.all_to_all(
            grad_kv.astype(jnp.bfloat16), "seq", split_axis=0, concat_axis=1, tiled=True
        ),
    )
    grad_kv_tok = grad_kv_tok.reshape(tok_count, KV_HEADS, 2, HEAD_DIM)
    grad_q_pre = rotate_back(
        grad_q_tok.reshape(tok_count, HEADS, HEAD_DIM).astype(jnp.float32), cos_part, sin_part
    )
    grad_q_pre = grad_q_pre.astype(jnp.bfloat16).reshape(tok_count, HEADS * HEAD_DIM)
    grad_k_pre = rotate_back(grad_kv_tok[:, :, 0].astype(jnp.float32), cos_part, sin_part)
    grad_k_pre = grad_k_pre.astype(jnp.bfloat16).reshape(tok_count, KV_HEADS * HEAD_DIM)
    grad_v_pre = grad_kv_tok[:, :, 1].reshape(tok_count, KV_HEADS * HEAD_DIM)
    grad_query = jnp.dot(normed_attn.T, grad_q_pre, preferred_element_type=jnp.float32)
    grad_key = jnp.dot(normed_attn.T, grad_k_pre, preferred_element_type=jnp.float32)
    grad_value = jnp.dot(normed_attn.T, grad_v_pre, preferred_element_type=jnp.float32)
    grad_normed_attn = (
        jnp.dot(grad_q_pre, query_full.T, preferred_element_type=jnp.float32)
        + jnp.dot(grad_k_pre, key_full.T, preferred_element_type=jnp.float32)
        + jnp.dot(grad_v_pre, value_full.T, preferred_element_type=jnp.float32)
    )
    grad_stream_part, grad_gain_one = norm_back(grad_normed_attn, unit_one, inv_one, gain_one)
    grad_input = (grad_middle + grad_stream_part)[None]
    shard_query, shard_key, shard_value, shard_out, shard_router, shard_gain_one, shard_gain_two = (
        lax.psum_scatter(grad_query, ("seq", "blk"), scatter_dimension=0, tiled=True),
        lax.psum_scatter(grad_key, ("seq", "blk"), scatter_dimension=0, tiled=True),
        lax.psum_scatter(grad_value, ("seq", "blk"), scatter_dimension=0, tiled=True),
        lax.psum_scatter(grad_out, ("seq", "blk"), scatter_dimension=1, tiled=True),
        lax.psum_scatter(grad_router, ("seq", "blk"), scatter_dimension=0, tiled=True),
        lax.psum_scatter(grad_gain_one, ("seq", "blk"), scatter_dimension=0, tiled=True),
        lax.psum_scatter(grad_gain_two, ("seq", "blk"), scatter_dimension=0, tiled=True),
    )
    shard_gate, shard_up, shard_down = (
        lax.psum_scatter(
            grad_gate[None].astype(jnp.bfloat16), "seq", scatter_dimension=1, tiled=True
        ).astype(jnp.float32),
        lax.psum_scatter(
            grad_up[None].astype(jnp.bfloat16), "seq", scatter_dimension=1, tiled=True
        ).astype(jnp.float32),
        lax.psum_scatter(
            grad_down[None].astype(jnp.bfloat16), "seq", scatter_dimension=1, tiled=True
        ).astype(jnp.float32),
    )
    return (
        block_out,
        grad_input,
        shard_query,
        shard_key,
        shard_value,
        shard_out,
        shard_router,
        shard_gain_one,
        shard_gain_two,
        shard_gate,
        shard_up,
        shard_down,
    )


def solution(mesh):
    return jax.shard_map(
        per_device,
        mesh=mesh,
        in_specs=(
            P("blk", "seq", None),
            P(),
            P("blk", "seq", None),
            P(("seq", "blk"), None),
            P(("seq", "blk"), None),
            P(("seq", "blk"), None),
            P(None, ("seq", "blk")),
            P(("seq", "blk"), None),
            P(("seq", "blk")),
            P(("seq", "blk")),
            P("blk", "seq", None),
            P("blk", "seq", None),
            P("blk", "seq", None),
            P("blk", "seq", None),
        ),
        out_specs=(
            P("blk", "seq", None),
            P("blk", "seq", None),
            P(("seq", "blk"), None),
            P(("seq", "blk"), None),
            P(("seq", "blk"), None),
            P(None, ("seq", "blk")),
            P(("seq", "blk"), None),
            P(("seq", "blk")),
            P(("seq", "blk")),
            P("blk", "seq", None),
            P("blk", "seq", None),
            P("blk", "seq", None),
        ),
        check_vma=False,
    )
```

profile of v0, /device:TPU:0, one launch (start us, length us, event | category | flops | bytes accessed | tf_op | source)
XLA Modules:
  0.0 1602.5 jit_solution(6602029202706272126)
XLA Ops:
  12.5 42.1 %all-reduce.5 = (bf16[1024]{0:T(1024)(128)(2,1)S(1)}, bf16[1024]{0:T(1024)(128)(2,1)S(1)}) all-reduce(bf16[1024]{0:T(1024)(128)(2,1)S(1)} %dynamic-update-slice, bf16[1024]{0:T(1024)(128)(2,1)S(1)} %dynamic-update-slice.1), channel_id=1, replica_groups=mesh['seq'=2,'blk'=16] {'seq','blk'}, use_global_device_ids=true, to_apply=%add | all-reduce | flops 2048 | bytes 8192
  55.9 12.4 all-gather.9.cloned.1.call-done
  69.8 53.9 %all-gather.11.cloned.1.call-done = bf16[1024,512]{1,0:T(8,128)(2,1)} async-done(((bf16[32,512]{1,0:T(8,128)(2,1)}), bf16[1024,512]{1,0:T(8,128)(2,1)}) %all-gather.11.cloned.1.call-update) | async-done | bytes 1048592 | tf_op jit(solution)/shard_map/all_gather | solution.py:102
  130.2 51.8 %all-gather.13.cloned.1.call-done = bf16[1024,1024]{1,0:T(8,128)(2,1)} async-done(((bf16[32,1024]{1,0:T(8,128)(2,1)}), bf16[1024,1024]{1,0:T(8,128)(2,1)}) %all-gather.13.cloned.1.call-update) | async-done | bytes 2097168 | tf_op jit(solution)/shard_map/all_gather | solution.py:100
  196.9 129.2 %while.44 = (s32[]{:T(128)}, f32[256,4,2]{0,2,1:T(2,128)S(1)}, f32[256,4,2]{0,2,1:T(2,128)S(1)}, f32[256,4,2,64]{0,3,2,1:T(8,128)S(1)}, bf16[256,512]{0,1:T(8,12...) while((s32[]{:T(128)}, f32[256,4,2]{0,2,1:T(2,128)S(1)}, ...), condition=%wide.region_6.7_spmd.clone.clone, body=%wide.region_1.6_spmd.clone.clone.sunk | while | flops 141496848 | bytes 9842178 | solution.py:198
  226.7 10.2 collective-permute-start
  330.4 51.4 %all-gather = bf16[32,32,16]{1,2,0:T(8,128)(2,1)S(1)} all-gather(bf16[1,32,16]{1,2,0:T(8,128)(2,1)S(1)} %bitcast.482), channel_id=1, replica_groups=mesh['seq'=2,'blk'=16] {'seq','blk'}, dimensions={0}, use_global_device_ids=true | all-gather | bytes 33792 | tf_op jit(solution)/shard_map/all_gather | solution.py:104
  396.9 55.3 %all-to-all-done.3 = bf16[16,96,1024]{2,1,0:T(8,128)(2,1)} async-done(((bf16[16,96,1024]{2,1,0:T(8,128)(2,1)}), bf16[16,96,1024]{2,1,0:T(8,128)(2,1)}, u32[]{:S(2)}, u32[]{:S(2)}) %all-to-all-start.3) | async-done | bytes 3145760 | tf_op jit(solution)/shard_map/all_to_all | solution.py:237
  452.2 15.4 all-to-all-start.5
  469.4 21.8 %all-gather.19.cloned.1.call-done = bf16[1,1024,512]{2,1,0:T(8,128)(2,1)} async-done(((bf16[1,512,512]{2,1,0:T(8,128)(2,1)}), bf16[1,1024,512]{2,1,0:T(8,128)(2,1)}) %all-gather.19.cloned.1.call-update) | async-done | bytes 1048592 | tf_op jit(solution)/shard_map/all_gather | solution.py:110
  496.9 17.0 %all-gather.17.cloned.1.call-done = bf16[1,1024,512]{2,1,0:T(8,128)(2,1)} async-done(((bf16[1,512,512]{2,1,0:T(8,128)(2,1)}), bf16[1,1024,512]{2,1,0:T(8,128)(2,1)}) %all-gather.17.cloned.1.call-update) | async-done | bytes 1048592 | tf_op jit(solution)/shard_map/all_gather | solution.py:109
  519.5 16.9 %all-gather.21.cloned.1.call-done = bf16[1,512,1024]{2,1,0:T(8,128)(2,1)} async-done(((bf16[1,256,1024]{2,1,0:T(8,128)(2,1)}), bf16[1,512,1024]{2,1,0:T(8,128)(2,1)}) %all-gather.21.cloned.1.call-update) | async-done | bytes 1048592 | tf_op jit(solution)/shard_map/all_gather | solution.py:111
  536.4 8.8 multiply_convert_fusion.1
  563.7 52.0 %all-to-all-done.4 = bf16[16,96,1024]{2,1,0:T(8,128)(2,1)} async-done(((bf16[16,96,1024]{2,1,0:T(8,128)(2,1)}), bf16[16,96,1024]{2,1,0:T(8,128)(2,1)}, u32[]{:S(2)}, u32[]{:S(2)}) %all-to-all-start.4) | async-done | bytes 3145760 | tf_op jit(solution)/shard_map/all_to_all | solution.py:244
  615.8 15.5 all-to-all-start.6
  649.8 40.9 %all-to-all-done.6 = bf16[16,96,1024]{2,1,0:T(8,128)(2,1)} async-done(((bf16[16,96,1024]{2,1,0:T(8,128)(2,1)}), bf16[16,96,1024]{2,1,0:T(8,128)(2,1)}, u32[]{:S(2)}, u32[]{:S(2)}) %all-to-all-start.6) | async-done | bytes 3145760 | tf_op jit(solution)/shard_map/all_to_all | solution.py:275
  706.8 184.1 %while.45 = (s32[]{:T(128)}, f32[256,4,2,64]{0,3,2,1:T(8,128)S(1)}, f32[256,512]{0,1:T(8,128)S(1)}, bf16[256,512]{0,1:T(8,128)(2,1)S(1)}, s32[]{:T(128)}, /*inde...) while((s32[]{:T(128)}, f32[256,4,2,64]{0,3,2,1:T(8,128)S(1)}, ...), condition=%wide.region_23.24_spmd.clone.clone, body=%wide.region_20.23_spmd.clone.clone.sunk | while | flops 340394496 | bytes 21524036 | solution.py:351
  714.7 12.3 collective-permute-done.1
  932.8 109.8 %reduce-scatter.25.cloned.1.call-done = f32[32,16]{1,0:T(8,128)} async-done(((f32[1024,16]{1,0:T(8,128)}), f32[32,16]{1,0:T(8,128)}) %reduce-scatter.25.cloned.1.call-update) | async-done | bytes 2064
  1046.4 37.1 %all-reduce.4 = (f32[1024]{0:T(1024)S(1)}, f32[1024]{0:T(1024)S(1)}) all-reduce(f32[1024]{0:T(1024)S(1)} %get-tuple-element.1014, f32[1024]{0:T(1024)S(1)} %copy-done.25), channel_id=7, replica_groups=mesh['seq'=2,'blk'=16] {'seq','blk'}, use_global_device_ids=true, to_apply=%region_33.34.clone | all-reduce | flops 2048 | bytes 16384
  1085.8 92.6 %reduce-scatter.13.cloned.1.call-done = f32[32,512]{1,0:T(8,128)} async-done(((f32[1024,512]{1,0:T(8,128)}), f32[32,512]{1,0:T(8,128)}) %reduce-scatter.13.cloned.1.call-update) | async-done | bytes 65552 | tf_op jit(solution)/shard_map/reduce_scatter | solution.py:386
  1178.3 135.8 %reduce-scatter.15.cloned.1.call-done = f32[32,512]{1,0:T(8,128)} async-done(((f32[1024,512]{1,0:T(8,128)}), f32[32,512]{1,0:T(8,128)}) %reduce-scatter.15.cloned.1.call-update) | async-done | bytes 65552 | tf_op jit(solution)/shard_map/reduce_scatter | solution.py:387
  1314.1 140.3 %reduce-scatter.17.cloned.1.call-done = f32[1024,32]{0,1:T(8,128)} async-done(((f32[1024,1024]{0,1:T(8,128)}), f32[1024,32]{0,1:T(8,128)}) %reduce-scatter.17.cloned.1.call-update) | async-done | bytes 131088 | tf_op jit(solution)/shard_map/reduce_scatter | solution.py:388
  1454.4 140.4 %reduce-scatter.11.cloned.1.call-done = f32[32,1024]{1,0:T(8,128)} async-done(((f32[1024,1024]{1,0:T(8,128)}), f32[32,1024]{1,0:T(8,128)}) %reduce-scatter.11.cloned.1.call-update) | async-done | bytes 131088 | tf_op jit(solution)/shard_map/reduce_scatter | solution.py:385
  (462 shorter events, 456.5 us)
Async XLA Ops:
  8.0 60.3 %all-gather.9.cloned.1.call-start = ((), (), s32[]{:S(2)}) async-start(), calls=%async_computation.18 | async-start | bytes 1081344 | tf_op jit(solution)/shard_map/all_gather | solution.py:101
  8.8 115.0 %all-gather.11.cloned.1.call-start = ((), (), s32[]{:S(2)}) async-start(), calls=%async_computation.19 | async-start | bytes 1081344 | tf_op jit(solution)/shard_map/all_gather | solution.py:102
  9.5 172.5 %all-gather.13.cloned.1.call-start = ((), (), s32[]{:S(2)}) async-start(), calls=%async_computation.20 | async-start | bytes 2162688 | tf_op jit(solution)/shard_map/all_gather | solution.py:100
  10.2 371.8 %all-gather.15.cloned.1.call-start = ((), (), s32[]{:S(2)}) async-start(), calls=%async_computation.21 | async-start | bytes 2162688 | tf_op jit(solution)/shard_map/all_gather | solution.py:103
  126.8 59.8 %all-to-all-start = ((bf16[128,2,512]{0,2,1:T(8,128)(2,1)}), bf16[128,2,512]{0,2,1:T(8,128)(2,1)S(1)}, u32[]{:S(2)}, u32[]{:S(2)}) async-start(bf16[128,2,512]{0,2,1:T(8,128)(2,1)} %bitcast.60), calls=%async_computation | async-start | bytes 524288 | tf_op jit(solution)/shard_map/all_to_all | solution.py:143
  226.7 11.5 collective-permute-start
  326.9 55.2 %all-to-all-start.2 = ((bf16[2,128,512]{1,2,0:T(8,128)(2,1)}), bf16[2,128,512]{1,2,0:T(8,128)(2,1)S(1)}, u32[]{:S(2)}, u32[]{:S(2)}) async-start(bf16[2,128,512]{1,2,0:T(8,128)(2,1)} %copy.207), calls=%async_computation.2 | async-start | bytes 524288 | tf_op jit(solution)/shard_map/all_to_all | solution.py:206
  388.1 64.1 %all-to-all-start.3 = ((bf16[16,96,1024]{2,1,0:T(8,128)(2,1)}), bf16[16,96,1024]{2,1,0:T(8,128)(2,1)}, u32[]{:S(2)}, u32[]{:S(2)}) async-start(bf16[16,96,1024]{2,1,0:T(8,128)(2,1)} %convolution_convert_fusion), calls=%async_computation.3 | async-start | bytes 6291456 | tf_op jit(solution)/shard_map/all_to_all | solution.py:237
  452.2 84.2 %all-to-all-start.5 = ((bf16[16,96,1024]{2,1,0:T(8,128)(2,1)}), bf16[16,96,1024]{2,1,0:T(8,128)(2,1)}, u32[]{:S(2)}, u32[]{:S(2)}) async-start(bf16[16,96,1024]{2,1,0:T(8,128)(2,1)} %multiply_convert_fusion), calls=%async_computation.5 | async-start | bytes 6291456 | tf_op jit(solution)/shard_map/all_to_all | solution.py:255
  467.7 23.5 %all-gather.19.cloned.1.call-start = ((), (), s32[]{:S(2)}) async-start(), calls=%async_computation.23 | async-start | bytes 1572864 | tf_op jit(solution)/shard_map/all_gather | solution.py:110
  468.3 45.5 %all-gather.17.cloned.1.call-start = ((), (), s32[]{:S(2)}) async-start(), calls=%async_computation.22 | async-start | bytes 1572864 | tf_op jit(solution)/shard_map/all_gather | solution.py:109
  468.9 67.6 %all-gather.21.cloned.1.call-start = ((), (), s32[]{:S(2)}) async-start(), calls=%async_computation.24 | async-start | bytes 1572864 | tf_op jit(solution)/shard_map/all_gather | solution.py:111
  550.0 65.8 %all-to-all-start.4 = ((bf16[16,96,1024]{2,1,0:T(8,128)(2,1)}), bf16[16,96,1024]{2,1,0:T(8,128)(2,1)}, u32[]{:S(2)}, u32[]{:S(2)}) async-start(bf16[16,96,1024]{2,1,0:T(8,128)(2,1)} %convolution_convert_fusion.1), calls=%async_computation.4 | async-start | bytes 6291456 | tf_op jit(solution)/shard_map/all_to_all | solution.py:244
  615.8 74.9 %all-to-all-start.6 = ((bf16[16,96,1024]{2,1,0:T(8,128)(2,1)}), bf16[16,96,1024]{2,1,0:T(8,128)(2,1)}, u32[]{:S(2)}, u32[]{:S(2)}) async-start(bf16[16,96,1024]{2,1,0:T(8,128)(2,1)} %add_convert_fusion), calls=%async_computation.6 | async-start | bytes 6291456 | tf_op jit(solution)/shard_map/all_to_all | solution.py:275
  631.3 295.0 %reduce-scatter.23.cloned.1.call-start = ((), (), s32[]{:S(2)}) async-start(), calls=%async_computation.31 | async-start | bytes 1572864 | tf_op jit(solution)/shard_map/reduce_scatter | solution.py:400
  636.5 292.0 %reduce-scatter.19.cloned.1.call-start = ((), (), s32[]{:S(2)}) async-start(), calls=%async_computation.29 | async-start | bytes 1572864 | tf_op jit(solution)/shard_map/reduce_scatter | solution.py:394
  700.0 230.7 %reduce-scatter.21.cloned.1.call-start = ((), (), s32[]{:S(2)}) async-start(), calls=%async_computation.30 | async-start | bytes 1572864 | tf_op jit(solution)/shard_map/reduce_scatter | solution.py:397
  709.7 17.2 %collective-permute-start.1 = (bf16[256,512]{0,1:T(8,128)(2,1)S(1)}, bf16[256,512]{0,1:T(8,128)(2,1)S(1)}, u32[]{:S(2)}, u32[]{:S(2)}) collective-permute-start(bf16[256,512]{0,1:T(8,128)(2,1)S(1)} %convert_element_type.446), channel_id=1, source_target_pairs={{0,1},{1,2},{2,3},{3,4},{4,5},{5,6},{6,7},{7,8},{8,9},{9,10},{10,1... | collective-permute-start | bytes 786440 | tf_op jit(solution)/shard_map/while/body/eval_jaxpr/ppermute | solution.py:27
  709.8 20.0 %collective-permute-start.2 = (bf16[256,512]{0,1:T(8,128)(2,1)S(1)}, bf16[256,512]{0,1:T(8,128)(2,1)S(1)}, u32[]{:S(2)}, u32[]{:S(2)}) collective-permute-start(bf16[256,512]{0,1:T(8,128)(2,1)S(1)} %copy.320), channel_id=1, source_target_pairs={{0,1},{1,2},{2,3},{3,4},{4,5},{5,6},{6,7},{7,8},{8,9},{9,10},{10,1... | collective-permute-start | bytes 786440 | tf_op jit(solution)/shard_map/while/body/eval_jaxpr/ppermute | solution.py:27
  903.2 139.5 %reduce-scatter.25.cloned.1.call-start = ((), (), s32[]{:S(2)}) async-start(), calls=%async_computation.32 | async-start | bytes 540672
  904.5 273.8 %reduce-scatter.13.cloned.1.call-start = ((), (), s32[]{:S(2)}) async-start(), calls=%async_computation.26 | async-start | bytes 2162688 | tf_op jit(solution)/shard_map/reduce_scatter | solution.py:386
  910.6 403.5 %reduce-scatter.15.cloned.1.call-start = ((), (), s32[]{:S(2)}) async-start(), calls=%async_computation.27 | async-start | bytes 2162688 | tf_op jit(solution)/shard_map/reduce_scatter | solution.py:387
  912.6 541.8 %reduce-scatter.17.cloned.1.call-start = ((), (), s32[]{:S(2)}) async-start(), calls=%async_computation.28 | async-start | bytes 4325376 | tf_op jit(solution)/shard_map/reduce_scatter | solution.py:388
  915.4 679.3 %reduce-scatter.11.cloned.1.call-start = ((), (), s32[]{:S(2)}) async-start(), calls=%async_computation.25 | async-start | bytes 4325376 | tf_op jit(solution)/shard_map/reduce_scatter | solution.py:385
  (76 other events, 1289.9 us)
Sparse Core Ops, SparseCore 0:
  11.7 56.5 all-gather.8
  71.1 52.5 all-gather.10
  126.6 55.4 all-gather.12
  184.7 60.2 all-gather.14
Sparse Core Ops, SparseCore 1:
  469.7 21.5 all-gather.18
  492.6 21.1 all-gather.16
  515.2 21.1 all-gather.20
  636.6 20.5 reduce-scatter.22
  660.1 20.2 reduce-scatter.18
  705.6 31.4 reduce-scatter.20
  906.6 136.1 reduce-scatter.24
  1045.4 132.9 reduce-scatter.12
  1181.1 132.9 reduce-scatter.14
  1317.0 137.3 reduce-scatter.16
  1457.1 137.6 reduce-scatter.10
where the time goes:
time: 1610 us; the launch traced here: 1600 us
  waiting for transfers between devices  1150 us (71%)
  starting transfers between devices  163 us (10%)
  blocking collectives  138 us (9%)
  matrix products  85.9 us (5%)
  local copies, waits for them, and re-layouts  28.4 us (2%)
  between operations  16.9 us (1%)
    ppermute x31, waiting for transfers between devices, passed_along(): lax.ppermute(value, axis, [(i, (i + by) % devices) for i in range(devices)])  180 us
    reduce_scatter x1, waiting for transfers between devices, per_device(): lax.psum_scatter(grad_query, ('seq', 'blk'), scatter_dimension=0, tiled=T...  140 us
    reduce_scatter x1, waiting for transfers between devices, per_device(): lax.psum_scatter(grad_out, ('seq', 'blk'), scatter_dimension=1, tiled=True)  140 us
    reduce_scatter x1, waiting for transfers between devices, per_device(): lax.psum_scatter(grad_value, ('seq', 'blk'), scatter_dimension=0, tiled=T...  136 us
    unnamed x16, waiting for transfers between devices  114 us
    ppermute x15, starting transfers between devices, shifted(): lax.ppermute(value, axis, [(source, source + steps) for source in range(l...  95.9 us
    reduce_scatter x1, waiting for transfers between devices, per_device(): lax.psum_scatter(grad_key, ('seq', 'blk'), scatter_dimension=0, tiled=True)  92.6 us
    unnamed x2, blocking collectives  79.2 us
  transfers between devices with their start and end apart: 70, of which 62 were waited for; matrix products, arithmetic and copies ran while one was open for 7% of the time, Pallas kernels for 0%

commit v1 on v0

v1 whole, which is shorter than its diff:
```python
import functools
import math

import jax
import jax.numpy as jnp
from jax import lax
from jax.experimental import pallas as pl
from jax.experimental.pallas import tpu as pltpu
from jax.sharding import PartitionSpec as P

HEADS = 16
KV_HEADS = 8
HEAD_DIM = 64
LANES = 128

f32 = jnp.float32
bf16 = jnp.bfloat16
epsilon = 1e-06
neg_large = -1e30


def swap_with(value, axis, mask):
    if mask == 0:
        return value
    count = lax.axis_size(axis)
    return lax.ppermute(value, axis, [(i, i ^ mask) for i in range(count)])


def shifted(value, axis, steps):
    count = lax.axis_size(axis)
    leading, last = (max(0, -steps), min(count, count - steps))
    return lax.ppermute(value, axis, [(i, i + steps) for i in range(leading, last)])


def gather_seq(value):
    count = lax.axis_size("seq")
    me = lax.axis_index("seq")
    whole = jnp.zeros((count,) + value.shape, value.dtype)
    for k in range(count):
        piece = swap_with(value, "seq", k)
        whole = lax.dynamic_update_index_in_dim(whole, piece, me ^ k, 0)
    return whole


def exchange_seq(parts):
    count = lax.axis_size("seq")
    me = lax.axis_index("seq")
    return [
        swap_with(lax.dynamic_index_in_dim(parts, me ^ k, 0, keepdims=False), "seq", k)
        for k in range(count)
    ]


def in_seq_order(pieces):
    me = lax.axis_index("seq")
    whole = jnp.zeros((len(pieces),) + pieces[0].shape, pieces[0].dtype)
    for k, piece in enumerate(pieces):
        whole = lax.dynamic_update_index_in_dim(whole, piece, me ^ k, 0)
    return whole


def gather_blk(value):
    groups = lax.axis_size("blk") // 4
    chunks = []
    for k in range(groups):
        far = swap_with(value, "blk", 4 * k)
        pair = jnp.stack([far, swap_with(far, "blk", 2)])
        chunks.append((pair, swap_with(pair, "blk", 1)))
    return chunks


def reduce_chunk(k, keep, send):
    total = (keep.astype(f32) + swap_with(send, "blk", 1).astype(f32)).astype(keep.dtype)
    near = (total[0].astype(f32) + swap_with(total[1], "blk", 2).astype(f32)).astype(keep.dtype)
    return swap_with(near, "blk", 4 * k)


def reduce_blk(terms):
    groups = lax.axis_size("blk") // 4
    total = None
    for k in reversed(range(groups)):
        piece = reduce_chunk(k, terms[4 * k : 4 * k + 2], terms[4 * k + 2 : 4 * k + 4]).astype(f32)
        total = piece if total is None else total + piece
    return total


def call(body, out_shape, **options):
    return pl.pallas_call(
        body,
        out_shape=out_shape,
        compiler_params=pltpu.CompilerParams(vmem_limit_bytes=40 * 1024 * 1024),
        **options,
    )


def shape_of(dims, dtype):
    return jax.ShapeDtypeStruct(dims, dtype)


def lane_ids(shape):
    return lax.broadcasted_iota(jnp.int32, shape, len(shape) - 1)


def half_swap(tile):
    lanes = lane_ids(tile.shape)
    return jnp.where(lanes % 64 < 32, pltpu.roll(tile, 96, 1), pltpu.roll(tile, 32, 1))


def nt(a, b):
    return lax.dot_general(a, b, (((1,), (1,)), ((), ())), preferred_element_type=f32)


def tn(a, b):
    return lax.dot_general(a, b, (((0,), (0,)), ((), ())), preferred_element_type=f32)


def nn(a, b):
    return jnp.dot(a, b, preferred_element_type=f32)


def project_body(q_cols, kv_cols, gain_lane, x_ref, w_ref, cq, sq, ck, sk, q_ref, kv_ref, normed_ref):
    x = x_ref[...].astype(f32)
    inverse = lax.rsqrt(jnp.mean(x * x, axis=-1, keepdims=True) + epsilon)
    cols = q_cols + kv_cols
    pick = (lane_ids((8, LANES)) == gain_lane).astype(bf16)
    gain = nt(pick, w_ref[:, cols : cols + LANES])[0:1, :]
    normed = (x * inverse * gain).astype(bf16)
    normed_ref[...] = normed
    for first in range(0, cols, LANES):
        tile = nn(normed, w_ref[:, first : first + LANES])
        if first < q_cols:
            tile = tile * cq[...] + half_swap(tile) * sq[...]
            q_ref[:, first : first + LANES] = tile.astype(bf16)
        else:
            tile = tile * ck[...] + half_swap(tile) * sk[...]
            kv_ref[:, first - q_cols : first - q_cols + LANES] = tile.astype(bf16)


def visible_keys(rows, keys, behind, first_row, seg_q, seg_k):
    key_ids = lax.broadcasted_iota(jnp.int32, (rows, keys), 1) - behind
    row_ids = lax.broadcasted_iota(jnp.int32, (rows, keys), 0) + first_row
    return (key_ids <= row_ids) & (seg_q == seg_k)


def attend_body(behind, scale, q_ref, kv_ref, seg_q, seg_k, out_ref, lse_ref):
    rows, keys = q_ref.shape[0], kv_ref.shape[0]
    visible = visible_keys(rows, keys, behind, pl.program_id(1) * rows, seg_q[...], seg_k[...])
    q = q_ref[...]
    kv = kv_ref[...]
    low = lane_ids(q.shape) < 64
    outs, lses = [], []
    for half in range(2):
        turned = (pltpu.roll(q.astype(f32), 64, 1) if half else q.astype(f32))
        head = jnp.where(low, turned, 0.0).astype(bf16)
        scores = jnp.where(visible, nt(head, kv) * scale, neg_large)
        most = jnp.max(scores, axis=-1, keepdims=True)
        weights = jnp.exp(scores - most)
        total = jnp.sum(weights, axis=-1, keepdims=True)
        outs.append(nn(weights.astype(bf16), kv) / total)
        lses.append(most + jnp.log(total))
    out_ref[...] = jnp.where(low, pltpu.roll(outs[0], 64, 1), outs[1]).astype(bf16)
    lse_ref[...] = jnp.where(low, lses[0], lses[1])


def attend_back_body(
    behind, scale, q_ref, kv_ref, mixed_ref, grad_ref, lse_ref, seg_q, seg_k, cq, sq, dq_ref, dkv_ref
):
    rows, keys = q_ref.shape[0], kv_ref.shape[0]
    visible = visible_keys(rows, keys, behind, pl.program_id(1) * rows, seg_q[...], seg_k[...])
    q = q_ref[...].astype(f32)
    kv = kv_ref[...]
    grad = grad_ref[...].astype(f32)
    low = lane_ids(q.shape) < 64
    product = grad * mixed_ref[...].astype(f32)
    lse = lse_ref[...]
    dqs = []
    dkv = jnp.zeros((keys, LANES), f32)
    for half in range(2):
        head = jnp.where(low, pltpu.roll(q, 64, 1) if half else q, 0.0).astype(bf16)
        grad_head = jnp.where(low, 0.0, grad if half else pltpu.roll(grad, 64, 1)).astype(bf16)
        mine = (low == (half == 0))
        delta = jnp.sum(jnp.where(mine, product, 0.0), axis=-1, keepdims=True)
        lse_head = lse[:, 64 * half : 64 * half + 1]
        probs = jnp.where(visible, jnp.exp(nt(head, kv) * scale - lse_head), 0.0)
        grad_scores = (probs * (nt(grad_head, kv) - delta)).astype(bf16)
        dqs.append(nn(grad_scores, kv) * scale)
        dkv = dkv + tn(grad_scores, head) * scale + tn(probs.astype(bf16), grad_head)
    dq = jnp.where(low, dqs[0], pltpu.roll(dqs[1], 64, 1)).astype(bf16).astype(f32)
    dq_ref[...] = (dq * cq[...] - half_swap(dq) * sq[...]).astype(bf16)

    @pl.when(pl.program_id(1) == 0)
    def _():
        dkv_ref[...] = dkv

    @pl.when(pl.program_id(1) > 0)
    def _():
        dkv_ref[...] += dkv


def turn_back_body(count, *refs):
    own, others, (ck, sk, out_ref) = refs[0], refs[1 : 1 + count], refs[1 + count :]
    for first in range(0, own.shape[1], LANES):
        span = slice(first, first + LANES)
        total = own[:, span]
        for other in others:
            total = total + other[:, span].astype(f32)
        total = total.astype(bf16).astype(f32)
        out_ref[:, span] = (total * ck[...] - half_swap(total) * sk[...]).astype(bf16)


def middle_body(count, experts, *refs):
    parts = refs[:count]
    res, gain, router, member, middle_ref, wide_ref, prob_ref = refs[count:]
    width = res.shape[1]
    middle = res[...].astype(f32)
    for part in parts:
        middle = middle + part[...].astype(f32)
    middle_ref[...] = middle
    inverse = lax.rsqrt(jnp.mean(middle * middle, axis=-1, keepdims=True) + epsilon)
    normed = (middle * inverse * gain[...]).astype(bf16)
    wide_ref[:, :width] = normed
    inside = member[...] > 0
    logits = jnp.where(inside, nn(normed, router[...]), neg_large)
    raised = jnp.where(inside, jnp.exp(logits - jnp.max(logits, axis=-1, keepdims=True)), 0.0)
    prob = raised / jnp.sum(raised, axis=-1, keepdims=True)
    prob_ref[...] = prob
    high = prob.astype(bf16).astype(f32)
    rest = (prob - high).astype(bf16).astype(f32)
    wide_ref[:, width:] = (high + pltpu.roll(rest, experts, 1)).astype(bf16)


def expert_body(experts, me_ref, *refs):
    (near, far, c0, c1, c2, c3, w_gate, w_up, w_down), outs = refs[:9], refs[9:]
    x_ref, y_keep, y_send, gi_keep, gi_send, hid_ref, ggp_ref, gup_ref, geo_ref = outs
    rows, width = c0.shape[1], c0.shape[2]
    me = me_ref[0]
    spots = ((near, 0), (near, 1), (far, 0), (far, 1))
    probs = []
    for i, (ref, xr) in enumerate(spots):
        x_ref[i * rows : (i + 1) * rows, :] = ref[xr, :, :width]
        extra = ref[xr, :, width:].astype(f32)
        lanes = lane_ids(extra.shape)
        mine = (lanes == me) | (lanes == me + experts)
        probs.append(jnp.sum(jnp.where(mine, extra, 0.0), axis=-1, keepdims=True))
    x = x_ref[...]
    gate = nn(x, w_gate[...])
    up = nn(x, w_up[...])
    sigmoid = 1.0 / (1.0 + jnp.exp(-gate))
    active = gate * sigmoid
    hidden = (active * up).astype(bf16)
    hid_ref[...] = hidden
    result = nn(hidden, w_down[...]).astype(bf16)
    marks = []
    for i, cot in enumerate((c0, c1, c2, c3)):
        part = result[i * rows : (i + 1) * rows, :].astype(f32)
        final = cot[0].astype(f32)
        out = y_send if i >= 2 else y_keep
        out[i % 2] = (probs[i] * part).astype(bf16)
        geo_ref[i * rows : (i + 1) * rows, :] = (probs[i] * final).astype(bf16)
        marks.append(jnp.sum(part * final, axis=-1, keepdims=True))
    grad_hidden = nt(geo_ref[...], w_down[...])
    ggp = (grad_hidden * up * sigmoid * (1.0 + gate * (1.0 - sigmoid))).astype(bf16)
    gup = (grad_hidden * active).astype(bf16)
    ggp_ref[...] = ggp
    gup_ref[...] = gup
    grad_in = (nt(ggp, w_gate[...]) + nt(gup, w_up[...])).astype(bf16)
    for i in range(4):
        out = gi_send if i >= 2 else gi_keep
        out[i % 2, :, :width] = grad_in[i * rows : (i + 1) * rows, :]
        high = marks[i].astype(bf16).astype(f32)
        lanes = lane_ids((rows, LANES))
        extra = jnp.where(lanes == me, high, 0.0) + jnp.where(lanes == me + experts, marks[i] - high, 0.0)
        out[i % 2, :, width:] = extra.astype(bf16)


def middle_back_body(count, experts, *refs):
    parts = refs[:count]
    middle_ref, prob_ref, cot, gain, router, grad_ref, branch_ref, pack_ref = refs[count:]
    width = cot.shape[1]
    total = parts[0][...].astype(f32)
    for part in parts[1:]:
        total = total + part[...].astype(f32)
    extra = total[:, width:]
    marks = extra + pltpu.roll(extra, LANES - experts, 1)
    prob = prob_ref[...]
    weighted = jnp.where(prob > 0, prob * marks, 0.0)
    spread = jnp.sum(weighted, axis=-1, keepdims=True)
    grad_logits = weighted - prob * spread
    high = grad_logits.astype(bf16)
    rest = (grad_logits - high.astype(f32)).astype(bf16)
    grad_normed = total[:, :width] + nt(high, router[...]) + nt(rest, router[...])
    middle = middle_ref[...]
    inverse = lax.rsqrt(jnp.mean(middle * middle, axis=-1, keepdims=True) + epsilon)
    unit = middle * inverse
    scaled = grad_normed * gain[...]
    grad = cot[...].astype(f32) + inverse * (
        scaled - unit * jnp.mean(scaled * unit, axis=-1, keepdims=True)
    )
    grad_ref[...] = grad
    branch_ref[...] = grad.astype(bf16)
    normed = (unit * gain[...]).astype(bf16)
    pack = tn(high, normed) + tn(rest, normed)
    gain_row = jnp.sum(grad_normed * unit, axis=0, keepdims=True)
    at_gain = lax.broadcasted_iota(jnp.int32, pack.shape, 0) == experts
    pack_ref[...] = jnp.where(at_gain, gain_row, pack).astype(bf16)


def input_back_body(count, *refs):
    parts = refs[:count]
    res, grad_middle, gain, out_ref = refs[count:]
    grad_normed = parts[0][...].astype(f32)
    for part in parts[1:]:
        grad_normed = grad_normed + part[...].astype(f32)
    x = res[...].astype(f32)
    inverse = lax.rsqrt(jnp.mean(x * x, axis=-1, keepdims=True) + epsilon)
    unit = x * inverse
    scaled = grad_normed * gain[...]
    out_ref[...] = grad_middle[...] + inverse * (
        scaled - unit * jnp.mean(scaled * unit, axis=-1, keepdims=True)
    )


def rope_tables(positions):
    half_dim = HEAD_DIM // 2
    inverse = jnp.exp(jnp.arange(half_dim, dtype=f32) * (-2.0 * math.log(10000.0) / HEAD_DIM))
    angles = positions.astype(f32)[:, None] * inverse[None, :]
    cos, sin = jnp.cos(angles), jnp.sin(angles)
    one, zero = jnp.ones_like(cos), jnp.zeros_like(sin)
    join = functools.partial(jnp.concatenate, axis=1)
    return (
        join([cos, cos, cos, cos]),
        join([-sin, sin, -sin, sin]),
        join([cos, cos, one, one]),
        join([-sin, sin, zero, zero]),
    )


def per_device(
    residual, segments, routes, w_query, w_key, w_value, w_out, w_router, attn_gain, moe_gain,
    w_gate, w_up, w_down, cotangent,
):
    seqs, blks = lax.axis_size("seq"), lax.axis_size("blk")
    seq_me, blk_me = lax.axis_index("seq"), lax.axis_index("blk")
    toks, width = residual.shape[1], residual.shape[2]
    rows = toks * seqs
    experts = blks
    own_rows = w_query.shape[0]
    kv_local = KV_HEADS // seqs
    q_cols, kv_cols = HEADS // seqs * HEAD_DIM, kv_local * 2 * HEAD_DIM
    scale = HEAD_DIM ** (-0.5)
    tokens = segments.shape[0]
    doc_most = tokens // 8
    hops = min(blks - 1, -(-(doc_most - 1) // rows))
    behind = hops * rows
    keys = behind + rows
    groups = blks // 4
    res = residual[0]
    cot = cotangent[0]

    extra = jnp.concatenate([w_router, attn_gain[:, None], moe_gain[:, None]], axis=1)
    extra = jnp.pad(extra, ((0, 0), (0, LANES - extra.shape[1])))
    by_seq = lambda w: w.reshape(own_rows, seqs, -1).swapaxes(0, 1)
    split_heads = lambda w: by_seq(w).reshape(seqs, own_rows, kv_local, HEAD_DIM)
    kv_parts = jnp.stack([split_heads(w_key), split_heads(w_value)], axis=3)
    out_parts = w_out.reshape(seqs, q_cols, own_rows).swapaxes(1, 2)
    weight_parts = jnp.concatenate(
        [
            by_seq(w_query),
            kv_parts.reshape(seqs, own_rows, kv_cols),
            jnp.broadcast_to(extra, (seqs,) + extra.shape),
            out_parts,
        ],
        axis=2,
    )
    weight_own = in_seq_order(exchange_seq(weight_parts)).reshape(seqs * own_rows, -1)
    res_all = gather_seq(res).reshape(rows, width)
    weight_rel = jnp.concatenate(
        [piece.reshape(2 * seqs * own_rows, -1) for pair in gather_blk(weight_own) for piece in pair],
        axis=0,
    )
    gate_all = gather_seq(w_gate[0]).reshape(width, -1)
    up_all = gather_seq(w_up[0]).reshape(width, -1)
    down_all = gather_seq(w_down[0]).reshape(-1, width)
    cot_all = lax.all_gather(cot, "blk", axis=0)

    spot = jnp.arange(width, dtype=jnp.int32)
    place, inner = spot // (seqs * own_rows), spot % (seqs * own_rows)
    device = blk_me ^ (4 * (place // 4) + 2 * (place % 2) + (place // 2) % 2)
    source = (inner // own_rows * blks + device) * own_rows + inner % own_rows
    order = (spot[:, None] == source[None, :]).astype(bf16)

    positions = blk_me * rows + jnp.arange(rows, dtype=jnp.int32)
    cos_q, sin_q, cos_k, sin_k = rope_tables(positions)
    x_rel = nn(res_all, order).astype(bf16)
    q_all, kv_own, normed_rel = call(
        functools.partial(project_body, q_cols, kv_cols, experts),
        (shape_of((rows, q_cols), bf16), shape_of((rows, kv_cols), bf16), shape_of((rows, width), bf16)),
    )(x_rel, weight_rel, cos_q, sin_q, cos_k, sin_k)
    weight_abs = nn(order, weight_rel).astype(bf16)
    cols = q_cols + kv_cols
    qkv_abs = weight_abs[:, :cols]
    router_abs = weight_abs[:, cols : cols + LANES]
    out_abs = weight_abs[:, cols + LANES :]
    gains = router_abs[:, experts : experts + 2].astype(f32).T
    gain_one, gain_two = gains[0:1], gains[1:2]

    kv_keys = jnp.concatenate([shifted(kv_own, "blk", n) for n in range(hops, 0, -1)] + [kv_own], axis=0)
    seg_padded = jnp.concatenate([jnp.full((behind,), -1, jnp.int32), segments])
    seg_k = lax.dynamic_slice_in_dim(seg_padded, blk_me * rows, keys)[None, :]
    seg_q = lax.dynamic_slice_in_dim(segments, blk_me * rows, rows)[:, None]
    step = min(rows, 256)
    grid = (kv_local, rows // step)
    row_block = pl.BlockSpec((step, LANES), lambda g, i: (i, g))
    key_block = pl.BlockSpec((keys, LANES), lambda g, i: (0, g))
    seg_q_block = pl.BlockSpec((step, 1), lambda g, i: (i, 0))
    seg_k_block = pl.BlockSpec((1, keys), lambda g, i: (0, 0))
    table_block = pl.BlockSpec((step, LANES), lambda g, i: (i, 0))
    mixed, lse = call(
        functools.partial(attend_body, behind, scale),
        (shape_of((rows, q_cols), bf16), shape_of((rows, q_cols), f32)),
        grid=grid,
        in_specs=[row_block, key_block, seg_q_block, seg_k_block],
        out_specs=(row_block, row_block),
    )(q_all, kv_keys, seg_q, seg_k)

    def sum_over_seq(partial):
        parts = partial.reshape(seqs, -1, partial.shape[-1])
        own = lax.dynamic_index_in_dim(parts, seq_me, 0, keepdims=False)
        others = exchange_seq(parts.astype(bf16))[1:]
        return [own] + others

    branch_parts = sum_over_seq(nt(mixed, out_abs))
    lanes = jnp.arange(LANES, dtype=jnp.int32)
    member = jnp.sum((routes[0][:, :, None] == lanes[None, None, :]).astype(f32), axis=1)
    middle, wide, prob = call(
        functools.partial(middle_body, seqs, experts),
        (shape_of((toks, width), f32), shape_of((toks, width + LANES), bf16), shape_of((toks, LANES), f32)),
    )(*branch_parts, res, gain_two, router_abs, member)

    hidden_cols = gate_all.shape[1]
    me = jnp.reshape(blk_me, (1,)).astype(jnp.int32)
    whole = lambda dims: pl.BlockSpec(dims, lambda i, me_ref: (0,) * len(dims))
    chunk_rows = 4 * toks
    keep_y, keep_gi = (2, toks, width), (2, toks, width + LANES)
    out_dims = [
        ((chunk_rows, width), bf16), (keep_y, bf16), (keep_y, bf16), (keep_gi, bf16), (keep_gi, bf16),
        ((chunk_rows, hidden_cols), bf16), ((chunk_rows, hidden_cols), bf16),
        ((chunk_rows, hidden_cols), bf16), ((chunk_rows, width), bf16),
    ]
    results = []
    for k, (near, far) in enumerate(gather_blk(wide)):
        cot_spec = lambda j: pl.BlockSpec((1, toks, width), lambda i, me_ref: (me_ref[0] ^ j, 0, 0))
        results.append(
            call(
                functools.partial(expert_body, experts),
                tuple(shape_of(d, t) for d, t in out_dims),
                grid_spec=pltpu.PrefetchScalarGridSpec(
                    num_scalar_prefetch=1,
                    grid=(1,),
                    in_specs=[whole(keep_gi), whole(keep_gi)]
                    + [cot_spec(4 * k + j) for j in (0, 2, 1, 3)]
                    + [whole(gate_all.shape), whole(up_all.shape), whole(down_all.shape)],
                    out_specs=[whole(d) for d, _ in out_dims],
                ),
            )(me, near, far, cot_all, cot_all, cot_all, cot_all, gate_all, up_all, down_all)
        )
    grad_parts = [reduce_chunk(k, results[k][3], results[k][4]) for k in range(groups)]
    join = lambda i: jnp.concatenate([r[i] for r in results], axis=0)
    x_all, hid_all, ggp_all, gup_all, geo_all = join(0), join(5), join(6), join(7), join(8)
    tdot = lambda a, b: lax.dot_general(a, b, (((0,), (0,)), ((), ())), preferred_element_type=f32)
    grad_gate, grad_up, grad_down = tdot(x_all, ggp_all), tdot(x_all, gup_all), tdot(hid_all, geo_all)

    grad_middle, grad_branch, pack = call(
        functools.partial(middle_back_body, groups, experts),
        (shape_of((toks, width), f32), shape_of((toks, width), bf16), shape_of((LANES, width), bf16)),
    )(*grad_parts, middle, prob, cot, gain_two, router_abs)

    branch_all = gather_seq(grad_branch).reshape(rows, width)
    grad_mixed = nn(branch_all, out_abs).astype(bf16)
    gq_pre, grad_kv = call(
        functools.partial(attend_back_body, behind, scale),
        (shape_of((rows, q_cols), bf16), shape_of((keys, kv_cols), f32)),
        grid=grid,
        in_specs=[row_block, key_block, row_block, row_block, row_block, seg_q_block, seg_k_block,
                  table_block, table_block],
        out_specs=(row_block, key_block),
    )(q_all, kv_keys, mixed, grad_mixed, lse, seg_q, seg_k, cos_q, sin_q)
    returned = [
        shifted(grad_kv[(hops - n) * rows : (hops - n + 1) * rows].astype(bf16), "blk", -n)
        for n in range(1, hops + 1)
    ]
    gkv_pre = call(
        functools.partial(turn_back_body, hops), shape_of((rows, kv_cols), bf16)
    )(grad_kv[behind:], *returned, cos_k, sin_k)

    def reduce_rows(grad):
        terms = grad.astype(bf16).reshape(blks, seqs, own_rows, -1)
        return in_seq_order(exchange_seq(reduce_blk(terms).astype(bf16)))

    q_rows = reduce_rows(tdot(normed_rel, gq_pre))
    kv_rows = reduce_rows(tdot(normed_rel, gkv_pre))
    normed_parts = sum_over_seq(nt(gq_pre, qkv_abs[:, :q_cols]) + nt(gkv_pre, qkv_abs[:, q_cols:]))
    grad_input = call(
        functools.partial(input_back_body, seqs), shape_of((toks, width), f32)
    )(*normed_parts, res, grad_middle, gain_one)

    branch_rel = nn(branch_all, order).astype(bf16)
    pack_rel = tdot(order, pack.T).astype(bf16)
    out_rows = reduce_rows(jnp.concatenate([tdot(branch_rel, mixed).astype(bf16), pack_rel], axis=1))
    shard_query = q_rows.astype(f32).swapaxes(0, 1).reshape(own_rows, -1)
    kv_rows = kv_rows.astype(f32).reshape(seqs, own_rows, kv_local, 2, HEAD_DIM).transpose(3, 1, 0, 2, 4)
    shard_key = kv_rows[0].reshape(own_rows, -1)
    shard_value = kv_rows[1].reshape(own_rows, -1)
    shard_out = out_rows[:, :, :q_cols].astype(f32).transpose(0, 2, 1).reshape(-1, own_rows)
    packed = jnp.sum(out_rows[:, :, q_cols:].astype(f32), axis=0)
    shard_router = packed[:, :experts]
    shard_gain_two = packed[:, experts]
    weigh = lambda w, g: jnp.sum(w.astype(f32) * g, axis=1)
    shard_gain_one = (
        weigh(w_query, shard_query) + weigh(w_key, shard_key) + weigh(w_value, shard_value)
    ) / attn_gain.astype(f32)

    def reduce_seq(grad):
        total = None
        for piece in sum_over_seq(grad):
            total = piece if total is None else total + piece.astype(f32)
        return total[None]

    shard_gate, shard_up, shard_down = reduce_seq(grad_gate), reduce_seq(grad_up), reduce_seq(grad_down)

    y_total = middle
    for k in range(groups):
        y_total = y_total + reduce_chunk(k, results[k][1], results[k][2]).astype(f32)
    block_out = y_total.astype(bf16)[None]
    return (
        block_out, grad_input[None], shard_query, shard_key, shard_value, shard_out, shard_router,
        shard_gain_one, shard_gain_two, shard_gate, shard_up, shard_down,
    )


def solution(mesh):
    both = ("seq", "blk")
    tokens, rows, cols, line = P("blk", "seq", None), P(both, None), P(None, both), P(both)
    return jax.shard_map(
        per_device,
        mesh=mesh,
        in_specs=(
            tokens, P(), tokens, rows, rows, rows, cols, rows, line, line, tokens, tokens, tokens, tokens,
        ),
        out_specs=(
            tokens, tokens, rows, rows, rows, cols, rows, line, line, tokens, tokens, tokens,
        ),
        check_vma=False,
    )
```

time: 1610 us -> 439 us (0.27)
  waiting for transfers between devices: 1150 us -> 197 us
  blocking collectives: 138 us -> 0 us
  starting transfers between devices: 163 us -> 84.3 us
  matrix products: 85.9 us -> 26.8 us
  Pallas kernels: 0 us -> 37.7 us
    reduce_scatter x7 -> x0, waiting for transfers between devices: 509 us -> none  [the longest x1 140 us: per_device(): lax.psum_scatter(grad_query, ('seq', 'blk'), scatter_dimension=0, tiled=T...]
    all_gather x7 -> x1, waiting for transfers between devices: 174 us -> 0.01 us  [per_device(): cot_all = lax.all_gather(cot, 'blk', axis=0)]
    all_to_all x9 -> x0, waiting for transfers between devices: 159 us -> none  [the longest x1 55.3 us: per_device(): lax.all_to_all(outgoing, 'blk', split_axis=0, concat_axis=0, tiled=True)]
    unnamed x16 -> x1, waiting for transfers between devices: 114 us -> 0.68 us
    unnamed x2 -> x0, blocking collectives: 79.2 us -> none
    all_to_all x9 -> x0, starting transfers between devices: 59.3 us -> none  [the longest x1 15.5 us: per_device(): lax.all_to_all(grad_inputs, 'blk', split_axis=0, concat_axis=0, tiled=True)]
    dot_general x36 -> x13, matrix products: 84.7 us -> 26.8 us  [the longest x7 13.4 us: per_device(): lax.dot_general(a, b, (((0,), (0,)), ((), ())), preferred_element_type=f32)]
    all_gather x1 -> x0, blocking collectives: 51.4 us -> none  [per_device(): lax.all_gather(w_router, ('seq', 'blk'), axis=0, tiled=True)]
  transfers between devices with their start and end apart: 70 -> 96, of which waited for: 62 -> 43; matrix products, arithmetic and copies ran while one was open for 7% -> 17% of each run, Pallas kernels for 0% -> 7%
where the time goes in v1:
time: 439 us; the launch traced here: 431 us
  waiting for transfers between devices  197 us (45%)
  starting transfers between devices  84.3 us (19%)
  local copies, waits for them, and re-layouts  43.9 us (10%)
  Pallas kernels  37.7 us (9%)
  matrix products  26.8 us (6%)
  other arithmetic  24.8 us (6%)
  between operations  16.3 us (4%)
    ppermute x91, waiting for transfers between devices, swap_with(): return lax.ppermute(value, axis, [(i, i ^ mask) for i in range(count)])  196 us
    ppermute x91, starting transfers between devices, swap_with(): return lax.ppermute(value, axis, [(i, i ^ mask) for i in range(count)])  74.9 us
    pallas_call x4, Pallas kernels, per_device(): call(functools.partial(expert_body, experts), tuple((shape_of(d, t) for d...  21 us
    unnamed x153, local copies, waits for them, and re-layouts  18.8 us
    dot_general x7, matrix products, per_device(): lax.dot_general(a, b, (((0,), (0,)), ((), ())), preferred_element_type=f32)  13.4 us
    convert_element_type x20, other arithmetic, reduce_chunk(): (keep.astype(f32) + swap_with(send, 'blk', 1).astype(f32)).astype(keep.dt...  11.9 us
    ppermute x4, starting transfers between devices, shifted(): lax.ppermute(value, axis, [(i, i + steps) for i in range(leading, last)])  9.29 us
  transfers between devices with their start and end apart: 96, of which 43 were waited for; matrix products, arithmetic and copies ran while one was open for 17% of the time, Pallas kernels for 7%

profile of v1, /device:TPU:0, one launch (start us, length us, event | category | flops | bytes accessed | tf_op | source)
XLA Modules:
  0.0 430.7 jit_solution(14125678547462465486)
XLA Ops:
  36.2 14.3 %collective-permute-done.7 = bf16[64,1664]{1,0:T(8,128)(2,1)S(1)} collective-permute-done((bf16[64,1664]{1,0:T(8,128)(2,1)S(1)}, bf16[64,1664]{1,0:T(8,128)(2,1)S(1)}, u32[]{:S(2)}, u32[]{:S(2)}) %collective-permute-start.7) | collective-permute-done | bytes 213024 | tf_op jit(solution)/shard_map/ppermute | solution.py:26
  52.6 18.2 %collective-permute-done.5 = bf16[64,1664]{1,0:T(8,128)(2,1)S(1)} collective-permute-done((bf16[64,1664]{1,0:T(8,128)(2,1)S(1)}, bf16[64,1664]{1,0:T(8,128)(2,1)S(1)}, u32[]{:S(2)}, u32[]{:S(2)}) %collective-permute-start.5) | collective-permute-done | bytes 213024 | tf_op jit(solution)/shard_map/ppermute | solution.py:26
  75.4 4.7 %collective-permute-start.13 = (bf16[256,512]{1,0:T(8,128)(2,1)S(1)}, bf16[256,512]{1,0:T(8,128)(2,1)S(1)}, u32[]{:S(2)}, u32[]{:S(2)}) collective-permute-start(bf16[256,512]{1,0:T(8,128)(2,1)S(1)} %get-tuple-element.62), channel_id=1, source_target_pairs={{0,2},{1,3},{2,4},{3,5},{4,6},{5,7},{6,8},{7,9},{8,10},{9,11},{10,... | collective-permute-start | bytes 786440 | tf_op jit(solution)/shard_map/ppermute | solution.py:32
  80.1 5.3 %fusion.12 = bf16[1024,1664]{0,1:T(8,128)(2,1)} fusion(bf16[1024,1664]{1,0:T(8,128)(2,1)S(1)} %constant_dynamic-update-slice_fusion.w_ref, s32[1024]{0:T(1024)S(1)} %fusion.103), kind=kOutput, calls=%fused_computation.13 | convolution fusion | flops 3492413440 | bytes 6819840 | tf_op jit(solution)/shard_map/dot_general | solution.py:118
  89.2 5.3 %shard_map.230 = (bf16[256,512]{1,0:T(8,128)(2,1)S(1)}, f32[256,512]{1,0:T(8,128)S(1)}) custom-call(bf16[256,512]{1,0:T(8,128)(2,1)S(1)} %get-tuple-element.61.q_ref, bf16[768,512]{1,0:T(8,128)(2,1)S(1)} %constant_dynamic-update-slice_fusion.8.kv_ref, s32[256,1]{1,0:T(8,128)S(1)} %copy.143.seg_q, s32[1,768]{1,0:T(1,128)S(1)} %broadcast_in_dim.96.seg_k), custom_call_target="tpu_custom_call" | custom-call | tf_op jit(solution)/shard_map/pallas_call | solution.py:418
  99.0 7.0 %collective-permute-done.15.refs_1_ = bf16[128,1024]{1,0:T(8,128)(2,1)S(1)} collective-permute-done((bf16[128,1024]{1,0:T(8,128)(2,1)S(1)}, bf16[128,1024]{1,0:T(8,128)(2,1)S(1)}, u32[]{:S(2)}, u32[]{:S(2)}) %collective-permute-start.15) | collective-permute-done | bytes 262176 | tf_op jit(solution)/shard_map/ppermute | solution.py:26
  119.1 7.9 %collective-permute-done.23 = bf16[128,1152]{1,0:T(8,128)(2,1)S(1)} collective-permute-done((bf16[128,1152]{1,0:T(8,128)(2,1)S(1)}, bf16[128,1152]{1,0:T(8,128)(2,1)S(1)}, u32[]{:S(2)}, u32[]{:S(2)}) %collective-permute-start.23) | collective-permute-done | bytes 294944 | tf_op jit(solution)/shard_map/ppermute | solution.py:26
  128.1 5.6 %collective-permute-done.29 = bf16[128,1152]{1,0:T(8,128)(2,1)S(1)} collective-permute-done((bf16[128,1152]{1,0:T(8,128)(2,1)S(1)}, bf16[128,1152]{1,0:T(8,128)(2,1)S(1)}, u32[]{:S(2)}, u32[]{:S(2)}) %collective-permute-start.29) | collective-permute-done | bytes 294944 | tf_op jit(solution)/shard_map/ppermute | solution.py:26
  138.7 5.6 %collective-permute-done.30 = bf16[128,1152]{1,0:T(8,128)(2,1)S(1)} collective-permute-done((bf16[128,1152]{1,0:T(8,128)(2,1)S(1)}, bf16[128,1152]{1,0:T(8,128)(2,1)S(1)}, u32[]{:S(2)}, u32[]{:S(2)}) %collective-permute-start.30) | collective-permute-done | bytes 294944 | tf_op jit(solution)/shard_map/ppermute | solution.py:26
  145.7 5.7 %collective-permute-done.18 = bf16[512,512]{1,0:T(8,128)(2,1)S(1)} collective-permute-done((bf16[512,512]{1,0:T(8,128)(2,1)S(1)}, bf16[512,512]{1,0:T(8,128)(2,1)S(1)}, u32[]{:S(2)}, u32[]{:S(2)}) %collective-permute-start.18) | collective-permute-done | bytes 524320 | tf_op jit(solution)/shard_map/ppermute | solution.py:26
  158.6 4.8 %shard_map.235 = (bf16[512,1024]{1,0:T(8,128)(2,1)S(1)}, bf16[2,128,1024]{2,1,0:T(8,128)(2,1)S(1)}, bf16[2,128,1024]{2,1,0:T(8,128)(2,1)}, bf16[2,128,1152]{2,1,...) custom-call(s32[1]{0:T(128)} %bitcast.33.me_ref, ...), custom_call_target="tpu_custom_call" | custom-call | tf_op jit(solution)/shard_map/pallas_call | solution.py:454
  166.8 5.3 %shard_map.234 = (bf16[512,1024]{1,0:T(8,128)(2,1)S(1)}, bf16[2,128,1024]{2,1,0:T(8,128)(2,1)S(1)}, bf16[2,128,1024]{2,1,0:T(8,128)(2,1)}, bf16[2,128,1152]{2,1,...) custom-call(s32[1]{0:T(128)} %bitcast.33.me_ref, ...), custom_call_target="tpu_custom_call" | custom-call | tf_op jit(solution)/shard_map/pallas_call | solution.py:454
  174.6 5.5 %shard_map.233 = (bf16[512,1024]{1,0:T(8,128)(2,1)S(1)}, bf16[2,128,1024]{2,1,0:T(8,128)(2,1)S(1)}, bf16[2,128,1024]{2,1,0:T(8,128)(2,1)S(1)}, bf16[2,128,1152]{...) custom-call(s32[1]{0:T(128)} %bitcast.33.me_ref, ...), custom_call_target="tpu_custom_call" | custom-call | tf_op jit(solution)/shard_map/pallas_call | solution.py:454
  184.1 5.4 %shard_map.232 = (bf16[512,1024]{1,0:T(8,128)(2,1)S(1)}, bf16[2,128,1024]{2,1,0:T(8,128)(2,1)S(1)}, bf16[2,128,1024]{2,1,0:T(8,128)(2,1)S(1)}, bf16[2,128,1152]{...) custom-call(s32[1]{0:T(128)} %bitcast.33.me_ref, ...), custom_call_target="tpu_custom_call" | custom-call | tf_op jit(solution)/shard_map/pallas_call | solution.py:454
  201.8 6.1 %collective-permute-done.94 = bf16[256,1024]{1,0:T(8,128)(2,1)S(1)} collective-permute-done((bf16[256,1024]{1,0:T(8,128)(2,1)S(1)}, bf16[256,1024]{1,0:T(8,128)(2,1)S(1)}, u32[]{:S(2)}, u32[]{:S(2)}) %collective-permute-start.94) | collective-permute-done | bytes 524320 | tf_op jit(solution)/shard_map/ppermute | solution.py:26
  213.4 12.2 %collective-permute-done.92 = bf16[512,512]{1,0:T(8,128)(2,1)S(1)} collective-permute-done((bf16[512,512]{1,0:T(8,128)(2,1)S(1)}, bf16[512,512]{1,0:T(8,128)(2,1)S(1)}, u32[]{:S(2)}, u32[]{:S(2)}) %collective-permute-start.92) | collective-permute-done | bytes 524320 | tf_op jit(solution)/shard_map/ppermute | solution.py:26
  226.7 9.1 %collective-permute-done.93 = bf16[512,512]{1,0:T(8,128)(2,1)S(1)} collective-permute-done((bf16[512,512]{1,0:T(8,128)(2,1)S(1)}, bf16[512,512]{1,0:T(8,128)(2,1)S(1)}, u32[]{:S(2)}, u32[]{:S(2)}) %collective-permute-start.93) | collective-permute-done | bytes 524320 | tf_op jit(solution)/shard_map/ppermute | solution.py:26
  250.8 5.5 %collective-permute-done.27 = bf16[128,1024]{1,0:T(8,128)(2,1)S(1)} collective-permute-done((bf16[128,1024]{1,0:T(8,128)(2,1)S(1)}, bf16[128,1024]{1,0:T(8,128)(2,1)S(1)}, u32[]{:S(2)}, u32[]{:S(2)}) %collective-permute-start.27) | collective-permute-done | bytes 262176 | tf_op jit(solution)/shard_map/ppermute | solution.py:26
  256.4 11.9 %collective-permute-done.50 = bf16[128,1152]{1,0:T(8,128)(2,1)S(1)} collective-permute-done((bf16[128,1152]{1,0:T(8,128)(2,1)S(1)}, bf16[128,1152]{1,0:T(8,128)(2,1)S(1)}, u32[]{:S(2)}, u32[]{:S(2)}) %collective-permute-start.50) | collective-permute-done | bytes 294944 | tf_op jit(solution)/shard_map/ppermute | solution.py:26
  268.4 6.2 %collective-permute-done.47 = bf16[128,1152]{1,0:T(8,128)(2,1)S(1)} collective-permute-done((bf16[128,1152]{1,0:T(8,128)(2,1)S(1)}, bf16[128,1152]{1,0:T(8,128)(2,1)S(1)}, u32[]{:S(2)}, u32[]{:S(2)}) %collective-permute-start.47) | collective-permute-done | bytes 294944 | tf_op jit(solution)/shard_map/ppermute | solution.py:26
  274.7 6.2 %collective-permute-done.44 = bf16[128,1152]{1,0:T(8,128)(2,1)S(1)} collective-permute-done((bf16[128,1152]{1,0:T(8,128)(2,1)S(1)}, bf16[128,1152]{1,0:T(8,128)(2,1)S(1)}, u32[]{:S(2)}, u32[]{:S(2)}) %collective-permute-start.44) | collective-permute-done | bytes 294944 | tf_op jit(solution)/shard_map/ppermute | solution.py:26
  285.9 17.7 %collective-permute-done.34 = bf16[128,1024]{1,0:T(8,128)(2,1)S(1)} collective-permute-done((bf16[128,1024]{1,0:T(8,128)(2,1)S(1)}, bf16[128,1024]{1,0:T(8,128)(2,1)S(1)}, u32[]{:S(2)}, u32[]{:S(2)}) %collective-permute-start.34) | collective-permute-done | bytes 262176 | tf_op jit(solution)/shard_map/ppermute | solution.py:26
  304.5 10.2 %collective-permute-done.48.refs_2_ = bf16[128,1152]{1,0:T(8,128)(2,1)S(1)} collective-permute-done((bf16[128,1152]{1,0:T(8,128)(2,1)S(1)}, bf16[128,1152]{1,0:T(8,128)(2,1)S(1)}, u32[]{:S(2)}, u32[]{:S(2)}) %collective-permute-start.48) | collective-permute-done | bytes 294944 | tf_op jit(solution)/shard_map/ppermute | solution.py:26
  327.6 7.4 %shard_map.237 = (bf16[256,512]{1,0:T(8,128)(2,1)S(1)}, f32[768,512]{1,0:T(8,128)S(1)}) custom-call(bf16[256,512]{1,0:T(8,128)(2,1)S(1)} %copy-done.24, bf16[768,512]{1,0:T(8,128)(2,1)S(1)} %copy-done.3, bf16[256,512]{1,0:T(8,128)(2,1)S(1)} %copy-done.22, bf16[256,512]{1,0:T(8,128)(2,1)S(1)} %convolution_convert_fusion.3.grad_ref, ...), custom_call_target="tpu_custom_call" | custom-call | tf_op jit(solution)/shard_map/pallas_call | solution.py:480
  (517 shorter events, 221.3 us)
Async XLA Ops:
  7.2 147.1 %all-gather.2.cloned.1.call-start = ((), (), s32[]{:S(2)}) async-start(), calls=%async_computation | async-start | bytes 4456448 | tf_op jit(solution)/shard_map/all_gather | solution.py:384
  24.5 26.0 %collective-permute-start.7 = (bf16[64,1664]{1,0:T(8,128)(2,1)S(1)}, bf16[64,1664]{1,0:T(8,128)(2,1)S(1)}, u32[]{:S(2)}, u32[]{:S(2)}) collective-permute-start(bf16[64,1664]{1,0:T(8,128)(2,1)S(1)} %bitcast.365), channel_id=1, source_target_pairs={{0,8},{1,9},{2,10},{3,11},{4,12},{5,13},{6,14},{7,15},{8,0},{9,1},... | collective-permute-start | bytes 638984 | tf_op jit(solution)/shard_map/ppermute | solution.py:26
  24.5 27.5 %collective-permute-start.4 = (bf16[64,1664]{1,0:T(8,128)(2,1)S(1)}, bf16[64,1664]{1,0:T(8,128)(2,1)S(1)}, u32[]{:S(2)}, u32[]{:S(2)}) collective-permute-start(bf16[64,1664]{1,0:T(8,128)(2,1)S(1)} %bitcast.366), channel_id=1, source_target_pairs={{0,4},{1,5},{2,6},{3,7},{4,0},{5,1},{6,2},{7,3},{8,12},{9,13},{10,... | collective-permute-start | bytes 638984 | tf_op jit(solution)/shard_map/ppermute | solution.py:26
  31.1 40.5 %collective-permute-start.3 = (bf16[2,64,1664]{2,1,0:T(8,128)(2,1)S(1)}, bf16[2,64,1664]{2,1,0:T(8,128)(2,1)S(1)}, u32[]{:S(2)}, u32[]{:S(2)}) collective-permute-start(bf16[2,64,1664]{2,1,0:T(8,128)(2,1)S(1)} %pad_maximum_fusion.4), channel_id=1, source_target_pairs={{0,1},{1,0},{2,3},{3,2},{4,5},{5,4},{6,7},{7,6},{8,9},{9,8},{10,11... | collective-permute-start | bytes 1277960 | tf_op jit(solution)/shard_map/ppermute | solution.py:26
  34.7 36.8 %collective-permute-start.11 = (bf16[64,1664]{1,0:T(8,128)(2,1)S(1)}, bf16[64,1664]{1,0:T(8,128)(2,1)S(1)}, u32[]{:S(2)}, u32[]{:S(2)}) collective-permute-start(bf16[64,1664]{1,0:T(8,128)(2,1)S(1)} %collective-permute-done.10), channel_id=1, source_target_pairs={{0,2},{1,3},{2,0},{3,1},{4,6},{5,7},{6,4},{7,5},{8,10},{9,11},{10,... | collective-permute-start | bytes 638984 | tf_op jit(solution)/shard_map/ppermute | solution.py:26
  110.9 34.2 %collective-permute-start.20 = (bf16[256,1024]{1,0:T(8,128)(2,1)S(1)}, bf16[256,1024]{1,0:T(8,128)(2,1)S(1)}, u32[]{:S(2)}, u32[]{:S(2)}) collective-permute-start(bf16[256,1024]{1,0:T(8,128)(2,1)S(1)} %bitcast.382), channel_id=1, source_target_pairs={{0,16},{16,0},{1,17},{17,1},{2,18},{18,2},{3,19},{19,3},{4,20},{20... | collective-permute-start | bytes 1572872 | tf_op jit(solution)/shard_map/ppermute | solution.py:26
  137.7 46.5 %collective-permute-start.17 = (bf16[2,128,1152]{2,1,0:T(8,128)(2,1)}, bf16[2,128,1152]{2,1,0:T(8,128)(2,1)}, u32[]{:S(2)}, u32[]{:S(2)}) collective-permute-start(bf16[2,128,1152]{2,1,0:T(8,128)(2,1)} %pad_maximum_fusion.refs_0_), channel_id=1, source_target_pairs={{0,1},{1,0},{2,3},{3,2},{4,5},{5,4},{6,7},{7,6},{8,9},{9,8},{10,11... | collective-permute-start | bytes 1769480 | tf_op jit(solution)/shard_map/ppermute | solution.py:26
  144.3 29.5 %collective-permute-start.25 = (bf16[2,128,1152]{2,1,0:T(8,128)(2,1)}, bf16[2,128,1152]{2,1,0:T(8,128)(2,1)}, u32[]{:S(2)}, u32[]{:S(2)}) collective-permute-start(bf16[2,128,1152]{2,1,0:T(8,128)(2,1)} %pad_maximum_fusion.1.refs_0_), channel_id=1, source_target_pairs={{0,1},{1,0},{2,3},{3,2},{4,5},{5,4},{6,7},{7,6},{8,9},{9,8},{10,11... | collective-permute-start | bytes 1769480 | tf_op jit(solution)/shard_map/ppermute | solution.py:26
  166.0 34.3 %collective-permute-start.38 = (bf16[2,128,1024]{2,1,0:T(8,128)(2,1)}, bf16[2,128,1024]{2,1,0:T(8,128)(2,1)}, u32[]{:S(2)}, u32[]{:S(2)}) collective-permute-start(bf16[2,128,1024]{2,1,0:T(8,128)(2,1)} %get-tuple-element.73), channel_id=1, source_target_pairs={{0,1},{1,0},{2,3},{3,2},{4,5},{5,4},{6,7},{7,6},{8,9},{9,8},{10,11... | collective-permute-start | bytes 1572872 | tf_op jit(solution)/shard_map/ppermute | solution.py:26
  166.1 70.9 %collective-permute-start.49 = (bf16[2,128,1152]{2,1,0:T(8,128)(2,1)}, bf16[2,128,1152]{2,1,0:T(8,128)(2,1)}, u32[]{:S(2)}, u32[]{:S(2)}) collective-permute-start(bf16[2,128,1152]{2,1,0:T(8,128)(2,1)} %get-tuple-element.81), channel_id=1, source_target_pairs={{0,1},{1,0},{2,3},{3,2},{4,5},{5,4},{6,7},{7,6},{8,9},{9,8},{10,11... | collective-permute-start | bytes 1769480 | tf_op jit(solution)/shard_map/ppermute | solution.py:26
  173.7 35.3 %collective-permute-start.32 = (bf16[2,128,1024]{2,1,0:T(8,128)(2,1)}, bf16[2,128,1024]{2,1,0:T(8,128)(2,1)}, u32[]{:S(2)}, u32[]{:S(2)}) collective-permute-start(bf16[2,128,1024]{2,1,0:T(8,128)(2,1)} %get-tuple-element.71), channel_id=1, source_target_pairs={{0,1},{1,0},{2,3},{3,2},{4,5},{5,4},{6,7},{7,6},{8,9},{9,8},{10,11... | collective-permute-start | bytes 1572872 | tf_op jit(solution)/shard_map/ppermute | solution.py:26
  174.5 65.8 %collective-permute-start.46 = (bf16[2,128,1152]{2,1,0:T(8,128)(2,1)S(1)}, bf16[2,128,1152]{2,1,0:T(8,128)(2,1)}, u32[]{:S(2)}, u32[]{:S(2)}) collective-permute-start(bf16[2,128,1152]{2,1,0:T(8,128)(2,1)S(1)} %get-tuple-element.79), channel_id=1, source_target_pairs={{0,1},{1,0},{2,3},{3,2},{4,5},{5,4},{6,7},{7,6},{8,9},{9,8},{10,11... | collective-permute-start | bytes 1769480 | tf_op jit(solution)/shard_map/ppermute | solution.py:26
  209.0 32.8 %collective-permute-start.43 = (bf16[2,128,1152]{2,1,0:T(8,128)(2,1)S(1)}, bf16[2,128,1152]{2,1,0:T(8,128)(2,1)S(1)}, u32[]{:S(2)}, u32[]{:S(2)}) collective-permute-start(bf16[2,128,1152]{2,1,0:T(8,128)(2,1)S(1)} %copy-done.36), channel_id=1, source_target_pairs={{0,1},{1,0},{2,3},{3,2},{4,5},{5,4},{6,7},{7,6},{8,9},{9,8},{10,11... | collective-permute-start | bytes 1769480 | tf_op jit(solution)/shard_map/ppermute | solution.py:26
  211.3 24.6 %collective-permute-start.93 = (bf16[512,512]{1,0:T(8,128)(2,1)S(1)}, bf16[512,512]{1,0:T(8,128)(2,1)S(1)}, u32[]{:S(2)}, u32[]{:S(2)}) collective-permute-start(bf16[512,512]{1,0:T(8,128)(2,1)S(1)} %fusion.57), channel_id=1, source_target_pairs={{0,16},{16,0},{1,17},{17,1},{2,18},{18,2},{3,19},{19,3},{4,20},{20... | collective-permute-start | bytes 1572872 | tf_op jit(solution)/shard_map/ppermute | solution.py:26
  241.8 39.2 %collective-permute-start.22 = (bf16[128,1024]{1,0:T(8,128)(2,1)S(1)}, bf16[128,1024]{1,0:T(8,128)(2,1)S(1)}, u32[]{:S(2)}, u32[]{:S(2)}) collective-permute-start(bf16[128,1024]{1,0:T(8,128)(2,1)S(1)} %slice_bitcast_fusion.14), channel_id=1, source_target_pairs={{0,2},{1,3},{2,0},{3,1},{4,6},{5,7},{6,4},{7,5},{8,10},{9,11},{10,... | collective-permute-start | bytes 786440 | tf_op jit(solution)/shard_map/ppermute | solution.py:26
  245.1 29.5 %collective-permute-start.47 = (bf16[128,1152]{1,0:T(8,128)(2,1)S(1)}, bf16[128,1152]{1,0:T(8,128)(2,1)S(1)}, u32[]{:S(2)}, u32[]{:S(2)}) collective-permute-start(bf16[128,1152]{1,0:T(8,128)(2,1)S(1)} %slice_bitcast_fusion.2), channel_id=1, source_target_pairs={{0,2},{1,3},{2,0},{3,1},{4,6},{5,7},{6,4},{7,5},{8,10},{9,11},{10,... | collective-permute-start | bytes 884744 | tf_op jit(solution)/shard_map/ppermute | solution.py:26
  250.7 30.2 %collective-permute-start.44 = (bf16[128,1152]{1,0:T(8,128)(2,1)S(1)}, bf16[128,1152]{1,0:T(8,128)(2,1)S(1)}, u32[]{:S(2)}, u32[]{:S(2)}) collective-permute-start(bf16[128,1152]{1,0:T(8,128)(2,1)S(1)} %slice_bitcast_fusion.4), channel_id=1, source_target_pairs={{0,2},{1,3},{2,0},{3,1},{4,6},{5,7},{6,4},{7,5},{8,10},{9,11},{10,... | collective-permute-start | bytes 884744 | tf_op jit(solution)/shard_map/ppermute | solution.py:26
  256.3 29.0 %collective-permute-start.42 = (bf16[128,1152]{1,0:T(8,128)(2,1)S(1)}, bf16[128,1152]{1,0:T(8,128)(2,1)S(1)}, u32[]{:S(2)}, u32[]{:S(2)}) collective-permute-start(bf16[128,1152]{1,0:T(8,128)(2,1)S(1)} %slice_bitcast_fusion.6), channel_id=1, source_target_pairs={{0,2},{1,3},{2,0},{3,1},{4,6},{5,7},{6,4},{7,5},{8,10},{9,11},{10,... | collective-permute-start | bytes 884744 | tf_op jit(solution)/shard_map/ppermute | solution.py:26
  274.6 29.0 %collective-permute-start.34 = (bf16[128,1024]{1,0:T(8,128)(2,1)S(1)}, bf16[128,1024]{1,0:T(8,128)(2,1)S(1)}, u32[]{:S(2)}, u32[]{:S(2)}) collective-permute-start(bf16[128,1024]{1,0:T(8,128)(2,1)S(1)} %fusion.60), channel_id=1, source_target_pairs={{0,8},{1,9},{2,10},{3,11},{4,12},{5,13},{6,14},{7,15},{8,0},{9,1},... | collective-permute-start | bytes 786440 | tf_op jit(solution)/shard_map/ppermute | solution.py:26
  285.4 29.3 %collective-permute-start.48 = (bf16[128,1152]{1,0:T(8,128)(2,1)S(1)}, bf16[128,1152]{1,0:T(8,128)(2,1)S(1)}, u32[]{:S(2)}, u32[]{:S(2)}) collective-permute-start(bf16[128,1152]{1,0:T(8,128)(2,1)S(1)} %fusion.53), channel_id=1, source_target_pairs={{0,8},{1,9},{2,10},{3,11},{4,12},{5,13},{6,14},{7,15},{8,0},{9,1},... | collective-permute-start | bytes 884744 | tf_op jit(solution)/shard_map/ppermute | solution.py:26
  285.5 29.2 %collective-permute-start.45 = (bf16[128,1152]{1,0:T(8,128)(2,1)S(1)}, bf16[128,1152]{1,0:T(8,128)(2,1)S(1)}, u32[]{:S(2)}, u32[]{:S(2)}) collective-permute-start(bf16[128,1152]{1,0:T(8,128)(2,1)S(1)} %fusion.54), channel_id=1, source_target_pairs={{0,4},{1,5},{2,6},{3,7},{4,0},{5,1},{6,2},{7,3},{8,12},{9,13},{10,... | collective-permute-start | bytes 884744 | tf_op jit(solution)/shard_map/ppermute | solution.py:26
  336.0 46.5 %collective-permute-start.54 = (bf16[256,512]{1,0:T(8,128)(2,1)}, bf16[256,512]{1,0:T(8,128)(2,1)S(1)}, u32[]{:S(2)}, u32[]{:S(2)}) collective-permute-start(bf16[256,512]{1,0:T(8,128)(2,1)} %get-tuple-element.170), channel_id=1, source_target_pairs={{2,0},{3,1},{4,2},{5,3},{6,4},{7,5},{8,6},{9,7},{10,8},{11,9},{12,... | collective-permute-start | bytes 786440 | tf_op jit(solution)/shard_map/ppermute | solution.py:32
  337.3 46.2 %collective-permute-start.53 = (bf16[256,512]{1,0:T(8,128)(2,1)}, bf16[256,512]{1,0:T(8,128)(2,1)S(1)}, u32[]{:S(2)}, u32[]{:S(2)}) collective-permute-start(bf16[256,512]{1,0:T(8,128)(2,1)} %get-tuple-element.171), channel_id=1, source_target_pairs={{1,0},{2,1},{3,2},{4,3},{5,4},{6,5},{7,6},{8,7},{9,8},{10,9},{11,1... | collective-permute-start | bytes 786440 | tf_op jit(solution)/shard_map/ppermute | solution.py:32
  361.3 26.8 %collective-permute-start.66 = (bf16[2,32,512]{2,1,0:T(8,128)(2,1)S(1)}, bf16[2,32,512]{2,1,0:T(8,128)(2,1)S(1)}, u32[]{:S(2)}, u32[]{:S(2)}) collective-permute-start(bf16[2,32,512]{2,1,0:T(8,128)(2,1)S(1)} %slice_bitcast_fusion.32), channel_id=1, source_target_pairs={{0,2},{1,3},{2,0},{3,1},{4,6},{5,7},{6,4},{7,5},{8,10},{9,11},{10,... | collective-permute-start | bytes 196616 | tf_op jit(solution)/shard_map/ppermute | solution.py:26
  (141 other events, 1601.8 us)
Sparse Core Ops, SparseCore 0:
  10.2 72.5 all-gather.1

commit v2 on v1

v2 whole, which is shorter than its diff:
```python
import functools
import math

import jax
import jax.numpy as jnp
import numpy as np
from jax import lax
from jax.experimental import pallas as pl
from jax.experimental.pallas import tpu as pltpu
from jax.sharding import PartitionSpec as P

HEADS = 16
KV_HEADS = 8
HEAD_DIM = 64
LANES = 128

f32 = jnp.float32
bf16 = jnp.bfloat16
epsilon = 1e-06
neg_large = -1e30


def swap_with(value, axis, mask):
    if mask == 0:
        return value
    count = lax.axis_size(axis)
    return lax.ppermute(value, axis, [(i, i ^ mask) for i in range(count)])


def shifted(value, axis, steps):
    count = lax.axis_size(axis)
    leading, last = (max(0, -steps), min(count, count - steps))
    return lax.ppermute(value, axis, [(i, i + steps) for i in range(leading, last)])


def gather_seq(value):
    count = lax.axis_size("seq")
    me = lax.axis_index("seq")
    whole = jnp.zeros((count,) + value.shape, value.dtype)
    for k in range(count):
        piece = swap_with(value, "seq", k)
        whole = lax.dynamic_update_index_in_dim(whole, piece, me ^ k, 0)
    return whole


def after(value, *others):
    return lax.optimization_barrier((value,) + others)[0]


def gather_masks(groups):
    near = [0, 2, 4, 6]
    far = [4 * k + x for k in range(2, groups) for x in (0, 2)]
    return [m + c for half in (near, far) for c in (0, 1) for m in half]


def gather_rows(value):
    groups = lax.axis_size("blk") // 4
    near_z = swap_with(value, "blk", 4)
    far, last = [], value
    for k in range(2, groups):
        last = swap_with(after(value, last), "blk", 4 * k)
        far += [last, swap_with(last, "blk", 2)]
    near = jnp.concatenate(
        [value, swap_with(value, "blk", 2), near_z, swap_with(near_z, "blk", 2)], axis=0
    )
    far = jnp.concatenate(far, axis=0)
    return jnp.concatenate([near, swap_with(near, "blk", 1), far, swap_with(far, "blk", 1)], axis=0)


def added(a, b):
    return (a.astype(f32) + b.astype(f32)).astype(a.dtype)


def scatter_core(keep, send):
    return added(keep, swap_with(send, "blk", 1))


def scatter_across(total):
    groups = lax.axis_size("blk") // 4
    parts = total.reshape(groups, 2, total.shape[0] // groups // 2, -1)
    return added(parts[:, 0], swap_with(parts[:, 1], "blk", 2))


def scatter_far(parts):
    return [swap_with(parts[k], "blk", 4 * k) for k in range(parts.shape[0] - 1, 0, -1)] + [parts[0]]


def call(body, out_shape, limit=16, flops=0, **options):
    many = isinstance(out_shape, (tuple, list))
    if "grid" not in options:
        space = pl.BlockSpec(memory_space=pltpu.VMEM)
        options.setdefault("out_specs", tuple(space for _ in out_shape) if many else space)
    sized = sum(math.prod(o.shape) * o.dtype.itemsize for o in (out_shape if many else [out_shape]))
    return pl.pallas_call(
        body,
        out_shape=out_shape,
        compiler_params=pltpu.CompilerParams(vmem_limit_bytes=limit * 1024 * 1024),
        cost_estimate=pl.CostEstimate(flops=flops, bytes_accessed=2 * sized, transcendentals=0),
        **options,
    )


def in_hbm(value):
    return pltpu.with_memory_space_constraint(value, pltpu.HBM)


def shape_of(dims, dtype):
    return jax.ShapeDtypeStruct(dims, dtype)


def lane_ids(shape):
    return lax.broadcasted_iota(jnp.int32, shape, len(shape) - 1)


def half_swap(tile):
    lanes = lane_ids(tile.shape)
    return jnp.where(lanes % 64 < 32, pltpu.roll(tile, 96, 1), pltpu.roll(tile, 32, 1))


def nt(a, b):
    return lax.dot_general(a, b, (((1,), (1,)), ((), ())), preferred_element_type=f32)


def tn(a, b):
    return lax.dot_general(a, b, (((0,), (0,)), ((), ())), preferred_element_type=f32)


def nn(a, b):
    return jnp.dot(a, b, preferred_element_type=f32)


def turned(tile, cos, sin, back=False):
    moved = half_swap(tile) * sin
    return tile * cos + (-moved if back else moved)


def key_tables(cos, sin):
    low = lane_ids(cos.shape) < HEAD_DIM
    return jnp.where(low, cos, 1.0), jnp.where(low, sin, 0.0)


def pack_body(seqs, dims, me_ref, *refs):
    q_cols, kv_cols, experts = dims
    sources, outs = refs[:7], refs[7 : 7 + seqs]
    held, sems = refs[7 + seqs : 14 + seqs], refs[14 + seqs]
    copies = [pltpu.make_async_copy(a, b, sems.at[i]) for i, (a, b) in enumerate(zip(sources, held))]
    for copy in copies:
        copy.start()
    for copy in copies:
        copy.wait()
    wq, wk, wv, wo, wr, gain_a, gain_m = held
    own_rows = wq.shape[0]
    lines = [wr[...].astype(f32), gain_a[...].astype(f32), gain_m[...].astype(f32)]
    lines.append(jnp.zeros((LANES - experts - 2, own_rows), f32))
    extra = jnp.concatenate(lines, axis=0).T.astype(bf16)
    half = kv_cols // 2
    for s in range(seqs):
        for k in range(seqs):

            @pl.when(me_ref[0] == s ^ k)
            def _(s=s, k=k):
                out = outs[k]
                out[:, :q_cols] = wq[:, s * q_cols : (s + 1) * q_cols]
                for g in range(half // HEAD_DIM):
                    span = slice(s * half + g * HEAD_DIM, s * half + (g + 1) * HEAD_DIM)
                    at = q_cols + 2 * g * HEAD_DIM
                    out[:, at : at + LANES] = jnp.concatenate([wk[:, span], wv[:, span]], axis=1)
                at = q_cols + kv_cols
                out[:, at : at + LANES] = extra
                out[:, at + LANES :] = wo[:, s * q_cols : (s + 1) * q_cols]


def restore_body(seqs, masks, experts, seq_ref, blk_ref, weight, qkv_ref, router_ref, gain_ref):
    cols = qkv_ref.shape[1]
    blks = len(masks)
    unit = weight.shape[0] // blks
    own_rows = unit // seqs
    for i, mask in enumerate(masks):
        for k in range(seqs):
            at = ((seq_ref[0] ^ k) * blks + (blk_ref[0] ^ mask)) * own_rows
            to = pl.ds(pl.multiple_of(at, own_rows), own_rows)
            span = slice(i * unit + k * own_rows, i * unit + (k + 1) * own_rows)
            qkv_ref[to, :] = weight[span, :cols]
            router_ref[to, :] = weight[span, cols:]
    pick = lax.broadcasted_iota(jnp.int32, (8, LANES), 0) + experts == lane_ids((8, LANES))
    gain_ref[...] = nt(pick.astype(bf16), router_ref[...])


def restore_out_body(seqs, blks, seq_ref, blk_ref, own, other, out_ref, sem):
    q_cols = out_ref.shape[1]
    own_rows = out_ref.shape[0] // blks // seqs
    copies = []
    for i in range(blks // 2):
        for c, weight in enumerate((own, other)):
            for k in range(seqs):
                blk = 2 * i + ((blk_ref[0] & 1) ^ c)
                at = ((seq_ref[0] ^ k) * blks + blk) * own_rows
                to = pl.ds(pl.multiple_of(at, own_rows), own_rows)
                part = weight.at[i, :, k * q_cols : (k + 1) * q_cols]
                copies.append(pltpu.make_async_copy(part, out_ref.at[to, :], sem.at[len(copies)]))
    for copy in copies:
        copy.start()
    for copy in copies:
        copy.wait()


def project_body(q_cols, kv_cols, gain_lane, x_ref, w_ref, cos, sin, q_ref, kv_ref, normed_ref):
    x = x_ref[...].astype(f32)
    inverse = lax.rsqrt(jnp.mean(x * x, axis=-1, keepdims=True) + epsilon)
    cols = q_cols + kv_cols
    pick = (lane_ids((8, LANES)) == gain_lane).astype(bf16)
    gain = nt(pick, w_ref[:, cols : cols + LANES])[0:1, :]
    normed = (x * inverse * gain).astype(bf16)
    normed_ref[...] = normed
    cos_q, sin_q = cos[...], sin[...]
    cos_k, sin_k = key_tables(cos_q, sin_q)
    wide = 2 * LANES if q_cols % (2 * LANES) == 0 and kv_cols % (2 * LANES) == 0 else LANES
    for first in range(0, cols, wide):
        both = nn(normed, w_ref[:, first : first + wide])
        for at in range(first, first + wide, LANES):
            tile = both[:, at - first : at - first + LANES]
            if at < q_cols:
                q_ref[:, at : at + LANES] = turned(tile, cos_q, sin_q).astype(bf16)
            else:
                kv_ref[:, at - q_cols : at - q_cols + LANES] = turned(tile, cos_k, sin_k).astype(bf16)


def visible_keys(meta_q, meta_k):
    mine = meta_q[...].T
    theirs = meta_k[...]
    return (theirs[1:2, :] <= mine[:, 1:2]) & (theirs[0:1, :] == mine[:, 0:1])


def attend_body(scale, q_ref, kv_ref, meta_q, meta_k, out_ref, lse_ref):
    visible = visible_keys(meta_q, meta_k)
    q = q_ref[...].astype(f32)
    kv = kv_ref[...]
    low = lane_ids(q.shape) < HEAD_DIM
    outs, lses = [], []
    for half in range(2):
        head = jnp.where(low, pltpu.roll(q, HEAD_DIM, 1) if half else q, 0.0).astype(bf16)
        scores = jnp.where(visible, nt(head, kv) * scale, neg_large)
        most = jnp.max(scores, axis=-1, keepdims=True)
        weights = jnp.exp(scores - most)
        total = jnp.sum(weights, axis=-1, keepdims=True)
        outs.append(nn(weights.astype(bf16), kv) / total)
        lses.append(most + jnp.log(total))
    out_ref[...] = jnp.where(low, pltpu.roll(outs[0], HEAD_DIM, 1), outs[1]).astype(bf16)
    lse_ref[...] = jnp.where(low, lses[0], lses[1])


def attend_back_body(
    scale, q_ref, kv_ref, mixed_ref, grad_ref, lse_ref, meta_q, meta_k, cos, sin, dq_ref, *outs
):
    outs, dkv_ref = outs[:-1], outs[-1]
    visible = visible_keys(meta_q, meta_k)
    q = q_ref[...].astype(f32)
    kv = kv_ref[...]
    grad = grad_ref[...].astype(f32)
    low = lane_ids(q.shape) < HEAD_DIM
    product = grad * mixed_ref[...].astype(f32)
    lse = lse_ref[...]
    dqs = []
    dkv = None
    for half in range(2):
        head = jnp.where(low, pltpu.roll(q, HEAD_DIM, 1) if half else q, 0.0).astype(bf16)
        grad_head = jnp.where(low, 0.0, grad if half else pltpu.roll(grad, HEAD_DIM, 1)).astype(bf16)
        delta = jnp.sum(jnp.where(low == (half == 0), product, 0.0), axis=-1, keepdims=True)
        lse_head = lse[:, HEAD_DIM * half : HEAD_DIM * half + 1]
        probs = jnp.where(visible, jnp.exp(nt(head, kv) * scale - lse_head), 0.0)
        grad_scores = (probs * (nt(grad_head, kv) - delta)).astype(bf16)
        dqs.append(nn(grad_scores, kv) * scale)
        term = tn(grad_scores, head) * scale + tn(probs.astype(bf16), grad_head)
        dkv = term if dkv is None else dkv + term
    dq = jnp.where(low, dqs[0], pltpu.roll(dqs[1], HEAD_DIM, 1)).astype(bf16).astype(f32)
    dq_ref[...] = turned(dq, cos[...], sin[...], back=True).astype(bf16)

    @pl.when(pl.program_id(1) == 0)
    def _():
        dkv_ref[...] = dkv

    @pl.when(pl.program_id(1) > 0)
    def _():
        dkv_ref[...] += dkv

    @pl.when(pl.program_id(1) == pl.num_programs(1) - 1)
    def _():
        at = 0
        for out in outs:
            out[...] = dkv_ref[at : at + out.shape[0], :].astype(out.dtype)
            at += out.shape[0]


def row_spans(width):
    near, far = 4, width // 2 - 4
    return ((0, near, 0, 0), (near, near, 1, 0), (2 * near, far, 0, near), (2 * near + far, far, 1, near))


def query_terms_body(blks, normed, gq, branch, mixed, pack, *outs):
    q_cols = gq.shape[1]
    unit = normed.shape[1] // blks
    for at, count, which, to in row_spans(blks):
        span, place = slice(at * unit, (at + count) * unit), slice(to * unit, (to + count) * unit)
        out = outs[which]
        out[place, :q_cols] = tn(normed[:, span], gq[...]).astype(bf16)
        out[place, q_cols : 2 * q_cols] = tn(branch[:, span], mixed[...]).astype(bf16)
        out[place, 2 * q_cols :] = pack[span, :]


def key_terms_body(blks, normed, gkv, *outs):
    unit = normed.shape[1] // blks
    for at, count, which, to in row_spans(blks):
        span, place = slice(at * unit, (at + count) * unit), slice(to * unit, (to + count) * unit)
        outs[which][place, :] = tn(normed[:, span], gkv[...]).astype(bf16)


def turn_back_body(count, seqs, *refs):
    own, others = refs[0], refs[1 : 1 + count]
    cos, sin, gq, weight = refs[1 + count : 5 + count]
    outs = refs[5 + count :]
    gkv_ref, parts = outs[0], outs[1:]
    cos_k, sin_k = key_tables(cos[...], sin[...])
    q_cols = gq.shape[1]
    for first in range(0, own.shape[1], LANES):
        span = slice(first, first + LANES)
        total = own[:, span]
        for other in others:
            total = total + other[:, span].astype(f32)
        gkv_ref[:, span] = turned(total.astype(bf16).astype(f32), cos_k, sin_k, back=True).astype(bf16)
    toks = parts[0].shape[0]
    for k in reversed(range(seqs)):
        span = slice(k * toks, (k + 1) * toks)
        grad = nt(gq[span, :], weight[:, :q_cols]) + nt(gkv_ref[span, :], weight[:, q_cols:])
        parts[k][...] = grad.astype(parts[k].dtype)


def to_row(column):
    count = column.shape[0]
    same = lax.broadcasted_iota(jnp.int32, (count, count), 0) == lane_ids((count, count))
    return jnp.sum(jnp.where(same, column, 0.0), axis=0, keepdims=True)


def finish_body(seqs, experts, me_ref, *refs):
    q_pieces, kv_pieces = refs[:seqs], refs[seqs : 2 * seqs]
    wq, wk, wv, gain = refs[2 * seqs : 2 * seqs + 4]
    query_ref, key_ref, value_ref, out_ref, router_ref, gain_one_ref, gain_two_ref = refs[2 * seqs + 4 :]
    q_cols = query_ref.shape[1] // seqs
    half = key_ref.shape[1] // seqs
    packed = None
    for k in range(seqs):
        part = q_pieces[k][:, 2 * q_cols :].astype(f32)
        packed = part if packed is None else packed + part
        for s in range(seqs):

            @pl.when(me_ref[0] == s ^ k)
            def _(s=s, k=k):
                span = slice(s * q_cols, (s + 1) * q_cols)
                query_ref[:, span] = q_pieces[k][:, :q_cols].astype(f32)
                out_ref[:, span] = q_pieces[k][:, q_cols : 2 * q_cols].astype(f32)
                for g in range(half // HEAD_DIM):
                    both = kv_pieces[k][:, 2 * g * HEAD_DIM : 2 * (g + 1) * HEAD_DIM].astype(f32)
                    span = slice(s * half + g * HEAD_DIM, s * half + (g + 1) * HEAD_DIM)
                    key_ref[:, span] = both[:, :HEAD_DIM]
                    value_ref[:, span] = both[:, HEAD_DIM:]

    router_ref[...] = packed.T[:experts, :]
    gain_two_ref[...] = to_row(packed[:, experts : experts + 1])
    weigh = lambda w, g: jnp.sum(w[...].astype(f32) * g[...], axis=1, keepdims=True)
    total = weigh(wq, query_ref) + weigh(wk, key_ref) + weigh(wv, value_ref)
    gain_one_ref[...] = to_row(total) / gain[...].astype(f32)


def middle_body(count, experts, *refs):
    parts = refs[:count]
    res, gains, router, routes, middle_ref, wide_ref, prob_ref = refs[count:]
    width = res.shape[1]
    middle = res[...].astype(f32)
    for part in parts:
        middle = middle + part[...].astype(f32)
    middle_ref[...] = middle
    inverse = lax.rsqrt(jnp.mean(middle * middle, axis=-1, keepdims=True) + epsilon)
    normed = (middle * inverse * gains[1:2, :]).astype(bf16)
    wide_ref[:, :width] = normed
    named = routes[...].astype(f32).T
    lanes = lane_ids((named.shape[0], LANES)).astype(f32)
    inside = lanes == named[:, 0:1]
    for i in range(1, named.shape[1]):
        inside = inside | (lanes == named[:, i : i + 1])
    logits = jnp.where(inside, nn(normed, router[...]), neg_large)
    raised = jnp.where(inside, jnp.exp(logits - jnp.max(logits, axis=-1, keepdims=True)), 0.0)
    prob = raised / jnp.sum(raised, axis=-1, keepdims=True)
    prob_ref[...] = prob
    high = prob.astype(bf16).astype(f32)
    rest = (prob - high).astype(bf16).astype(f32)
    wide_ref[:, width:] = (high + pltpu.roll(rest, experts, 1)).astype(bf16)


def expert_body(experts, k, seqs, me_ref, seq_ref, *refs):
    pieces, cot_all, packs = refs[:2], refs[2], refs[3 : 3 + 2 * seqs]
    outs, scratch = refs[-18:-11], refs[-11:]
    y_all, x_all, hid_all, ggp_all, gup_all, geo_all, gi_ref = outs
    wide, cot_ref, y_ref, x_ref, hid_ref, ggp_ref, gup_ref, geo_ref, wgu, wd, sems = scratch
    rows, width = cot_ref.shape[1], cot_ref.shape[2]
    high, low, cols = width // seqs, wd.shape[1] // seqs, wgu.shape[2] // 2
    me = me_ref[0]
    loads = [pltpu.make_async_copy(p, wide.at[i], sems.at[0, i]) for i, p in enumerate(pieces)]
    gates, downs = [], []
    for e in range(2):
        for j in range(seqs):
            at = pl.ds(pl.multiple_of((seq_ref[0] ^ j) * high, high), high)
            to = pl.ds(pl.multiple_of((seq_ref[0] ^ j) * low, low), low)
            pack = packs[e * seqs + j]
            gates.append(pltpu.make_async_copy(pack.at[:high, :], wgu.at[e, at, :], sems.at[1 + e, j]))
            downs.append(pltpu.make_async_copy(pack.at[high:, :], wd.at[e, to, :], sems.at[3 + e, j]))
    cots = [
        pltpu.make_async_copy(cot_all.at[(me ^ (4 * k + 2 * i)) // 2, :rows, :], cot_ref.at[i], sems.at[5, i])
        for i in range(2)
    ]
    for copies in (loads, gates[:seqs], downs[:seqs], cots, gates[seqs:], downs[seqs:]):
        for copy in copies:
            copy.start()
    for copy in loads:
        copy.wait()
    probs = [[], []]
    for i in range(2):
        x_ref[i * rows : (i + 1) * rows, :] = wide[i, :, :width]
        extra = wide[i, :, width:].astype(f32)
        lanes = lane_ids(extra.shape)
        for e in range(2):
            mine = (lanes == (me ^ e)) | (lanes == (me ^ e) + experts)
            probs[e].append(jnp.sum(jnp.where(mine, extra, 0.0), axis=-1, keepdims=True))
    x = x_ref[...]
    place = pl.ds(2 * k * rows, 2 * rows)
    stores = []

    def store(a, b, sem):
        stores.append(pltpu.make_async_copy(a, b, sem))
        stores[-1].start()

    store(x_ref, x_all.at[place, :], sems.at[8, 2])
    out, grad_in, marks, kept = None, None, [], []
    for e in range(2):
        prob = jnp.concatenate(probs[e], axis=0)
        for copy in gates[e * seqs : (e + 1) * seqs]:
            copy.wait()
        gate = nn(x, wgu[e, :, :cols])
        up = nn(x, wgu[e, :, cols:])
        sigmoid = 1.0 / (1.0 + jnp.exp(-gate))
        active = gate * sigmoid
        hidden = (active * up).astype(bf16)
        hid_ref[e] = hidden
        store(hid_ref.at[e], hid_all.at[e, place, :], sems.at[6 + e, 0])
        for copy in downs[e * seqs : (e + 1) * seqs]:
            copy.wait()
        result = nn(hidden, wd[e]).astype(bf16).astype(f32)
        if e == 0:
            for copy in cots:
                copy.wait()
        final = jnp.concatenate([cot_ref[0], cot_ref[1]], axis=0).astype(f32)
        out = prob * result if out is None else out + prob * result
        marks.append(jnp.sum(result * final, axis=-1, keepdims=True))
        geo_ref[e] = (prob * final).astype(bf16)
        store(geo_ref.at[e], geo_all.at[e, place, :], sems.at[6 + e, 3])
        kept.append((gate, up, sigmoid, active))
    y_ref[...] = out.astype(bf16)
    for i in range(2):
        store(y_ref.at[i * rows : (i + 1) * rows, :], y_all.at[(me ^ (4 * k + 2 * i)) // 2], sems.at[8, i])
    for e in range(2):
        gate, up, sigmoid, active = kept[e]
        grad_hidden = nt(geo_ref[e], wd[e])
        ggp = (grad_hidden * up * sigmoid * (1.0 + gate * (1.0 - sigmoid))).astype(bf16)
        gup = (grad_hidden * active).astype(bf16)
        ggp_ref[e] = ggp
        gup_ref[e] = gup
        store(ggp_ref.at[e], ggp_all.at[e, place, :], sems.at[6 + e, 1])
        store(gup_ref.at[e], gup_all.at[e, place, :], sems.at[6 + e, 2])
        grad = nt(ggp, wgu[e, :, :cols]) + nt(gup, wgu[e, :, cols:])
        grad_in = grad if grad_in is None else grad_in + grad
    lanes = lane_ids((2 * rows, LANES))
    extra = jnp.zeros((2 * rows, LANES), f32)
    for e in range(2):
        mark = marks[e].astype(bf16).astype(f32)
        extra = extra + jnp.where(lanes == (me ^ e), mark, 0.0)
        extra = extra + jnp.where(lanes == (me ^ e) + experts, marks[e] - mark, 0.0)
    for i in range(2):
        span = slice(i * rows, (i + 1) * rows)
        gi_ref[i, :, :width] = grad_in[span, :].astype(bf16)
        gi_ref[i, :, width:] = extra[span, :].astype(bf16)
    for copy in stores:
        copy.wait()


def expert_grads_body(e, seqs, me_ref, *refs):
    sources, (x, ggp, gup, hid, geo, sems) = refs[:5], refs[-6:]
    outs = refs[5:-6]
    copies = [
        pltpu.make_async_copy(a if i == 0 else a.at[e], b, sems.at[i])
        for i, (a, b) in enumerate(zip(sources, (x, ggp, gup, hid, geo)))
    ]
    for copy in copies:
        copy.start()
    for copy in copies:
        copy.wait()
    high, cols, low = x.shape[1] // seqs, hid.shape[1], hid.shape[1] // seqs
    places = (
        (slice(0, high), slice(0, cols)),
        (slice(0, high), slice(cols, 2 * cols)),
        (slice(high, high + low), slice(0, 2 * cols)),
    )
    for s in range(seqs):
        at, to = slice(s * high, (s + 1) * high), slice(s * low, (s + 1) * low)
        k = me_ref[0] ^ s
        for i, (rows, lanes) in enumerate(places):
            if i < 2:
                part = tn(x[:, at], (ggp, gup)[i][...])
            else:
                part = tn(hid[:, to], geo[...])
            if e == 1:
                outs[0][k, rows, lanes] = part.astype(bf16)
            else:
                part = part + outs[0][k, rows, lanes].astype(f32)

                @pl.when(k == 0)
                def _(part=part, i=i):
                    outs[1 + i][...] = part

                @pl.when(k != 0)
                def _(part=part, rows=rows, lanes=lanes):
                    outs[4][k - 1, rows, lanes] = part.astype(bf16)


def middle_back_body(count, experts, *refs):
    parts = refs[:count]
    middle_ref, prob_ref, cot, gains, router, grad_ref, branch_ref, pack_ref = refs[count:]
    width = cot.shape[1]
    gain = gains[1:2, :]
    total = parts[0][...].astype(f32)
    for part in parts[1:]:
        total = total + part[...].astype(f32)
    extra = total[:, width:]
    marks = extra + pltpu.roll(extra, LANES - experts, 1)
    prob = prob_ref[...]
    weighted = jnp.where(prob > 0, prob * marks, 0.0)
    spread = jnp.sum(weighted, axis=-1, keepdims=True)
    grad_logits = weighted - prob * spread
    high = grad_logits.astype(bf16)
    rest = (grad_logits - high.astype(f32)).astype(bf16)
    grad_normed = total[:, :width] + nt(high, router[...]) + nt(rest, router[...])
    middle = middle_ref[...]
    inverse = lax.rsqrt(jnp.mean(middle * middle, axis=-1, keepdims=True) + epsilon)
    unit = middle * inverse
    scaled = grad_normed * gain
    grad = cot[...].astype(f32) + inverse * (
        scaled - unit * jnp.mean(scaled * unit, axis=-1, keepdims=True)
    )
    grad_ref[...] = grad
    branch_ref[...] = grad.astype(bf16)
    normed = (unit * gain).astype(bf16)
    pack = tn(high, normed) + tn(rest, normed)
    gain_row = jnp.sum(grad_normed * unit, axis=0, keepdims=True)
    at_gain = lax.broadcasted_iota(jnp.int32, pack.shape, 0) == experts
    pack_ref[...] = jnp.where(at_gain, gain_row, pack).astype(bf16)


def input_back_body(count, *refs):
    parts = refs[:count]
    res, grad_middle, gains, out_ref = refs[count:]
    grad_normed = parts[0][...].astype(f32)
    for part in parts[1:]:
        grad_normed = grad_normed + part[...].astype(f32)
    x = res[...].astype(f32)
    inverse = lax.rsqrt(jnp.mean(x * x, axis=-1, keepdims=True) + epsilon)
    unit = x * inverse
    scaled = grad_normed * gains[0:1, :]
    out_ref[...] = grad_middle[...] + inverse * (
        scaled - unit * jnp.mean(scaled * unit, axis=-1, keepdims=True)
    )


def per_device(
    residual, segments, routes, w_query, w_key, w_value, w_out, w_router, attn_gain, moe_gain,
    w_gate, w_up, w_down, cotangent,
):
    seqs, blks = lax.axis_size("seq"), lax.axis_size("blk")
    seq_me, blk_me = lax.axis_index("seq"), lax.axis_index("blk")
    toks, width = residual.shape[1], residual.shape[2]
    rows = toks * seqs
    experts = blks
    own_rows = w_query.shape[0]
    kv_local = KV_HEADS // seqs
    q_cols, kv_cols = HEADS // seqs * HEAD_DIM, kv_local * 2 * HEAD_DIM
    cols = q_cols + kv_cols
    scale = HEAD_DIM ** (-0.5)
    tokens = segments.shape[0]
    doc_most = tokens // 8
    hops = min(blks - 1, -(-(doc_most - 1) // rows))
    behind = hops * rows
    keys = behind + rows
    groups = blks // 4
    masks = gather_masks(groups)
    res = residual[0]
    cot = cotangent[0]
    vmem = pl.BlockSpec(memory_space=pltpu.VMEM)
    smem = pl.BlockSpec(memory_space=pltpu.SMEM)
    seq_scalar = jnp.reshape(seq_me, (1,)).astype(jnp.int32)
    blk_scalar = jnp.reshape(blk_me, (1,)).astype(jnp.int32)
    hbm = pl.BlockSpec(memory_space=pltpu.HBM)
    gain_row = attn_gain[None, :]

    weight_dims = (own_rows, cols + LANES + q_cols)
    sources = (w_query, w_key, w_value, w_out.T, w_router.T, gain_row, moe_gain[None, :])
    weight_parts = call(
        functools.partial(pack_body, seqs, (q_cols, kv_cols, experts)),
        tuple(shape_of(weight_dims, bf16) for _ in range(seqs)),
        in_specs=[smem] + [hbm] * 7,
        scratch_shapes=[pltpu.VMEM(a.shape, a.dtype) for a in sources] + [pltpu.SemaphoreType.DMA((7,))],
    )(seq_scalar, *[in_hbm(a) for a in sources])
    weight_both = jnp.concatenate([swap_with(p, "seq", k) for k, p in enumerate(weight_parts)], axis=0)
    weight_own = weight_both[:, : cols + LANES]
    late_res = after(res, weight_both)
    res_parts = [res] + [swap_with(late_res, "seq", k) for k in range(1, seqs)]
    weight_rel = gather_rows(weight_own)
    same_core = [[2 * i + c for i in range(blks // 2)] for c in range(2)]
    joint = seqs * own_rows * q_cols // width
    out_own = weight_both[:, cols + LANES :].reshape(seqs, own_rows, q_cols)
    out_own = jnp.concatenate([out_own[k] for k in range(seqs)], axis=1).reshape(joint, width)
    both_all = lax.all_gather(
        jnp.concatenate([cot, out_own], axis=0), "blk", axis=0, axis_index_groups=same_core
    )
    gate, up, down, *_ = lax.optimization_barrier((w_gate[0], w_up[0], w_down[0], *res_parts))
    expert_pack = jnp.concatenate([jnp.concatenate([gate, up], axis=1), down], axis=0)
    packs = [swap_with(expert_pack, "seq", k) for k in range(seqs)]
    seq_me, blk_me = after(seq_me, weight_own), after(blk_me, weight_own)

    spot = np.arange(width)
    place, inner = spot // (seqs * own_rows), spot % (seqs * own_rows)
    mask_row = jnp.asarray(np.asarray(masks)[place], jnp.int32)
    seq_row = jnp.asarray(inner // own_rows, jnp.int32)
    source = ((seq_me ^ seq_row) * blks + (blk_me ^ mask_row)) * own_rows + (inner % own_rows)
    order = (lax.broadcasted_iota(jnp.int32, (width, width), 0) == source[None, :]).astype(bf16)

    turn = lambda i: (seq_me ^ (i // toks % seqs)) * toks + i % toks
    half_dim = HEAD_DIM // 2
    lanes = lane_ids((rows, LANES))
    inverse = jnp.exp((lanes % half_dim).astype(f32) * (-2.0 * math.log(10000.0) / HEAD_DIM))
    position = blk_me * rows + turn(lax.broadcasted_iota(jnp.int32, (rows, LANES), 0))
    angles = position.astype(f32) * inverse
    cos, sin = jnp.cos(angles), jnp.where(lanes % HEAD_DIM < half_dim, -1.0, 1.0) * jnp.sin(angles)
    key_ids = jnp.arange(keys, dtype=jnp.int32)
    key_places = key_ids // rows * rows - behind + turn(key_ids % rows)
    seg_padded = jnp.concatenate([jnp.full((behind,), -1, jnp.int32), segments])
    seg_near = lax.dynamic_slice_in_dim(seg_padded, blk_me * rows, keys).reshape(hops + 1, seqs, toks)
    seg_keys = jnp.stack(
        [lax.dynamic_index_in_dim(seg_near, seq_me ^ k, 1, keepdims=False) for k in range(seqs)], axis=1
    ).reshape(keys)
    meta = jnp.concatenate(
        [seg_keys.astype(f32)[None], key_places.astype(f32)[None], jnp.zeros((6, keys), f32)], axis=0
    )

    x_rel = jnp.concatenate([nn(part, order).astype(bf16) for part in res_parts], axis=0)
    q_all, kv_own, normed_rel = call(
        functools.partial(project_body, q_cols, kv_cols, experts),
        (shape_of((rows, q_cols), bf16), shape_of((rows, kv_cols), bf16), shape_of((rows, width), bf16)),
    )(x_rel, weight_rel, cos, sin)
    if own_rows % 16 == 0:
        qkv_abs, router_abs, gains = call(
            functools.partial(restore_body, seqs, masks, experts),
            (shape_of((width, cols), bf16), shape_of((width, LANES), bf16), shape_of((8, width), f32)),
            in_specs=[smem, smem, vmem],
        )(seq_scalar, blk_scalar, weight_rel)
    else:
        weight_abs = nn(order, weight_rel).astype(bf16)
        qkv_abs, router_abs = weight_abs[:, :cols], weight_abs[:, cols:]
        gains = jnp.pad(router_abs[:, experts : experts + 2].astype(f32).T, ((0, 6), (0, 0)))

    kv_keys = jnp.concatenate([shifted(kv_own, "blk", n) for n in range(hops, 0, -1)] + [kv_own], axis=0)
    step = min(rows, 256)
    grid = (kv_local, rows // step)
    row_block = pl.BlockSpec((step, LANES), lambda g, i: (i, g))
    key_block = pl.BlockSpec((keys, LANES), lambda g, i: (0, g))
    meta_q_block = pl.BlockSpec((8, step), lambda g, i: (0, behind // step + i))
    meta_k_block = pl.BlockSpec((8, keys), lambda g, i: (0, 0))
    table_block = pl.BlockSpec((step, LANES), lambda g, i: (i, 0))
    attend_limit = 8 + step * keys * 40 // 1024 // 1024
    mixed, lse = call(
        functools.partial(attend_body, scale),
        (shape_of((rows, q_cols), bf16), shape_of((rows, q_cols), f32)),
        limit=attend_limit,
        grid=grid,
        in_specs=[row_block, key_block, meta_q_block, meta_k_block],
        out_specs=(row_block, row_block),
    )(q_all, kv_keys, meta, meta)

    packs += [swap_with(after(p, mixed), "blk", 1) for p in packs]

    out_same = after(both_all[:, toks:], mixed)
    out_pair = [out_same, swap_with(out_same, "blk", 1)]
    if own_rows % 16 == 0:
        out_abs = call(
            functools.partial(restore_out_body, seqs, blks),
            shape_of((width, q_cols), bf16),
            in_specs=[smem, smem, hbm, hbm],
            scratch_shapes=[pltpu.SemaphoreType.DMA((blks * seqs,))],
        )(seq_scalar, blk_scalar, *[in_hbm(a) for a in out_pair])
    else:
        odd = blk_me % 2 == 1
        pair = jnp.stack([jnp.where(odd, out_pair[1 - c], out_pair[c]) for c in range(2)], axis=1)
        out_parts = pair.reshape(blks, own_rows, seqs, q_cols).swapaxes(1, 2)
        out_abs = jnp.stack(
            [lax.dynamic_index_in_dim(out_parts, seq_me ^ k, 1, keepdims=False) for k in range(seqs)]
        ).reshape(width, q_cols)

    branch = nt(mixed, out_abs)
    branch_parts = [branch[:toks]] + [
        swap_with(branch[k * toks : (k + 1) * toks].astype(bf16), "seq", k) for k in range(1, seqs)
    ]
    middle, wide, prob = call(
        functools.partial(middle_body, seqs, experts),
        (shape_of((toks, width), f32), shape_of((toks, width + LANES), bf16), shape_of((toks, LANES), f32)),
    )(*branch_parts, res, gains, router_abs, routes[0].T)

    hidden_cols = w_gate.shape[2]
    held = 2 * toks * groups
    buffers = [
        (2 * groups, toks, width), (held, width), (2, held, hidden_cols),
        (2, held, hidden_cols), (2, held, hidden_cols), (2, held, width),
    ]

    def run_experts(k, pieces, before):
        operands = [*pieces, both_all, *packs, *before]
        fixed = len(operands) - len(before) + 2
        return call(
            functools.partial(expert_body, experts, k, seqs),
            tuple(pltpu.HBM(d, bf16) for d in buffers) + (shape_of((2, toks, width + LANES), bf16),),
            limit=32,
            flops=48 * toks * width * hidden_cols,
            in_specs=[smem, smem] + [hbm] * len(operands),
            out_specs=(hbm,) * len(buffers) + (vmem,),
            input_output_aliases={fixed + i: i for i in range(len(before))},
            scratch_shapes=[
                pltpu.VMEM((2, toks, width + LANES), bf16),
                pltpu.VMEM((2, toks, width), bf16),
                pltpu.VMEM((2 * toks, width), bf16),
                pltpu.VMEM((2 * toks, width), bf16),
                pltpu.VMEM((2, 2 * toks, hidden_cols), bf16),
                pltpu.VMEM((2, 2 * toks, hidden_cols), bf16),
                pltpu.VMEM((2, 2 * toks, hidden_cols), bf16),
                pltpu.VMEM((2, 2 * toks, width), bf16),
                pltpu.VMEM((2, width, 2 * hidden_cols), bf16),
                pltpu.VMEM((2, hidden_cols, width), bf16),
                pltpu.SemaphoreType.DMA((9, max(4, seqs))),
            ],
        )(blk_scalar, seq_scalar, *[in_hbm(a) for a in operands])

    turns = [1] + list(range(groups - 1, 1, -1)) + [0]
    far = {0: wide}
    last = wide
    for k in turns[:-1]:
        far[k] = swap_with(after(wide, last), "blk", 4 * k)
        last = far[k] if k > 1 else last
    across = {k: swap_with(far[k], "blk", 2) for k in far}
    grads, nears, before = {}, {}, []
    for i, k in enumerate(turns):
        holds = [prob]
        if i > 0:
            holds.append(grads[turns[i - 1]])
        if i > 1:
            n = turns[i - 2]
            nears[n] = added(grads[n][0], swap_with(grads[n][1], "blk", 2))
            holds.append(nears[n])
        *before, grads[k] = run_experts(k, [after(far[k], *holds), across[k]], before)
    for n in turns[-2:]:
        nears[n] = added(grads[n][0], swap_with(grads[n][1], "blk", 2))
    grad_parts = [swap_with(nears[k], "blk", 4 * k) for k in turns]
    y_all, x_all, hid_all, ggp_all, gup_all, geo_all = before
    tdot = lambda a, b: lax.dot_general(a, b, (((0,), (0,)), ((), ())), preferred_element_type=f32)

    grad_middle, grad_branch, pack = call(
        functools.partial(middle_back_body, groups, experts),
        (shape_of((toks, width), f32), shape_of((toks, width), bf16), shape_of((LANES, width), bf16)),
    )(*grad_parts, middle, prob, cot, gains, router_abs)

    high, low = width // seqs, hidden_cols // seqs

    def expert_grads(e, outs, *others):
        operands = [in_hbm(a) for a in (x_all, ggp_all, gup_all, hid_all, geo_all)]
        return call(
            functools.partial(expert_grads_body, e, seqs),
            outs,
            limit=20 + 14 * held // 2048,
            flops=6 * held * width * hidden_cols,
            in_specs=[smem] + [hbm] * 5 + [vmem] * len(others),
            scratch_shapes=[
                pltpu.VMEM((held, width), bf16), pltpu.VMEM((held, hidden_cols), bf16),
                pltpu.VMEM((held, hidden_cols), bf16), pltpu.VMEM((held, hidden_cols), bf16),
                pltpu.VMEM((held, width), bf16), pltpu.SemaphoreType.DMA((5,)),
            ],
        )(seq_scalar, *operands, *others)

    partner_terms = expert_grads(1, shape_of((seqs, high + low, width), bf16))
    branch_others = [swap_with(grad_branch, "seq", k) for k in range(1, seqs)]
    branch_all = after(jnp.concatenate([grad_branch] + branch_others, axis=0), partner_terms)
    grad_mixed = nn(branch_all, out_abs).astype(bf16)
    block_spec = pl.BlockSpec((rows, LANES), lambda g, i: (0, g))
    gq_pre, *grad_kv = call(
        functools.partial(attend_back_body, scale),
        (shape_of((rows, q_cols), bf16),)
        + (shape_of((rows, kv_cols), bf16),) * hops
        + (shape_of((rows, kv_cols), f32),),
        limit=attend_limit,
        grid=grid,
        in_specs=[row_block, key_block, row_block, row_block, row_block, meta_q_block, meta_k_block,
                  table_block, table_block],
        out_specs=(row_block,) + (block_spec,) * (hops + 1),
        scratch_shapes=[pltpu.VMEM((keys, LANES), f32)],
    )(q_all, kv_keys, mixed, grad_mixed, lse, meta, meta, cos, sin)
    returned = [shifted(grad_kv[hops - n], "blk", -n) for n in range(1, hops + 1)]
    *shards, grad_sends = expert_grads(
        0,
        (shape_of((high, hidden_cols), f32), shape_of((high, hidden_cols), f32), shape_of((low, width), f32),
         shape_of((max(1, seqs - 1), high + low, width), bf16)),
        after(swap_with(partner_terms, "blk", 1), gq_pre),
    )
    branch_rel = nn(branch_all, order).astype(bf16)
    pack_rel = tdot(order, pack.T).astype(bf16)
    unit = seqs * own_rows
    q_terms = call(
        functools.partial(query_terms_body, blks),
        (shape_of((width // 2, 2 * q_cols + LANES), bf16),) * 2,
    )(normed_rel, gq_pre, branch_rel, mixed, pack_rel)

    def for_this_row(terms):
        total = sum(t.astype(f32) for t in terms).astype(bf16)
        return [swap_with(total[k * own_rows : (k + 1) * own_rows], "seq", k) for k in range(seqs)]

    q_total = scatter_core(*q_terms)
    q_stage = scatter_across(q_total)
    own_kv = after(grad_kv[-1], q_total, grad_sends)

    gkv_pre, *normed_parts = call(
        functools.partial(turn_back_body, hops, seqs),
        (shape_of((rows, kv_cols), bf16),)
        + tuple(shape_of((toks, width), bf16 if k else f32) for k in range(seqs)),
    )(own_kv, *returned, cos, sin, gq_pre, qkv_abs)
    kv_terms = call(
        functools.partial(key_terms_body, blks), (shape_of((width // 2, kv_cols), bf16),) * 2
    )(normed_rel, gkv_pre)
    q_pieces = for_this_row(scatter_far(q_stage))
    kv_pieces = for_this_row(scatter_far(scatter_across(scatter_core(*kv_terms))))
    shard_query, shard_key, shard_value, shard_out, shard_router, shard_gain_one, shard_gain_two = call(
        functools.partial(finish_body, seqs, experts),
        (shape_of(w_query.shape, f32), shape_of(w_key.shape, f32), shape_of(w_value.shape, f32),
         shape_of(w_out.shape[::-1], f32), shape_of(w_router.shape[::-1], f32),
         shape_of((1, own_rows), f32), shape_of((1, own_rows), f32)),
        in_specs=[smem] + [vmem] * (2 * seqs + 4),
    )(seq_scalar, *q_pieces, *kv_pieces, w_query, w_key, w_value, gain_row)
    normed_others = [swap_with(p, "seq", k) for k, p in enumerate(normed_parts) if k]
    grads_from = [swap_with(after(grad_sends[k - 1], *normed_others), "seq", k) for k in range(1, seqs)]
    grad_input = call(
        functools.partial(input_back_body, seqs), shape_of((toks, width), f32)
    )(normed_parts[0], *normed_others, res, grad_middle, gains)

    high_cols = slice(0, hidden_cols), slice(hidden_cols, 2 * hidden_cols)
    for k in range(1, seqs):
        other = grads_from[k - 1].astype(f32)
        parts = other[:high, high_cols[0]], other[:high, high_cols[1]], other[high:]
        shards = [a + b for a, b in zip(shards, parts)]
    shard_gate, shard_up, shard_down = (s[None] for s in shards)

    y_sum = lax.psum_scatter(
        after(y_all, nears[turns[-1]]).reshape(-1, width), "blk", scatter_dimension=0, tiled=True,
        axis_index_groups=same_core,
    )
    y_sum = after(y_sum, shard_key, grad_input)
    block_out = (middle + y_sum.astype(f32)).astype(bf16)[None]
    return (
        block_out, grad_input[None], shard_query, shard_key, shard_value, shard_out.T, shard_router.T,
        shard_gain_one[0], shard_gain_two[0], shard_gate, shard_up, shard_down,
    )


def solution(mesh):
    both = ("seq", "blk")
    tokens, rows, cols, line = P("blk", "seq", None), P(both, None), P(None, both), P(both)
    return jax.shard_map(
        per_device,
        mesh=mesh,
        in_specs=(
            tokens, P(), tokens, rows, rows, rows, cols, rows, line, line, tokens, tokens, tokens, tokens,
        ),
        out_specs=(
            tokens, tokens, rows, rows, rows, cols, rows, line, line, tokens, tokens, tokens,
        ),
        check_vma=False,
    )
```

time: 439 us -> 309 us (0.70)
  the two profiles are of different devices: /device:TPU:0 before, /device:TPU:8 now
where the time goes in v2:
time: 309 us; the launch traced here: 304 us
  waiting for transfers between devices  128 us (41%)
  Pallas kernels  72.9 us (24%)
  starting transfers between devices  59.1 us (19%)
  between operations  15.4 us (5%)
  other arithmetic  11.4 us (4%)
  local copies, waits for them, and re-layouts  10.7 us (3%)
  matrix products  6.27 us (2%)
    ppermute x46, waiting for transfers between devices, swap_with(): return lax.ppermute(value, axis, [(i, i ^ mask) for i in range(count)])  92.9 us
    ppermute x46, starting transfers between devices, swap_with(): return lax.ppermute(value, axis, [(i, i ^ mask) for i in range(count)])  46.6 us
    ppermute x4, waiting for transfers between devices, shifted(): lax.ppermute(value, axis, [(i, i + steps) for i in range(leading, last)])  29.7 us
    pallas_call x4, Pallas kernels, run_experts(): call(functools.partial(expert_body, experts, k, seqs), tuple((pltpu.HBM(d...  28 us
    pallas_call x2, Pallas kernels, expert_grads(): call(functools.partial(expert_grads_body, e, seqs), outs, limit=20 + 14 *...  19.5 us
    ppermute x4, starting transfers between devices, shifted(): lax.ppermute(value, axis, [(i, i + steps) for i in range(leading, last)])  12.5 us
    unnamed x124, local copies, waits for them, and re-layouts  9.05 us
    pallas_call x1, Pallas kernels, per_device(): call(functools.partial(attend_back_body, scale), (shape_of((rows, q_cols)...  8.83 us
  transfers between devices with their start and end apart: 52, of which 26 were waited for; matrix products, arithmetic and copies ran while one was open for 5% of the time, Pallas kernels for 23%

profile of v2, /device:TPU:8, one launch (start us, length us, event | category | flops | bytes accessed | tf_op | source)
XLA Modules:
  0.0 303.7 jit_solution(2615340946246408743)
XLA Ops:
  36.8 5.7 %collective-permute-done.9 = bf16[64,1152]{1,0:T(8,128)(2,1)S(1)} collective-permute-done((bf16[64,1152]{1,0:T(8,128)(2,1)S(1)}, bf16[64,1152]{1,0:T(8,128)(2,1)S(1)}, u32[]{:S(2)}, u32[]{:S(2)}) %collective-permute-start.9) | collective-permute-done | bytes 147488 | tf_op jit(solution)/shard_map/ppermute | solution.py:27
  51.0 13.1 %collective-permute-done.11 = bf16[256,512]{1,0:T(8,128)(2,1)S(1)} collective-permute-done((bf16[256,512]{1,0:T(8,128)(2,1)S(1)}, bf16[256,512]{1,0:T(8,128)(2,1)S(1)}, u32[]{:S(2)}, u32[]{:S(2)}) %collective-permute-start.11) | collective-permute-done | bytes 262176 | tf_op jit(solution)/shard_map/ppermute | solution.py:33
  64.1 7.6 %collective-permute-done.12 = bf16[256,512]{1,0:T(8,128)(2,1)S(1)} collective-permute-done((bf16[256,512]{1,0:T(8,128)(2,1)S(1)}, bf16[256,512]{1,0:T(8,128)(2,1)S(1)}, u32[]{:S(2)}, u32[]{:S(2)}) %collective-permute-start.12) | collective-permute-done | bytes 262176 | tf_op jit(solution)/shard_map/ppermute | solution.py:33
  71.8 5.3 %shard_map.258 = (bf16[256,512]{1,0:T(8,128)(2,1)S(1)}, f32[256,512]{1,0:T(8,128)S(1)}) custom-call(bf16[256,512]{1,0:T(8,128)(2,1)S(1)} %get-tuple-element.108.q_ref, bf16[768,512]{1,0:T(8,128)(2,1)S(1)} %constant_dynamic-update-slice_fusion.12.kv_ref, f32[8,768]{1,0:T(8,128)S(1)} %maximum_maximum_fusion.1.meta_q.meta_k, ...), custom_call_target="tpu_custom_call" | custom-call | bytes 1572864 | tf_op jit(solution)/shard_map/pallas_call | solution.py:685
  77.9 5.3 %all-gather.3.cloned.1.call-done = bf16[1280,1024]{1,0:T(8,128)(2,1)} async-done(((bf16[160,1024]{1,0:T(8,128)(2,1)}), bf16[1280,1024]{1,0:T(8,128)(2,1)}) %all-gather.3.cloned.1.call-update) | async-done | bytes 2621456 | tf_op jit(solution)/shard_map/all_gather | solution.py:627
  92.1 5.3 %collective-permute-done.14.refs_1_ = bf16[128,1024]{1,0:T(8,128)(2,1)S(1)} collective-permute-done((bf16[128,1024]{1,0:T(8,128)(2,1)S(1)}, bf16[128,1024]{1,0:T(8,128)(2,1)S(1)}, u32[]{:S(2)}, u32[]{:S(2)}) %collective-permute-start.14) | collective-permute-done | bytes 262176 | tf_op jit(solution)/shard_map/ppermute | solution.py:27
  99.5 8.7 %collective-permute-done.17.refs_0_ = bf16[128,1152]{1,0:T(8,128)(2,1)S(1)} collective-permute-done((bf16[128,1152]{1,0:T(8,128)(2,1)S(1)}, bf16[128,1152]{1,0:T(8,128)(2,1)S(1)}, u32[]{:S(2)}, u32[]{:S(2)}) %collective-permute-start.17) | collective-permute-done | bytes 294944 | tf_op jit(solution)/shard_map/ppermute | solution.py:27
  110.3 4.9 %collective-permute-start.16 = (bf16[128,1152]{1,0:T(8,128)(2,1)S(1)}, bf16[128,1152]{1,0:T(8,128)(2,1)S(1)}, u32[]{:S(2)}, u32[]{:S(2)}) collective-permute-start(bf16[128,1152]{1,0:T(8,128)(2,1)S(1)} %get-tuple-element.142.refs_0_), channel_id=1, source_target_pairs={{0,8},{1,9},{2,10},{3,11},{4,12},{5,13},{6,14},{7,15},{8,0},{9,1},... | collective-permute-start | bytes 884744 | tf_op jit(solution)/shard_map/ppermute | solution.py:27
  118.7 6.9 %shard_map.262 = (bf16[8,128,1024]{2,1,0:T(8,128)(2,1)}, bf16[1024,1024]{1,0:T(8,128)(2,1)}, bf16[2,1024,512]{2,1,0:T(8,128)(2,1)}, bf16[2,1024,512]{2,1,0:T(8,1...) custom-call(s32[1]{0:T(128)} %bitcast.8.blk_ref.me_ref, ...), custom_call_target="tpu_custom_call" | custom-call | flops 3221225472 | bytes 30539776 | tf_op jit(solution)/shard_map/pallas_call | solution.py:732
  128.2 6.9 %shard_map.263 = (bf16[8,128,1024]{2,1,0:T(8,128)(2,1)}, bf16[1024,1024]{1,0:T(8,128)(2,1)}, bf16[2,1024,512]{2,1,0:T(8,128)(2,1)}, bf16[2,1024,512]{2,1,0:T(8,1...) custom-call(s32[1]{0:T(128)} %bitcast.8.blk_ref.me_ref, ...), custom_call_target="tpu_custom_call", output_to_operand_aliasing={{0}: (9, {}), {1}: (10, {}), {2}: (11, {}), {3}: (12, {}), ... | custom-call | flops 3221225472 | bytes 30539776 | tf_op jit(solution)/shard_map/pallas_call | solution.py:732
  138.4 5.1 %collective-permute-done.25 = bf16[128,1152]{1,0:T(8,128)(2,1)S(1)} collective-permute-done((bf16[128,1152]{1,0:T(8,128)(2,1)S(1)}, bf16[128,1152]{1,0:T(8,128)(2,1)S(1)}, u32[]{:S(2)}, u32[]{:S(2)}) %collective-permute-start.25) | collective-permute-done | bytes 294944 | tf_op jit(solution)/shard_map/ppermute | solution.py:27
  147.4 7.3 %shard_map.264 = (bf16[8,128,1024]{2,1,0:T(8,128)(2,1)}, bf16[1024,1024]{1,0:T(8,128)(2,1)}, bf16[2,1024,512]{2,1,0:T(8,128)(2,1)}, bf16[2,1024,512]{2,1,0:T(8,1...) custom-call(s32[1]{0:T(128)} %bitcast.8.blk_ref.me_ref, ...), custom_call_target="tpu_custom_call", output_to_operand_aliasing={{0}: (9, {}), {1}: (10, {}), {2}: (11, {}), {3}: (12, {}), ... | custom-call | flops 3221225472 | bytes 30539776 | tf_op jit(solution)/shard_map/pallas_call | solution.py:732
  156.3 6.9 %shard_map.265 = (bf16[8,128,1024]{2,1,0:T(8,128)(2,1)}, bf16[1024,1024]{1,0:T(8,128)(2,1)}, bf16[2,1024,512]{2,1,0:T(8,128)(2,1)}, bf16[2,1024,512]{2,1,0:T(8,1...) custom-call(s32[1]{0:T(128)} %bitcast.8.blk_ref.me_ref, ...), custom_call_target="tpu_custom_call", output_to_operand_aliasing={{0}: (9, {}), {1}: (10, {}), {2}: (11, {}), {3}: (12, {}), ... | custom-call | flops 3221225472 | bytes 30539776 | tf_op jit(solution)/shard_map/pallas_call | solution.py:732
  165.0 5.0 %collective-permute-done.27 = bf16[128,1152]{1,0:T(8,128)(2,1)S(1)} collective-permute-done((bf16[128,1152]{1,0:T(8,128)(2,1)S(1)}, bf16[128,1152]{1,0:T(8,128)(2,1)S(1)}, u32[]{:S(2)}, u32[]{:S(2)}) %collective-permute-start.27) | collective-permute-done | bytes 294944 | tf_op jit(solution)/shard_map/ppermute | solution.py:27
  175.3 8.4 %shard_map.267 = bf16[2,768,1024]{2,1,0:T(8,128)(2,1)} custom-call(s32[1]{0:T(128)} %bitcast.me_ref.seq_ref, bf16[1024,1024]{1,0:T(8,128)(2,1)} %get-tuple-element.154.refs_0_, bf16[2,1024,512]{2,1,0:T(8,128)(2,1)} %get-tuple-element.155.refs_1_, bf16[2,1024,512]{2,1,0:T(8,128)(2,1)} %get-tuple-element.156.refs_2_, ...), custom_call_target="tpu_custom_call" | custom-call | flops 3221225472 | bytes 6291456 | tf_op jit(solution)/shard_map/pallas_call | solution.py:787
  185.3 8.8 %shard_map.268 = (bf16[256,512]{1,0:T(8,128)(2,1)S(1)}, bf16[256,512]{1,0:T(8,128)(2,1)S(1)}, bf16[256,512]{1,0:T(8,128)(2,1)}, f32[256,512]{1,0:T(8,128)S(1)}) custom-call(bf16[256,512]{1,0:T(8,128)(2,1)S(1)} %copy-done.14, bf16[768,512]{1,0:T(8,128)(2,1)S(1)} %constant_dynamic-update-slice_fusion.12.kv_ref, ...), custom_call_target="tpu_custom_call" | custom-call | bytes 2621440 | tf_op jit(solution)/shard_map/pallas_call | solution.py:805
  202.2 4.6 %collective-permute-start.40 = (bf16[256,512]{1,0:T(8,128)(2,1)}, bf16[256,512]{1,0:T(8,128)(2,1)S(1)}, u32[]{:S(2)}, u32[]{:S(2)}) collective-permute-start(bf16[256,512]{1,0:T(8,128)(2,1)} %get-tuple-element.169), channel_id=1, source_target_pairs={{1,0},{2,1},{3,2},{4,3},{5,4},{6,5},{7,6},{8,7},{9,8},{10,9},{11,1... | collective-permute-start | bytes 786440 | tf_op jit(solution)/shard_map/ppermute | solution.py:33
  206.9 3.5 %collective-permute-start.41 = (bf16[256,512]{1,0:T(8,128)(2,1)S(1)}, bf16[256,512]{1,0:T(8,128)(2,1)S(1)}, u32[]{:S(2)}, u32[]{:S(2)}) collective-permute-start(bf16[256,512]{1,0:T(8,128)(2,1)S(1)} %copy-done.39), channel_id=1, source_target_pairs={{2,0},{3,1},{4,2},{5,3},{6,4},{7,5},{8,6},{9,7},{10,8},{11,9},{12,... | collective-permute-start | bytes 786440 | tf_op jit(solution)/shard_map/ppermute | solution.py:33
  210.4 11.1 %shard_map.270 = (f32[512,512]{1,0:T(8,128)S(1)}, f32[512,512]{1,0:T(8,128)S(1)}, f32[256,1024]{1,0:T(8,128)S(1)}, bf16[1,768,1024]{2,1,0:T(8,128)(2,1)}) custom-call(s32[1]{0:T(128)} %bitcast.me_ref.seq_ref, bf16[1024,1024]{1,0:T(8,128)(2,1)} %get-tuple-element.154.refs_0_, bf16[2,1024,512]{2,1,0:T(8,128)(2,1)} %get-tuple-element.155.refs_1_, ...), custom_call_target="tpu_custom_call" | custom-call | flops 3221225472 | bytes 9437184 | tf_op jit(solution)/shard_map/pallas_call | solution.py:787
  221.6 9.0 %collective-permute-done.41.refs_2_ = bf16[256,512]{1,0:T(8,128)(2,1)S(1)} collective-permute-done((bf16[256,512]{1,0:T(8,128)(2,1)S(1)}, bf16[256,512]{1,0:T(8,128)(2,1)S(1)}, u32[]{:S(2)}, u32[]{:S(2)}) %collective-permute-start.41) | collective-permute-done | bytes 262176 | tf_op jit(solution)/shard_map/ppermute | solution.py:33
  238.4 3.8 %collective-permute-done.37 = bf16[64,1152]{1,0:T(8,128)(2,1)S(1)} collective-permute-done((bf16[64,1152]{1,0:T(8,128)(2,1)S(1)}, bf16[64,1152]{1,0:T(8,128)(2,1)S(1)}, u32[]{:S(2)}, u32[]{:S(2)}) %collective-permute-start.37) | collective-permute-done | bytes 147488 | tf_op jit(solution)/shard_map/ppermute | solution.py:27
  242.2 4.9 %collective-permute-done.36 = bf16[64,1152]{1,0:T(8,128)(2,1)S(1)} collective-permute-done((bf16[64,1152]{1,0:T(8,128)(2,1)S(1)}, bf16[64,1152]{1,0:T(8,128)(2,1)S(1)}, u32[]{:S(2)}, u32[]{:S(2)}) %collective-permute-start.36) | collective-permute-done | bytes 147488 | tf_op jit(solution)/shard_map/ppermute | solution.py:27
  247.0 4.1 %collective-permute-done.35 = bf16[64,1152]{1,0:T(8,128)(2,1)S(1)} collective-permute-done((bf16[64,1152]{1,0:T(8,128)(2,1)S(1)}, bf16[64,1152]{1,0:T(8,128)(2,1)S(1)}, u32[]{:S(2)}, u32[]{:S(2)}) %collective-permute-start.35) | collective-permute-done | bytes 147488 | tf_op jit(solution)/shard_map/ppermute | solution.py:27
  263.5 26.0 %collective-permute-done.38.refs_1_ = bf16[32,1152]{1,0:T(8,128)(2,1)S(1)} collective-permute-done((bf16[32,1152]{1,0:T(8,128)(2,1)S(1)}, bf16[32,1152]{1,0:T(8,128)(2,1)S(1)}, u32[]{:S(2)}, u32[]{:S(2)}) %collective-permute-start.38) | collective-permute-done | bytes 73760 | tf_op jit(solution)/shard_map/ppermute | solution.py:27
  (285 shorter events, 110.2 us)
Async XLA Ops:
  7.2 75.9 %all-gather.3.cloned.1.call-start = ((), (), s32[]{:S(2)}) async-start(), calls=%async_computation.2 | async-start | bytes 2949120 | tf_op jit(solution)/shard_map/all_gather | solution.py:627
  13.3 14.5 %collective-permute-start.2 = (bf16[64,1152]{1,0:T(8,128)(2,1)S(1)}, bf16[64,1152]{1,0:T(8,128)(2,1)S(1)}, u32[]{:S(2)}, u32[]{:S(2)}) collective-permute-start(bf16[64,1152]{1,0:T(8,128)(2,1)S(1)} %get-tuple-element.107), channel_id=1, source_target_pairs={{0,2},{1,3},{2,0},{3,1},{4,6},{5,7},{6,4},{7,5},{8,10},{9,11},{10,... | collective-permute-start | bytes 442376 | tf_op jit(solution)/shard_map/ppermute | solution.py:27
  15.3 12.5 %collective-permute-start.1 = (bf16[128,1024]{1,0:T(8,128)(2,1)}, bf16[128,1024]{1,0:T(8,128)(2,1)}, u32[]{:S(2)}, u32[]{:S(2)}) collective-permute-start(bf16[128,1024]{1,0:T(8,128)(2,1)} %bitcast.110), channel_id=1, source_target_pairs={{0,16},{16,0},{1,17},{17,1},{2,18},{18,2},{3,19},{19,3},{4,20},{20... | collective-permute-start | bytes 786440 | tf_op jit(solution)/shard_map/ppermute | solution.py:27
  21.2 269.6 %reduce-scatter.2.cloned.1.call-start = ((), (), s32[]{:S(2)}) async-start(), calls=%async_computation.1 | async-start | bytes 2359296 | tf_op jit(solution)/shard_map/reduce_scatter | solution.py:870
  30.5 54.3 %collective-permute-start.19 = (bf16[768,1024]{1,0:T(8,128)(2,1)}, bf16[768,1024]{1,0:T(8,128)(2,1)}, u32[]{:S(2)}, u32[]{:S(2)}) collective-permute-start(bf16[768,1024]{1,0:T(8,128)(2,1)} %pad_maximum_fusion.refs_3_), channel_id=1, source_target_pairs={{0,16},{16,0},{1,17},{17,1},{2,18},{18,2},{3,19},{19,3},{4,20},{20... | collective-permute-start | bytes 4718600 | tf_op jit(solution)/shard_map/ppermute | solution.py:27
  46.6 17.5 %collective-permute-start.11 = (bf16[256,512]{1,0:T(8,128)(2,1)S(1)}, bf16[256,512]{1,0:T(8,128)(2,1)S(1)}, u32[]{:S(2)}, u32[]{:S(2)}) collective-permute-start(bf16[256,512]{1,0:T(8,128)(2,1)S(1)} %get-tuple-element.109), channel_id=1, source_target_pairs={{0,2},{1,3},{2,4},{3,5},{4,6},{5,7},{6,8},{7,9},{8,10},{9,11},{10,... | collective-permute-start | bytes 786440 | tf_op jit(solution)/shard_map/ppermute | solution.py:33
  49.0 22.7 %collective-permute-start.12 = (bf16[256,512]{1,0:T(8,128)(2,1)S(1)}, bf16[256,512]{1,0:T(8,128)(2,1)S(1)}, u32[]{:S(2)}, u32[]{:S(2)}) collective-permute-start(bf16[256,512]{1,0:T(8,128)(2,1)S(1)} %get-tuple-element.109), channel_id=1, source_target_pairs={{0,1},{1,2},{2,3},{3,4},{4,5},{5,6},{6,7},{7,8},{8,9},{9,10},{10,1... | collective-permute-start | bytes 786440 | tf_op jit(solution)/shard_map/ppermute | solution.py:33
  84.3 30.8 %collective-permute-start.20 = (bf16[768,1024]{1,0:T(8,128)(2,1)}, bf16[768,1024]{1,0:T(8,128)(2,1)S(1)}, u32[]{:S(2)}, u32[]{:S(2)}) collective-permute-start(bf16[768,1024]{1,0:T(8,128)(2,1)} %pad_maximum_fusion.refs_3_), channel_id=1, source_target_pairs={{0,1},{1,0},{2,3},{3,2},{4,5},{5,4},{6,7},{7,6},{8,9},{9,8},{10,11... | collective-permute-start | bytes 4718600 | tf_op jit(solution)/shard_map/ppermute | solution.py:27
  84.8 30.9 %collective-permute-start.21 = (bf16[768,1024]{1,0:T(8,128)(2,1)}, bf16[768,1024]{1,0:T(8,128)(2,1)S(1)}, u32[]{:S(2)}, u32[]{:S(2)}) collective-permute-start(bf16[768,1024]{1,0:T(8,128)(2,1)} %collective-permute-done.19.refs_4_), channel_id=1, source_target_pairs={{0,1},{1,0},{2,3},{3,2},{4,5},{5,4},{6,7},{7,6},{8,9},{9,8},{10,11... | collective-permute-start | bytes 4718600 | tf_op jit(solution)/shard_map/ppermute | solution.py:27
  108.8 46.8 %collective-permute-start.26 = (bf16[128,1152]{1,0:T(8,128)(2,1)S(1)}, bf16[128,1152]{1,0:T(8,128)(2,1)S(1)}, u32[]{:S(2)}, u32[]{:S(2)}) collective-permute-start(bf16[128,1152]{1,0:T(8,128)(2,1)S(1)} %get-tuple-element.142.refs_0_), channel_id=1, source_target_pairs={{0,2},{1,3},{2,0},{3,1},{4,6},{5,7},{6,4},{7,5},{8,10},{9,11},{10,... | collective-permute-start | bytes 884744 | tf_op jit(solution)/shard_map/ppermute | solution.py:27
  110.3 25.2 %collective-permute-start.16 = (bf16[128,1152]{1,0:T(8,128)(2,1)S(1)}, bf16[128,1152]{1,0:T(8,128)(2,1)S(1)}, u32[]{:S(2)}, u32[]{:S(2)}) collective-permute-start(bf16[128,1152]{1,0:T(8,128)(2,1)S(1)} %get-tuple-element.142.refs_0_), channel_id=1, source_target_pairs={{0,8},{1,9},{2,10},{3,11},{4,12},{5,13},{6,14},{7,15},{8,0},{9,1},... | collective-permute-start | bytes 884744 | tf_op jit(solution)/shard_map/ppermute | solution.py:27
  115.2 12.3 %collective-permute-start.22 = (bf16[128,1152]{1,0:T(8,128)(2,1)S(1)}, bf16[128,1152]{1,0:T(8,128)(2,1)S(1)}, u32[]{:S(2)}, u32[]{:S(2)}) collective-permute-start(bf16[128,1152]{1,0:T(8,128)(2,1)S(1)} %collective-permute-done.15.refs_0_), channel_id=1, source_target_pairs={{0,2},{1,3},{2,0},{3,1},{4,6},{5,7},{6,4},{7,5},{8,10},{9,11},{10,... | collective-permute-start | bytes 884744 | tf_op jit(solution)/shard_map/ppermute | solution.py:27
  137.3 32.8 %collective-permute-start.28 = (bf16[128,1152]{1,0:T(8,128)(2,1)S(1)}, bf16[128,1152]{1,0:T(8,128)(2,1)S(1)}, u32[]{:S(2)}, u32[]{:S(2)}) collective-permute-start(bf16[128,1152]{1,0:T(8,128)(2,1)S(1)} %fusion.24), channel_id=1, source_target_pairs={{0,4},{1,5},{2,6},{3,7},{4,0},{5,1},{6,2},{7,3},{8,12},{9,13},{10,... | collective-permute-start | bytes 884744 | tf_op jit(solution)/shard_map/ppermute | solution.py:27
  143.6 26.6 %collective-permute-start.29 = (bf16[128,1152]{1,0:T(8,128)(2,1)S(1)}, bf16[128,1152]{1,0:T(8,128)(2,1)S(1)}, u32[]{:S(2)}, u32[]{:S(2)}) collective-permute-start(bf16[128,1152]{1,0:T(8,128)(2,1)S(1)} %fusion.23), channel_id=1, source_target_pairs={{0,12},{1,13},{2,14},{3,15},{4,8},{5,9},{6,10},{7,11},{8,4},{9,5},... | collective-permute-start | bytes 884744 | tf_op jit(solution)/shard_map/ppermute | solution.py:27
  183.7 26.7 %collective-permute-start.39 = (bf16[2,768,1024]{2,1,0:T(8,128)(2,1)}, bf16[2,768,1024]{2,1,0:T(8,128)(2,1)}, u32[]{:S(2)}, u32[]{:S(2)}) collective-permute-start(bf16[2,768,1024]{2,1,0:T(8,128)(2,1)} %shard_map.267), channel_id=1, source_target_pairs={{0,1},{1,0},{2,3},{3,2},{4,5},{5,4},{6,7},{7,6},{8,9},{9,8},{10,11... | collective-permute-start | bytes 9437192 | tf_op jit(solution)/shard_map/ppermute | solution.py:27
  200.9 31.9 %collective-permute-start.34 = (bf16[4,64,1152]{2,1,0:T(8,128)(2,1)S(1)}, bf16[4,64,1152]{2,1,0:T(8,128)(2,1)S(1)}, u32[]{:S(2)}, u32[]{:S(2)}) collective-permute-start(bf16[4,64,1152]{2,1,0:T(8,128)(2,1)S(1)} %slice_bitcast_fusion), channel_id=1, source_target_pairs={{0,2},{1,3},{2,0},{3,1},{4,6},{5,7},{6,4},{7,5},{8,10},{9,11},{10,... | collective-permute-start | bytes 1769480 | tf_op jit(solution)/shard_map/ppermute | solution.py:27
  202.2 19.3 %collective-permute-start.40 = (bf16[256,512]{1,0:T(8,128)(2,1)}, bf16[256,512]{1,0:T(8,128)(2,1)S(1)}, u32[]{:S(2)}, u32[]{:S(2)}) collective-permute-start(bf16[256,512]{1,0:T(8,128)(2,1)} %get-tuple-element.169), channel_id=1, source_target_pairs={{1,0},{2,1},{3,2},{4,3},{5,4},{6,5},{7,6},{8,7},{9,8},{10,9},{11,1... | collective-permute-start | bytes 786440 | tf_op jit(solution)/shard_map/ppermute | solution.py:33
  206.9 23.7 %collective-permute-start.41 = (bf16[256,512]{1,0:T(8,128)(2,1)S(1)}, bf16[256,512]{1,0:T(8,128)(2,1)S(1)}, u32[]{:S(2)}, u32[]{:S(2)}) collective-permute-start(bf16[256,512]{1,0:T(8,128)(2,1)S(1)} %copy-done.39), channel_id=1, source_target_pairs={{2,0},{3,1},{4,2},{5,3},{6,4},{7,5},{8,6},{9,7},{10,8},{11,9},{12,... | collective-permute-start | bytes 786440 | tf_op jit(solution)/shard_map/ppermute | solution.py:33
  236.5 14.6 %collective-permute-start.35 = (bf16[64,1152]{1,0:T(8,128)(2,1)S(1)}, bf16[64,1152]{1,0:T(8,128)(2,1)S(1)}, u32[]{:S(2)}, u32[]{:S(2)}) collective-permute-start(bf16[64,1152]{1,0:T(8,128)(2,1)S(1)} %get-tuple-element.192), channel_id=1, source_target_pairs={{0,12},{1,13},{2,14},{3,15},{4,8},{5,9},{6,10},{7,11},{8,4},{9,5},... | collective-permute-start | bytes 442376 | tf_op jit(solution)/shard_map/ppermute | solution.py:27
  237.4 13.9 %collective-permute-start.48 = (bf16[128,1024]{1,0:T(8,128)(2,1)S(1)}, bf16[128,1024]{1,0:T(8,128)(2,1)S(1)}, u32[]{:S(2)}, u32[]{:S(2)}) collective-permute-start(bf16[128,1024]{1,0:T(8,128)(2,1)S(1)} %get-tuple-element.177), channel_id=1, source_target_pairs={{0,16},{16,0},{1,17},{17,1},{2,18},{18,2},{3,19},{19,3},{4,20},{20... | collective-permute-start | bytes 786440 | tf_op jit(solution)/shard_map/ppermute | solution.py:27
  238.3 13.8 %collective-permute-start.43 = (bf16[4,64,512]{2,1,0:T(8,128)(2,1)S(1)}, bf16[4,64,512]{2,1,0:T(8,128)(2,1)S(1)}, u32[]{:S(2)}, u32[]{:S(2)}) collective-permute-start(bf16[4,64,512]{2,1,0:T(8,128)(2,1)S(1)} %slice_bitcast_fusion.6), channel_id=1, source_target_pairs={{0,2},{1,3},{2,0},{3,1},{4,6},{5,7},{6,4},{7,5},{8,10},{9,11},{10,... | collective-permute-start | bytes 786440 | tf_op jit(solution)/shard_map/ppermute | solution.py:27
  251.3 41.2 %collective-permute-start.49 = (bf16[768,1024]{1,0:T(8,128)(2,1)}, bf16[768,1024]{1,0:T(8,128)(2,1)S(1)}, u32[]{:S(2)}, u32[]{:S(2)}) collective-permute-start(bf16[768,1024]{1,0:T(8,128)(2,1)} %bitcast.45), channel_id=1, source_target_pairs={{0,16},{16,0},{1,17},{17,1},{2,18},{18,2},{3,19},{19,3},{4,20},{20... | collective-permute-start | bytes 4718600 | tf_op jit(solution)/shard_map/ppermute | solution.py:27
  255.7 33.8 %collective-permute-start.38 = (bf16[32,1152]{1,0:T(8,128)(2,1)S(1)}, bf16[32,1152]{1,0:T(8,128)(2,1)S(1)}, u32[]{:S(2)}, u32[]{:S(2)}) collective-permute-start(bf16[32,1152]{1,0:T(8,128)(2,1)S(1)} %get-tuple-element.200), channel_id=1, source_target_pairs={{0,16},{16,0},{1,17},{17,1},{2,18},{18,2},{3,19},{19,3},{4,20},{20... | collective-permute-start | bytes 221192 | tf_op jit(solution)/shard_map/ppermute | solution.py:27
  261.1 28.7 %collective-permute-start.47 = (bf16[32,512]{1,0:T(8,128)(2,1)S(1)}, bf16[32,512]{1,0:T(8,128)(2,1)S(1)}, u32[]{:S(2)}, u32[]{:S(2)}) collective-permute-start(bf16[32,512]{1,0:T(8,128)(2,1)S(1)} %get-tuple-element.202), channel_id=1, source_target_pairs={{0,16},{16,0},{1,17},{17,1},{2,18},{18,2},{3,19},{19,3},{4,20},{20... | collective-permute-start | bytes 98312 | tf_op jit(solution)/shard_map/ppermute | solution.py:27
  (84 other events, 1031.9 us)
Sparse Core Ops, SparseCore 0:
  21.3 61.8 all-gather.2
  198.0 78.1 reduce-scatter.1

commit v3 on v2

--- a/solution.py
+++ b/solution.py
@@ -64,7 +64,7 @@
         [value, swap_with(value, "blk", 2), near_z, swap_with(near_z, "blk", 2)], axis=0
     )
     far = jnp.concatenate(far, axis=0)
-    return jnp.concatenate([near, swap_with(near, "blk", 1), far, swap_with(far, "blk", 1)], axis=0)
+    return [near, swap_with(near, "blk", 1), far, swap_with(far, "blk", 1)]
 
 
 def added(a, b):
@@ -170,16 +170,17 @@
                 out[:, at + LANES :] = wo[:, s * q_cols : (s + 1) * q_cols]
 
 
-def restore_body(seqs, masks, experts, seq_ref, blk_ref, weight, qkv_ref, router_ref, gain_ref):
+def restore_body(seqs, masks, experts, seq_ref, blk_ref, w0, w1, w2, w3, qkv_ref, router_ref, gain_ref):
     cols = qkv_ref.shape[1]
     blks = len(masks)
-    unit = weight.shape[0] // blks
+    unit = qkv_ref.shape[0] // blks
     own_rows = unit // seqs
-    for i, mask in enumerate(masks):
+    places = [(weight, r) for weight in (w0, w1, w2, w3) for r in range(0, weight.shape[0], unit)]
+    for (weight, row), mask in zip(places, masks):
         for k in range(seqs):
             at = ((seq_ref[0] ^ k) * blks + (blk_ref[0] ^ mask)) * own_rows
             to = pl.ds(pl.multiple_of(at, own_rows), own_rows)
-            span = slice(i * unit + k * own_rows, i * unit + (k + 1) * own_rows)
+            span = slice(row + k * own_rows, row + (k + 1) * own_rows)
             qkv_ref[to, :] = weight[span, :cols]
             router_ref[to, :] = weight[span, cols:]
     pick = lax.broadcasted_iota(jnp.int32, (8, LANES), 0) + experts == lane_ids((8, LANES))
@@ -204,19 +205,27 @@
         copy.wait()
 
 
-def project_body(q_cols, kv_cols, gain_lane, x_ref, w_ref, cos, sin, q_ref, kv_ref, normed_ref):
+def project_body(q_cols, kv_cols, gain_lane, x_ref, *refs):
+    weights, (cos, sin, q_ref, kv_ref, normed_ref) = refs[:4], refs[4:]
     x = x_ref[...].astype(f32)
     inverse = lax.rsqrt(jnp.mean(x * x, axis=-1, keepdims=True) + epsilon)
     cols = q_cols + kv_cols
     pick = (lane_ids((8, LANES)) == gain_lane).astype(bf16)
-    gain = nt(pick, w_ref[:, cols : cols + LANES])[0:1, :]
-    normed = (x * inverse * gain).astype(bf16)
-    normed_ref[...] = normed
+    spans, at = [], 0
+    for weight in weights:
+        span = slice(at, at + weight.shape[0])
+        gain = nt(pick, weight[:, cols : cols + LANES])[0:1, :]
+        normed_ref[:, span] = (x[:, span] * inverse * gain).astype(bf16)
+        spans.append(span)
+        at += weight.shape[0]
     cos_q, sin_q = cos[...], sin[...]
     cos_k, sin_k = key_tables(cos_q, sin_q)
     wide = 2 * LANES if q_cols % (2 * LANES) == 0 and kv_cols % (2 * LANES) == 0 else LANES
     for first in range(0, cols, wide):
-        both = nn(normed, w_ref[:, first : first + wide])
+        both = None
+        for span, weight in zip(spans, weights):
+            term = nn(normed_ref[:, span], weight[:, first : first + wide])
+            both = term if both is None else both + term
         for at in range(first, first + wide, LANES):
             tile = both[:, at - first : at - first + LANES]
             if at < q_cols:
@@ -397,9 +406,9 @@
 
 def expert_body(experts, k, seqs, me_ref, seq_ref, *refs):
     pieces, cot_all, packs = refs[:2], refs[2], refs[3 : 3 + 2 * seqs]
-    outs, scratch = refs[-18:-11], refs[-11:]
-    y_all, x_all, hid_all, ggp_all, gup_all, geo_all, gi_ref = outs
-    wide, cot_ref, y_ref, x_ref, hid_ref, ggp_ref, gup_ref, geo_ref, wgu, wd, sems = scratch
+    outs, scratch = refs[-17:-10], refs[-10:]
+    y_keep, y_send, x_all, hid_all, gg_all, geo_all, gi_ref = outs
+    wide, cot_ref, y_ref, x_ref, hid_ref, gg_ref, geo_ref, wgu, wd, sems = scratch
     rows, width = cot_ref.shape[1], cot_ref.shape[2]
     high, low, cols = width // seqs, wd.shape[1] // seqs, wgu.shape[2] // 2
     me = me_ref[0]
@@ -443,8 +452,8 @@
         prob = jnp.concatenate(probs[e], axis=0)
         for copy in gates[e * seqs : (e + 1) * seqs]:
             copy.wait()
-        gate = nn(x, wgu[e, :, :cols])
-        up = nn(x, wgu[e, :, cols:])
+        both = nn(x, wgu[e])
+        gate, up = both[:, :cols], both[:, cols:]
         sigmoid = 1.0 / (1.0 + jnp.exp(-gate))
         active = gate * sigmoid
         hidden = (active * up).astype(bf16)
@@ -463,18 +472,17 @@
         store(geo_ref.at[e], geo_all.at[e, place, :], sems.at[6 + e, 3])
         kept.append((gate, up, sigmoid, active))
     y_ref[...] = out.astype(bf16)
-    for i in range(2):
-        store(y_ref.at[i * rows : (i + 1) * rows, :], y_all.at[(me ^ (4 * k + 2 * i)) // 2], sems.at[8, i])
+    store(y_ref.at[:rows, :], y_keep.at[k], sems.at[8, 0])
+    store(y_ref.at[rows:, :], y_send.at[k], sems.at[8, 1])
     for e in range(2):
         gate, up, sigmoid, active = kept[e]
         grad_hidden = nt(geo_ref[e], wd[e])
         ggp = (grad_hidden * up * sigmoid * (1.0 + gate * (1.0 - sigmoid))).astype(bf16)
         gup = (grad_hidden * active).astype(bf16)
-        ggp_ref[e] = ggp
-        gup_ref[e] = gup
-        store(ggp_ref.at[e], ggp_all.at[e, place, :], sems.at[6 + e, 1])
-        store(gup_ref.at[e], gup_all.at[e, place, :], sems.at[6 + e, 2])
-        grad = nt(ggp, wgu[e, :, :cols]) + nt(gup, wgu[e, :, cols:])
+        gg_ref[e, :, :cols] = ggp
+        gg_ref[e, :, cols:] = gup
+        store(gg_ref.at[e], gg_all.at[e, place, :], sems.at[6 + e, 1])
+        grad = nt(gg_ref[e], wgu[e])
         grad_in = grad if grad_in is None else grad_in + grad
     lanes = lane_ids((2 * rows, LANES))
     extra = jnp.zeros((2 * rows, LANES), f32)
@@ -491,42 +499,34 @@
 
 
 def expert_grads_body(e, seqs, me_ref, *refs):
-    sources, (x, ggp, gup, hid, geo, sems) = refs[:5], refs[-6:]
-    outs = refs[5:-6]
+    sources, (x, gg, hid, geo, sems) = refs[:4], refs[-5:]
+    outs = refs[4:-5]
     copies = [
         pltpu.make_async_copy(a if i == 0 else a.at[e], b, sems.at[i])
-        for i, (a, b) in enumerate(zip(sources, (x, ggp, gup, hid, geo)))
+        for i, (a, b) in enumerate(zip(sources, (x, gg, hid, geo)))
     ]
     for copy in copies:
         copy.start()
-    for copy in copies:
-        copy.wait()
-    high, cols, low = x.shape[1] // seqs, hid.shape[1], hid.shape[1] // seqs
-    places = (
-        (slice(0, high), slice(0, cols)),
-        (slice(0, high), slice(cols, 2 * cols)),
-        (slice(high, high + low), slice(0, 2 * cols)),
-    )
-    for s in range(seqs):
-        at, to = slice(s * high, (s + 1) * high), slice(s * low, (s + 1) * low)
-        k = me_ref[0] ^ s
-        for i, (rows, lanes) in enumerate(places):
-            if i < 2:
-                part = tn(x[:, at], (ggp, gup)[i][...])
+    high, low = x.shape[1] // seqs, hid.shape[1] // seqs
+    for i, (rows, a, b) in enumerate(((slice(0, high), x, gg), (slice(high, high + low), hid, geo))):
+        for copy in copies[2 * i : 2 * i + 2]:
+            copy.wait()
+        size = rows.stop - rows.start
+        for s in range(seqs):
+            k = me_ref[0] ^ s
+            part = tn(a[:, s * size : (s + 1) * size], b[...])
+            if e == 1:
+                outs[0][k, rows, :] = part.astype(bf16)
             else:
-                part = tn(hid[:, to], geo[...])
-            if e == 1:
-                outs[0][k, rows, lanes] = part.astype(bf16)
-            else:
-                part = part + outs[0][k, rows, lanes].astype(f32)
+                part = part + outs[0][k, rows, :].astype(f32)
 
                 @pl.when(k == 0)
                 def _(part=part, i=i):
                     outs[1 + i][...] = part
 
                 @pl.when(k != 0)
-                def _(part=part, rows=rows, lanes=lanes):
-                    outs[4][k - 1, rows, lanes] = part.astype(bf16)
+                def _(part=part, i=i):
+                    outs[3 + i][k - 1] = part.astype(bf16)
 
 
 def middle_back_body(count, experts, *refs):
@@ -661,15 +661,15 @@
     q_all, kv_own, normed_rel = call(
         functools.partial(project_body, q_cols, kv_cols, experts),
         (shape_of((rows, q_cols), bf16), shape_of((rows, kv_cols), bf16), shape_of((rows, width), bf16)),
-    )(x_rel, weight_rel, cos, sin)
+    )(x_rel, *weight_rel, cos, sin)
     if own_rows % 16 == 0:
         qkv_abs, router_abs, gains = call(
             functools.partial(restore_body, seqs, masks, experts),
             (shape_of((width, cols), bf16), shape_of((width, LANES), bf16), shape_of((8, width), f32)),
-            in_specs=[smem, smem, vmem],
-        )(seq_scalar, blk_scalar, weight_rel)
+            in_specs=[smem, smem] + [vmem] * 4,
+        )(seq_scalar, blk_scalar, *weight_rel)
     else:
-        weight_abs = nn(order, weight_rel).astype(bf16)
+        weight_abs = nn(order, jnp.concatenate(weight_rel, axis=0)).astype(bf16)
         qkv_abs, router_abs = weight_abs[:, :cols], weight_abs[:, cols:]
         gains = jnp.pad(router_abs[:, experts : experts + 2].astype(f32).T, ((0, 6), (0, 0)))
 
@@ -722,8 +722,8 @@
     hidden_cols = w_gate.shape[2]
     held = 2 * toks * groups
     buffers = [
-        (2 * groups, toks, width), (held, width), (2, held, hidden_cols),
-        (2, held, hidden_cols), (2, held, hidden_cols), (2, held, width),
+        (groups, toks, width), (groups, toks, width), (held, width), (2, held, hidden_cols), (2, held, 2 * hidden_cols),
+        (2, held, width),
     ]
 
     def run_experts(k, pieces, before):
@@ -732,7 +732,7 @@
         return call(
             functools.partial(expert_body, experts, k, seqs),
             tuple(pltpu.HBM(d, bf16) for d in buffers) + (shape_of((2, toks, width + LANES), bf16),),
-            limit=32,
+            limit=24,
             flops=48 * toks * width * hidden_cols,
             in_specs=[smem, smem] + [hbm] * len(operands),
             out_specs=(hbm,) * len(buffers) + (vmem,),
@@ -743,8 +743,7 @@
                 pltpu.VMEM((2 * toks, width), bf16),
                 pltpu.VMEM((2 * toks, width), bf16),
                 pltpu.VMEM((2, 2 * toks, hidden_cols), bf16),
-                pltpu.VMEM((2, 2 * toks, hidden_cols), bf16),
-                pltpu.VMEM((2, 2 * toks, hidden_cols), bf16),
+                pltpu.VMEM((2, 2 * toks, 2 * hidden_cols), bf16),
                 pltpu.VMEM((2, 2 * toks, width), bf16),
                 pltpu.VMEM((2, width, 2 * hidden_cols), bf16),
                 pltpu.VMEM((2, hidden_cols, width), bf16),
@@ -772,7 +771,7 @@
     for n in turns[-2:]:
         nears[n] = added(grads[n][0], swap_with(grads[n][1], "blk", 2))
     grad_parts = [swap_with(nears[k], "blk", 4 * k) for k in turns]
-    y_all, x_all, hid_all, ggp_all, gup_all, geo_all = before
+    y_keep, y_send, x_all, hid_all, gg_all, geo_all = before
     tdot = lambda a, b: lax.dot_general(a, b, (((0,), (0,)), ((), ())), preferred_element_type=f32)
 
     grad_middle, grad_branch, pack = call(
@@ -782,18 +781,21 @@
 
     high, low = width // seqs, hidden_cols // seqs
 
+    x_all = after(x_all, nears[turns[-1]])
+    y_far = swap_with(after(y_send, grad_branch), "blk", 2)
+
     def expert_grads(e, outs, *others):
-        operands = [in_hbm(a) for a in (x_all, ggp_all, gup_all, hid_all, geo_all)]
+        operands = [in_hbm(a) for a in (x_all, gg_all, hid_all, geo_all)]
         return call(
             functools.partial(expert_grads_body, e, seqs),
             outs,
-            limit=20 + 14 * held // 2048,
+            limit=10 + 7 * held // 1024,
             flops=6 * held * width * hidden_cols,
-            in_specs=[smem] + [hbm] * 5 + [vmem] * len(others),
+            in_specs=[smem] + [hbm] * 4 + [vmem] * len(others),
             scratch_shapes=[
-                pltpu.VMEM((held, width), bf16), pltpu.VMEM((held, hidden_cols), bf16),
-                pltpu.VMEM((held, hidden_cols), bf16), pltpu.VMEM((held, hidden_cols), bf16),
-                pltpu.VMEM((held, width), bf16), pltpu.SemaphoreType.DMA((5,)),
+                pltpu.VMEM((held, width), bf16), pltpu.VMEM((held, 2 * hidden_cols), bf16),
+                pltpu.VMEM((held, hidden_cols), bf16), pltpu.VMEM((held, width), bf16),
+                pltpu.SemaphoreType.DMA((4,)),
             ],
         )(seq_scalar, *operands, *others)
 
@@ -809,18 +811,22 @@
         + (shape_of((rows, kv_cols), f32),),
         limit=attend_limit,
         grid=grid,
+        flops=24 * rows * keys * q_cols,
         in_specs=[row_block, key_block, row_block, row_block, row_block, meta_q_block, meta_k_block,
                   table_block, table_block],
         out_specs=(row_block,) + (block_spec,) * (hops + 1),
         scratch_shapes=[pltpu.VMEM((keys, LANES), f32)],
     )(q_all, kv_keys, mixed, grad_mixed, lse, meta, meta, cos, sin)
     returned = [shifted(grad_kv[hops - n], "blk", -n) for n in range(1, hops + 1)]
-    *shards, grad_sends = expert_grads(
+    spare = max(1, seqs - 1)
+    gg_own, down_own, gg_sends, down_sends = expert_grads(
         0,
-        (shape_of((high, hidden_cols), f32), shape_of((high, hidden_cols), f32), shape_of((low, width), f32),
-         shape_of((max(1, seqs - 1), high + low, width), bf16)),
+        (shape_of((high, 2 * hidden_cols), f32), shape_of((low, width), f32),
+         shape_of((spare, high, 2 * hidden_cols), bf16), shape_of((spare, low, width), bf16)),
         after(swap_with(partner_terms, "blk", 1), gq_pre),
     )
+    down_from = [swap_with(down_sends[k - 1], "seq", k) for k in range(1, seqs)]
+    y_near = added(y_keep, y_far)
     branch_rel = nn(branch_all, order).astype(bf16)
     pack_rel = tdot(order, pack.T).astype(bf16)
     unit = seqs * own_rows
@@ -834,8 +840,8 @@
         return [swap_with(total[k * own_rows : (k + 1) * own_rows], "seq", k) for k in range(seqs)]
 
     q_total = scatter_core(*q_terms)
-    q_stage = scatter_across(q_total)
-    own_kv = after(grad_kv[-1], q_total, grad_sends)
+    q_stage = scatter_across(after(q_total, gg_sends, *returned))
+    own_kv = after(grad_kv[-1], q_total, gg_sends)
 
     gkv_pre, *normed_parts = call(
         functools.partial(turn_back_body, hops, seqs),
@@ -846,7 +852,9 @@
         functools.partial(key_terms_body, blks), (shape_of((width // 2, kv_cols), bf16),) * 2
     )(normed_rel, gkv_pre)
     q_pieces = for_this_row(scatter_far(q_stage))
-    kv_pieces = for_this_row(scatter_far(scatter_across(scatter_core(*kv_terms))))
+    gg_from = [swap_with(gg_sends[k - 1], "seq", k) for k in range(1, seqs)]
+    kv_stage = scatter_across(scatter_core(*kv_terms))
+    kv_pieces = for_this_row(scatter_far(kv_stage))
     shard_query, shard_key, shard_value, shard_out, shard_router, shard_gain_one, shard_gain_two = call(
         functools.partial(finish_body, seqs, experts),
         (shape_of(w_query.shape, f32), shape_of(w_key.shape, f32), shape_of(w_value.shape, f32),
@@ -855,24 +863,20 @@
         in_specs=[smem] + [vmem] * (2 * seqs + 4),
     )(seq_scalar, *q_pieces, *kv_pieces, w_query, w_key, w_value, gain_row)
     normed_others = [swap_with(p, "seq", k) for k, p in enumerate(normed_parts) if k]
-    grads_from = [swap_with(after(grad_sends[k - 1], *normed_others), "seq", k) for k in range(1, seqs)]
     grad_input = call(
         functools.partial(input_back_body, seqs), shape_of((toks, width), f32)
     )(normed_parts[0], *normed_others, res, grad_middle, gains)
 
-    high_cols = slice(0, hidden_cols), slice(hidden_cols, 2 * hidden_cols)
     for k in range(1, seqs):
-        other = grads_from[k - 1].astype(f32)
-        parts = other[:high, high_cols[0]], other[:high, high_cols[1]], other[high:]
-        shards = [a + b for a, b in zip(shards, parts)]
-    shard_gate, shard_up, shard_down = (s[None] for s in shards)
-
-    y_sum = lax.psum_scatter(
-        after(y_all, nears[turns[-1]]).reshape(-1, width), "blk", scatter_dimension=0, tiled=True,
-        axis_index_groups=same_core,
-    )
-    y_sum = after(y_sum, shard_key, grad_input)
-    block_out = (middle + y_sum.astype(f32)).astype(bf16)[None]
+        gg_own = gg_own + gg_from[k - 1].astype(f32)
+        down_own = down_own + down_from[k - 1].astype(f32)
+    shard_gate, shard_up = gg_own[None, :, :hidden_cols], gg_own[None, :, hidden_cols:]
+    shard_down = down_own[None]
+
+    y_sum = middle + y_near[0].astype(f32)
+    for k in range(1, groups):
+        y_sum = y_sum + swap_with(after(y_near[k], *returned), "blk", 4 * k).astype(f32)
+    block_out = y_sum.astype(bf16)[None]
     return (
         block_out, grad_input[None], shard_query, shard_key, shard_value, shard_out.T, shard_router.T,
         shard_gain_one[0], shard_gain_two[0], shard_gate, shard_up, shard_down,

time: 309 us -> 292 us (0.945)
  the two profiles are of different devices: /device:TPU:8 before, /device:TPU:0 now
where the time goes in v3:
time: 292 us; the launch traced here: 287 us
  waiting for transfers between devices  116 us (40%)
  starting transfers between devices  68.2 us (23%)
  Pallas kernels  63.7 us (22%)
  between operations  15.2 us (5%)
  local copies, waits for them, and re-layouts  8.77 us (3%)
  other arithmetic  7.96 us (3%)
  matrix products  6.52 us (2%)
    ppermute x51, waiting for transfers between devices, swap_with(): return lax.ppermute(value, axis, [(i, i ^ mask) for i in range(count)])  92.3 us
    ppermute x51, starting transfers between devices, swap_with(): return lax.ppermute(value, axis, [(i, i ^ mask) for i in range(count)])  60 us
    pallas_call x4, Pallas kernels, run_experts(): call(functools.partial(expert_body, experts, k, seqs), tuple((pltpu.HBM(d...  26.9 us
    pallas_call x2, Pallas kernels, expert_grads(): call(functools.partial(expert_grads_body, e, seqs), outs, limit=10 + 7 *...  12.8 us
    all_gather x1, waiting for transfers between devices, per_device(): lax.all_gather(jnp.concatenate([cot, out_own], axis=0), 'blk', axis=0, ax...  12.5 us
    ppermute x4, waiting for transfers between devices, shifted(): lax.ppermute(value, axis, [(i, i + steps) for i in range(leading, last)])  11.5 us
    pallas_call x1, Pallas kernels, per_device(): call(functools.partial(attend_back_body, scale), (shape_of((rows, q_cols)...  8.37 us
    ppermute x4, starting transfers between devices, shifted(): lax.ppermute(value, axis, [(i, i + steps) for i in range(leading, last)])  8.21 us
  transfers between devices with their start and end apart: 56, of which 30 were waited for; matrix products, arithmetic and copies ran while one was open for 5% of the time, Pallas kernels for 22%

profile of v3, /device:TPU:0, one launch (start us, length us, event | category | flops | bytes accessed | tf_op | source)
XLA Modules:
  0.0 286.6 jit_solution(12389801195392288913)
XLA Ops:
  40.8 4.6 %collective-permute-done.9 = bf16[64,1152]{1,0:T(8,128)(2,1)S(1)} collective-permute-done((bf16[64,1152]{1,0:T(8,128)(2,1)S(1)}, bf16[64,1152]{1,0:T(8,128)(2,1)S(1)}, u32[]{:S(2)}, u32[]{:S(2)}) %collective-permute-start.9) | collective-permute-done | bytes 147488 | tf_op jit(solution)/shard_map/ppermute | solution.py:27
  49.2 3.5 %collective-permute-start.11 = (bf16[256,512]{1,0:T(8,128)(2,1)S(1)}, bf16[256,512]{1,0:T(8,128)(2,1)S(1)}, u32[]{:S(2)}, u32[]{:S(2)}) collective-permute-start(bf16[256,512]{1,0:T(8,128)(2,1)S(1)} %get-tuple-element.112), channel_id=1, source_target_pairs={{0,2},{1,3},{2,4},{3,5},{4,6},{5,7},{6,8},{7,9},{8,10},{9,11},{10,... | collective-permute-start | bytes 786440 | tf_op jit(solution)/shard_map/ppermute | solution.py:33
  55.0 10.0 %collective-permute-done.11 = bf16[256,512]{1,0:T(8,128)(2,1)S(1)} collective-permute-done((bf16[256,512]{1,0:T(8,128)(2,1)S(1)}, bf16[256,512]{1,0:T(8,128)(2,1)S(1)}, u32[]{:S(2)}, u32[]{:S(2)}) %collective-permute-start.11) | collective-permute-done | bytes 262176 | tf_op jit(solution)/shard_map/ppermute | solution.py:33
  65.1 5.3 %shard_map.258 = (bf16[256,512]{1,0:T(8,128)(2,1)S(1)}, f32[256,512]{1,0:T(8,128)S(1)}) custom-call(bf16[256,512]{1,0:T(8,128)(2,1)S(1)} %get-tuple-element.111.q_ref, bf16[768,512]{1,0:T(8,128)(2,1)S(1)} %constant_dynamic-update-slice_fusion.6.kv_ref, f32[8,768]{1,0:T(8,128)S(1)} %maximum_maximum_fusion.1.meta_q.meta_k, ...), custom_call_target="tpu_custom_call" | custom-call | bytes 1572864 | tf_op jit(solution)/shard_map/pallas_call | solution.py:685
  72.1 12.5 %all-gather.3.cloned.1.call-done = bf16[1280,1024]{1,0:T(8,128)(2,1)} async-done(((bf16[160,1024]{1,0:T(8,128)(2,1)}), bf16[1280,1024]{1,0:T(8,128)(2,1)}) %all-gather.3.cloned.1.call-update) | async-done | bytes 2621456 | tf_op jit(solution)/shard_map/all_gather | solution.py:627
  92.4 6.5 %collective-permute-done.14.refs_1_ = bf16[128,1024]{1,0:T(8,128)(2,1)S(1)} collective-permute-done((bf16[128,1024]{1,0:T(8,128)(2,1)S(1)}, bf16[128,1024]{1,0:T(8,128)(2,1)S(1)}, u32[]{:S(2)}, u32[]{:S(2)}) %collective-permute-start.14) | collective-permute-done | bytes 262176 | tf_op jit(solution)/shard_map/ppermute | solution.py:27
  102.7 6.0 %collective-permute-done.17.refs_0_ = bf16[128,1152]{1,0:T(8,128)(2,1)S(1)} collective-permute-done((bf16[128,1152]{1,0:T(8,128)(2,1)S(1)}, bf16[128,1152]{1,0:T(8,128)(2,1)S(1)}, u32[]{:S(2)}, u32[]{:S(2)}) %collective-permute-start.17) | collective-permute-done | bytes 294944 | tf_op jit(solution)/shard_map/ppermute | solution.py:27
  110.7 4.6 %collective-permute-done.15.refs_0_ = bf16[128,1152]{1,0:T(8,128)(2,1)S(1)} collective-permute-done((bf16[128,1152]{1,0:T(8,128)(2,1)S(1)}, bf16[128,1152]{1,0:T(8,128)(2,1)S(1)}, u32[]{:S(2)}, u32[]{:S(2)}) %collective-permute-start.15) | collective-permute-done | bytes 294944 | tf_op jit(solution)/shard_map/ppermute | solution.py:27
  119.3 6.7 %shard_map.262 = (bf16[4,128,1024]{2,1,0:T(8,128)(2,1)}, bf16[4,128,1024]{2,1,0:T(8,128)(2,1)}, bf16[1024,1024]{1,0:T(8,128)(2,1)}, bf16[2,1024,512]{2,1,0:T(8,1...) custom-call(s32[1]{0:T(128)} %bitcast.8.blk_ref.me_ref, ...), custom_call_target="tpu_custom_call" | custom-call | flops 3221225472 | bytes 30539776 | tf_op jit(solution)/shard_map/pallas_call | solution.py:732
  130.2 6.7 %shard_map.263 = (bf16[4,128,1024]{2,1,0:T(8,128)(2,1)}, bf16[4,128,1024]{2,1,0:T(8,128)(2,1)}, bf16[1024,1024]{1,0:T(8,128)(2,1)}, bf16[2,1024,512]{2,1,0:T(8,1...) custom-call(s32[1]{0:T(128)} %bitcast.8.blk_ref.me_ref, ...), custom_call_target="tpu_custom_call", output_to_operand_aliasing={{0}: (9, {}), {1}: (10, {}), {2}: (11, {}), {3}: (12, {}), ... | custom-call | flops 3221225472 | bytes 30539776 | tf_op jit(solution)/shard_map/pallas_call | solution.py:732
  139.4 4.7 %collective-permute-done.25 = bf16[128,1152]{1,0:T(8,128)(2,1)S(1)} collective-permute-done((bf16[128,1152]{1,0:T(8,128)(2,1)S(1)}, bf16[128,1152]{1,0:T(8,128)(2,1)S(1)}, u32[]{:S(2)}, u32[]{:S(2)}) %collective-permute-start.25) | collective-permute-done | bytes 294944 | tf_op jit(solution)/shard_map/ppermute | solution.py:27
  148.0 6.9 %shard_map.264 = (bf16[4,128,1024]{2,1,0:T(8,128)(2,1)}, bf16[4,128,1024]{2,1,0:T(8,128)(2,1)}, bf16[1024,1024]{1,0:T(8,128)(2,1)}, bf16[2,1024,512]{2,1,0:T(8,1...) custom-call(s32[1]{0:T(128)} %bitcast.8.blk_ref.me_ref, ...), custom_call_target="tpu_custom_call", output_to_operand_aliasing={{0}: (9, {}), {1}: (10, {}), {2}: (11, {}), {3}: (12, {}), ... | custom-call | flops 3221225472 | bytes 30539776 | tf_op jit(solution)/shard_map/pallas_call | solution.py:732
  155.6 6.7 %shard_map.265 = (bf16[4,128,1024]{2,1,0:T(8,128)(2,1)}, bf16[4,128,1024]{2,1,0:T(8,128)(2,1)}, bf16[1024,1024]{1,0:T(8,128)(2,1)}, bf16[2,1024,512]{2,1,0:T(8,1...) custom-call(s32[1]{0:T(128)} %bitcast.8.blk_ref.me_ref, ...), custom_call_target="tpu_custom_call", output_to_operand_aliasing={{0}: (9, {}), {1}: (10, {}), {2}: (11, {}), {3}: (12, {}), ... | custom-call | flops 3221225472 | bytes 30539776 | tf_op jit(solution)/shard_map/pallas_call | solution.py:732
  164.5 4.6 %collective-permute-done.31 = bf16[128,1152]{1,0:T(8,128)(2,1)S(1)} collective-permute-done((bf16[128,1152]{1,0:T(8,128)(2,1)S(1)}, bf16[128,1152]{1,0:T(8,128)(2,1)S(1)}, u32[]{:S(2)}, u32[]{:S(2)}) %collective-permute-start.31) | collective-permute-done | bytes 294944 | tf_op jit(solution)/shard_map/ppermute | solution.py:27
  175.3 6.0 %shard_map.267 = bf16[2,768,1024]{2,1,0:T(8,128)(2,1)S(1)} custom-call(s32[1]{0:T(128)} %bitcast.me_ref.seq_ref, bf16[1024,1024]{1,0:T(8,128)(2,1)} %get-tuple-element.158.refs_0_, bf16[2,1024,1024]{2,1,0:T(8,128)(2,1)} %get-tuple-element.159.refs_1_, bf16[2,1024,512]{2,1,0:T(8,128)(2,1)} %get-tuple-element.160.refs_2_, ...), custom_call_target="tpu_custom_call" | custom-call | flops 3221225472 | bytes 6291456 | tf_op jit(solution)/shard_map/pallas_call | solution.py:789
  187.7 3.2 %collective-permute-done.33 = bf16[128,1024]{1,0:T(8,128)(2,1)S(1)} collective-permute-done((bf16[128,1024]{1,0:T(8,128)(2,1)S(1)}, bf16[128,1024]{1,0:T(8,128)(2,1)S(1)}, u32[]{:S(2)}, u32[]{:S(2)}) %collective-permute-start.33) | collective-permute-done | bytes 262176 | tf_op jit(solution)/shard_map/ppermute | solution.py:27
  191.4 8.4 %shard_map.268 = (bf16[256,512]{1,0:T(8,128)(2,1)S(1)}, bf16[256,512]{1,0:T(8,128)(2,1)S(1)}, bf16[256,512]{1,0:T(8,128)(2,1)S(1)}, f32[256,512]{1,0:T(8,128)S(1)}) custom-call(bf16[256,512]{1,0:T(8,128)(2,1)S(1)} %copy-done.8, bf16[768,512]{1,0:T(8,128)(2,1)S(1)} %copy-done.1, bf16[256,512]{1,0:T(8,128)(2,1)S(1)} %get-tuple-element.113.mixed_ref.mixed, ...), custom_call_target="tpu_custom_call" | custom-call | flops 2415919104 | bytes 2621440 | tf_op jit(solution)/shard_map/pallas_call | solution.py:807
  204.3 11.2 %collective-permute-done.32 = bf16[4,128,1024]{2,1,0:T(8,128)(2,1)S(1)} collective-permute-done((bf16[4,128,1024]{2,1,0:T(8,128)(2,1)S(1)}, bf16[4,128,1024]{2,1,0:T(8,128)(2,1)S(1)}, u32[]{:S(2)}, u32[]{:S(2)}) %collective-permute-start.32) | collective-permute-done | bytes 1048608 | tf_op jit(solution)/shard_map/ppermute | solution.py:27
  222.1 6.8 %shard_map.270 = (f32[512,1024]{1,0:T(8,128)S(1)}, f32[256,1024]{1,0:T(8,128)S(1)}, bf16[1,512,1024]{2,1,0:T(8,128)(2,1)S(1)}, bf16[1,256,1024]{2,1,0:T(8,128)(2,1)S(1)}) custom-call(s32[1]{0:T(128)} %bitcast.me_ref.seq_ref, bf16[1024,1024]{1,0:T(8,128)(2,1)} %get-tuple-element.158.refs_0_, bf16[2,1024,1024]{2,1,0:T(8,128)(2,1)} %get-tuple-element.159.refs_1_, ...), custom_call_target="tpu_custom_call" | custom-call | flops 3221225472 | bytes 9437184 | tf_op jit(solution)/shard_map/pallas_call | solution.py:789
  232.4 5.0 %collective-permute-done.37 = bf16[128,1024]{1,0:T(8,128)(2,1)S(1)} collective-permute-done((bf16[128,1024]{1,0:T(8,128)(2,1)S(1)}, bf16[128,1024]{1,0:T(8,128)(2,1)S(1)}, u32[]{:S(2)}, u32[]{:S(2)}) %collective-permute-start.37) | collective-permute-done | bytes 262176 | tf_op jit(solution)/shard_map/ppermute | solution.py:27
  242.6 4.3 %collective-permute-done.42 = bf16[4,64,1152]{2,1,0:T(8,128)(2,1)S(1)} collective-permute-done((bf16[4,64,1152]{2,1,0:T(8,128)(2,1)S(1)}, bf16[4,64,1152]{2,1,0:T(8,128)(2,1)S(1)}, u32[]{:S(2)}, u32[]{:S(2)}) %collective-permute-start.42) | collective-permute-done | bytes 589856 | tf_op jit(solution)/shard_map/ppermute | solution.py:27
  251.6 4.3 %collective-permute-done.43 = bf16[64,1152]{1,0:T(8,128)(2,1)S(1)} collective-permute-done((bf16[64,1152]{1,0:T(8,128)(2,1)S(1)}, bf16[64,1152]{1,0:T(8,128)(2,1)S(1)}, u32[]{:S(2)}, u32[]{:S(2)}) %collective-permute-start.43) | collective-permute-done | bytes 147488 | tf_op jit(solution)/shard_map/ppermute | solution.py:27
  257.0 3.8 %collective-permute-done.44 = bf16[64,1152]{1,0:T(8,128)(2,1)S(1)} collective-permute-done((bf16[64,1152]{1,0:T(8,128)(2,1)S(1)}, bf16[64,1152]{1,0:T(8,128)(2,1)S(1)}, u32[]{:S(2)}, u32[]{:S(2)}) %collective-permute-start.44) | collective-permute-done | bytes 147488 | tf_op jit(solution)/shard_map/ppermute | solution.py:27
  272.3 4.1 %collective-permute-done.46.refs_1_ = bf16[32,1152]{1,0:T(8,128)(2,1)S(1)} collective-permute-done((bf16[32,1152]{1,0:T(8,128)(2,1)S(1)}, bf16[32,1152]{1,0:T(8,128)(2,1)S(1)}, u32[]{:S(2)}, u32[]{:S(2)}) %collective-permute-start.46) | collective-permute-done | bytes 73760 | tf_op jit(solution)/shard_map/ppermute | solution.py:27
  (250 shorter events, 125.3 us)
Async XLA Ops:
  7.2 77.4 %all-gather.3.cloned.1.call-start = ((), (), s32[]{:S(2)}) async-start(), calls=%async_computation | async-start | bytes 2949120 | tf_op jit(solution)/shard_map/all_gather | solution.py:627
  16.5 17.3 %collective-permute-start.3 = (bf16[64,1152]{1,0:T(8,128)(2,1)S(1)}, bf16[64,1152]{1,0:T(8,128)(2,1)S(1)}, u32[]{:S(2)}, u32[]{:S(2)}) collective-permute-start(bf16[64,1152]{1,0:T(8,128)(2,1)S(1)} %slice.152), channel_id=1, source_target_pairs={{0,4},{1,5},{2,6},{3,7},{4,0},{5,1},{6,2},{7,3},{8,12},{9,13},{10,... | collective-permute-start | bytes 442376 | tf_op jit(solution)/shard_map/ppermute | solution.py:27
  18.3 18.8 %collective-permute-start.2 = (bf16[64,1152]{1,0:T(8,128)(2,1)S(1)}, bf16[64,1152]{1,0:T(8,128)(2,1)S(1)}, u32[]{:S(2)}, u32[]{:S(2)}) collective-permute-start(bf16[64,1152]{1,0:T(8,128)(2,1)S(1)} %slice.152), channel_id=1, source_target_pairs={{0,2},{1,3},{2,0},{3,1},{4,6},{5,7},{6,4},{7,5},{8,10},{9,11},{10,... | collective-permute-start | bytes 442376 | tf_op jit(solution)/shard_map/ppermute | solution.py:27
  35.2 51.0 %collective-permute-start.19 = (bf16[768,1024]{1,0:T(8,128)(2,1)}, bf16[768,1024]{1,0:T(8,128)(2,1)}, u32[]{:S(2)}, u32[]{:S(2)}) collective-permute-start(bf16[768,1024]{1,0:T(8,128)(2,1)} %pad_maximum_fusion.refs_3_), channel_id=1, source_target_pairs={{0,16},{16,0},{1,17},{17,1},{2,18},{18,2},{3,19},{19,3},{4,20},{20... | collective-permute-start | bytes 4718600 | tf_op jit(solution)/shard_map/ppermute | solution.py:27
  49.2 15.7 %collective-permute-start.11 = (bf16[256,512]{1,0:T(8,128)(2,1)S(1)}, bf16[256,512]{1,0:T(8,128)(2,1)S(1)}, u32[]{:S(2)}, u32[]{:S(2)}) collective-permute-start(bf16[256,512]{1,0:T(8,128)(2,1)S(1)} %get-tuple-element.112), channel_id=1, source_target_pairs={{0,2},{1,3},{2,4},{3,5},{4,6},{5,7},{6,8},{7,9},{8,10},{9,11},{10,... | collective-permute-start | bytes 786440 | tf_op jit(solution)/shard_map/ppermute | solution.py:33
  85.8 29.5 %collective-permute-start.20 = (bf16[768,1024]{1,0:T(8,128)(2,1)}, bf16[768,1024]{1,0:T(8,128)(2,1)S(1)}, u32[]{:S(2)}, u32[]{:S(2)}) collective-permute-start(bf16[768,1024]{1,0:T(8,128)(2,1)} %pad_maximum_fusion.refs_3_), channel_id=1, source_target_pairs={{0,1},{1,0},{2,3},{3,2},{4,5},{5,4},{6,7},{7,6},{8,9},{9,8},{10,11... | collective-permute-start | bytes 4718600 | tf_op jit(solution)/shard_map/ppermute | solution.py:27
  86.3 30.4 %collective-permute-start.21 = (bf16[768,1024]{1,0:T(8,128)(2,1)}, bf16[768,1024]{1,0:T(8,128)(2,1)S(1)}, u32[]{:S(2)}, u32[]{:S(2)}) collective-permute-start(bf16[768,1024]{1,0:T(8,128)(2,1)} %collective-permute-done.19.refs_4_), channel_id=1, source_target_pairs={{0,1},{1,0},{2,3},{3,2},{4,5},{5,4},{6,7},{7,6},{8,9},{9,8},{10,11... | collective-permute-start | bytes 4718600 | tf_op jit(solution)/shard_map/ppermute | solution.py:27
  100.8 14.5 %collective-permute-start.15 = (bf16[128,1152]{1,0:T(8,128)(2,1)S(1)}, bf16[128,1152]{1,0:T(8,128)(2,1)S(1)}, u32[]{:S(2)}, u32[]{:S(2)}) collective-permute-start(bf16[128,1152]{1,0:T(8,128)(2,1)S(1)} %get-tuple-element.145.refs_0_), channel_id=1, source_target_pairs={{0,12},{1,13},{2,14},{3,15},{4,8},{5,9},{6,10},{7,11},{8,4},{9,5},... | collective-permute-start | bytes 884744 | tf_op jit(solution)/shard_map/ppermute | solution.py:27
  109.7 45.2 %collective-permute-start.26 = (bf16[128,1152]{1,0:T(8,128)(2,1)S(1)}, bf16[128,1152]{1,0:T(8,128)(2,1)S(1)}, u32[]{:S(2)}, u32[]{:S(2)}) collective-permute-start(bf16[128,1152]{1,0:T(8,128)(2,1)S(1)} %get-tuple-element.145.refs_0_), channel_id=1, source_target_pairs={{0,2},{1,3},{2,0},{3,1},{4,6},{5,7},{6,4},{7,5},{8,10},{9,11},{10,... | collective-permute-start | bytes 884744 | tf_op jit(solution)/shard_map/ppermute | solution.py:27
  115.3 23.0 %collective-permute-start.16 = (bf16[128,1152]{1,0:T(8,128)(2,1)S(1)}, bf16[128,1152]{1,0:T(8,128)(2,1)S(1)}, u32[]{:S(2)}, u32[]{:S(2)}) collective-permute-start(bf16[128,1152]{1,0:T(8,128)(2,1)S(1)} %get-tuple-element.145.refs_0_), channel_id=1, source_target_pairs={{0,8},{1,9},{2,10},{3,11},{4,12},{5,13},{6,14},{7,15},{8,0},{9,1},... | collective-permute-start | bytes 884744 | tf_op jit(solution)/shard_map/ppermute | solution.py:27
  115.3 14.2 %collective-permute-start.22 = (bf16[128,1152]{1,0:T(8,128)(2,1)S(1)}, bf16[128,1152]{1,0:T(8,128)(2,1)S(1)}, u32[]{:S(2)}, u32[]{:S(2)}) collective-permute-start(bf16[128,1152]{1,0:T(8,128)(2,1)S(1)} %collective-permute-done.15.refs_0_), channel_id=1, source_target_pairs={{0,2},{1,3},{2,0},{3,1},{4,6},{5,7},{6,4},{7,5},{8,10},{9,11},{10,... | collective-permute-start | bytes 884744 | tf_op jit(solution)/shard_map/ppermute | solution.py:27
  139.1 42.3 %collective-permute-start.27 = (bf16[128,1152]{1,0:T(8,128)(2,1)S(1)}, bf16[128,1152]{1,0:T(8,128)(2,1)S(1)}, u32[]{:S(2)}, u32[]{:S(2)}) collective-permute-start(bf16[128,1152]{1,0:T(8,128)(2,1)S(1)} %fusion.21), channel_id=1, source_target_pairs={{0,4},{1,5},{2,6},{3,7},{4,0},{5,1},{6,2},{7,3},{8,12},{9,13},{10,... | collective-permute-start | bytes 884744 | tf_op jit(solution)/shard_map/ppermute | solution.py:27
  144.2 37.2 %collective-permute-start.28 = (bf16[128,1152]{1,0:T(8,128)(2,1)S(1)}, bf16[128,1152]{1,0:T(8,128)(2,1)S(1)}, u32[]{:S(2)}, u32[]{:S(2)}) collective-permute-start(bf16[128,1152]{1,0:T(8,128)(2,1)S(1)} %fusion.20), channel_id=1, source_target_pairs={{0,12},{1,13},{2,14},{3,15},{4,8},{5,9},{6,10},{7,11},{8,4},{9,5},... | collective-permute-start | bytes 884744 | tf_op jit(solution)/shard_map/ppermute | solution.py:27
  181.3 40.8 %collective-permute-start.40 = (bf16[2,768,1024]{2,1,0:T(8,128)(2,1)S(1)}, bf16[2,768,1024]{2,1,0:T(8,128)(2,1)S(1)}, u32[]{:S(2)}, u32[]{:S(2)}) collective-permute-start(bf16[2,768,1024]{2,1,0:T(8,128)(2,1)S(1)} %shard_map.267), channel_id=1, source_target_pairs={{0,1},{1,0},{2,3},{3,2},{4,5},{5,4},{6,7},{7,6},{8,9},{9,8},{10,11... | collective-permute-start | bytes 9437192 | tf_op jit(solution)/shard_map/ppermute | solution.py:27
  185.7 29.7 %collective-permute-start.32 = (bf16[4,128,1024]{2,1,0:T(8,128)(2,1)S(1)}, bf16[4,128,1024]{2,1,0:T(8,128)(2,1)S(1)}, u32[]{:S(2)}, u32[]{:S(2)}) collective-permute-start(bf16[4,128,1024]{2,1,0:T(8,128)(2,1)S(1)} %copy-done.18), channel_id=1, source_target_pairs={{0,2},{1,3},{2,0},{3,1},{4,6},{5,7},{6,4},{7,5},{8,10},{9,11},{10,... | collective-permute-start | bytes 3145736 | tf_op jit(solution)/shard_map/ppermute | solution.py:27
  201.6 20.2 %collective-permute-start.39 = (bf16[512,1152]{1,0:T(8,128)(2,1)S(1)}, bf16[512,1152]{1,0:T(8,128)(2,1)S(1)}, u32[]{:S(2)}, u32[]{:S(2)}) collective-permute-start(bf16[512,1152]{1,0:T(8,128)(2,1)S(1)} %get-tuple-element.174), channel_id=1, source_target_pairs={{0,1},{1,0},{2,3},{3,2},{4,5},{5,4},{6,7},{7,6},{8,9},{9,8},{10,11... | collective-permute-start | bytes 3538952 | tf_op jit(solution)/shard_map/ppermute | solution.py:27
  201.7 14.3 %collective-permute-start.34 = (bf16[256,512]{1,0:T(8,128)(2,1)S(1)}, bf16[256,512]{1,0:T(8,128)(2,1)S(1)}, u32[]{:S(2)}, u32[]{:S(2)}) collective-permute-start(bf16[256,512]{1,0:T(8,128)(2,1)S(1)} %get-tuple-element.164), channel_id=1, source_target_pairs={{1,0},{2,1},{3,2},{4,3},{5,4},{6,5},{7,6},{8,7},{9,8},{10,9},{11,1... | collective-permute-start | bytes 786440 | tf_op jit(solution)/shard_map/ppermute | solution.py:33
  203.0 14.4 %collective-permute-start.35 = (bf16[256,512]{1,0:T(8,128)(2,1)S(1)}, bf16[256,512]{1,0:T(8,128)(2,1)S(1)}, u32[]{:S(2)}, u32[]{:S(2)}) collective-permute-start(bf16[256,512]{1,0:T(8,128)(2,1)S(1)} %get-tuple-element.165), channel_id=1, source_target_pairs={{2,0},{3,1},{4,2},{5,3},{6,4},{7,5},{8,6},{9,7},{10,8},{11,9},{12,... | collective-permute-start | bytes 786440 | tf_op jit(solution)/shard_map/ppermute | solution.py:33
  217.4 14.9 %collective-permute-start.36 = (bf16[128,1024]{1,0:T(8,128)(2,1)S(1)}, bf16[128,1024]{1,0:T(8,128)(2,1)S(1)}, u32[]{:S(2)}, u32[]{:S(2)}) collective-permute-start(bf16[128,1024]{1,0:T(8,128)(2,1)S(1)} %get-tuple-element.166), channel_id=1, source_target_pairs={{0,4},{1,5},{2,6},{3,7},{4,0},{5,1},{6,2},{7,3},{8,12},{9,13},{10,... | collective-permute-start | bytes 786440 | tf_op jit(solution)/shard_map/ppermute | solution.py:27
  217.4 20.0 %collective-permute-start.37 = (bf16[128,1024]{1,0:T(8,128)(2,1)S(1)}, bf16[128,1024]{1,0:T(8,128)(2,1)S(1)}, u32[]{:S(2)}, u32[]{:S(2)}) collective-permute-start(bf16[128,1024]{1,0:T(8,128)(2,1)S(1)} %get-tuple-element.167), channel_id=1, source_target_pairs={{0,8},{1,9},{2,10},{3,11},{4,12},{5,13},{6,14},{7,15},{8,0},{9,1},... | collective-permute-start | bytes 786440 | tf_op jit(solution)/shard_map/ppermute | solution.py:27
  219.9 17.5 %collective-permute-start.38 = (bf16[128,1024]{1,0:T(8,128)(2,1)S(1)}, bf16[128,1024]{1,0:T(8,128)(2,1)S(1)}, u32[]{:S(2)}, u32[]{:S(2)}) collective-permute-start(bf16[128,1024]{1,0:T(8,128)(2,1)S(1)} %get-tuple-element.168), channel_id=1, source_target_pairs={{0,12},{1,13},{2,14},{3,15},{4,8},{5,9},{6,10},{7,11},{8,4},{9,5},... | collective-permute-start | bytes 786440 | tf_op jit(solution)/shard_map/ppermute | solution.py:27
  231.1 15.8 %collective-permute-start.42 = (bf16[4,64,1152]{2,1,0:T(8,128)(2,1)S(1)}, bf16[4,64,1152]{2,1,0:T(8,128)(2,1)S(1)}, u32[]{:S(2)}, u32[]{:S(2)}) collective-permute-start(bf16[4,64,1152]{2,1,0:T(8,128)(2,1)S(1)} %slice_bitcast_fusion.2), channel_id=1, source_target_pairs={{0,2},{1,3},{2,0},{3,1},{4,6},{5,7},{6,4},{7,5},{8,10},{9,11},{10,... | collective-permute-start | bytes 1769480 | tf_op jit(solution)/shard_map/ppermute | solution.py:27
  238.3 32.9 %collective-permute-start.54 = (bf16[256,1024]{1,0:T(8,128)(2,1)S(1)}, bf16[256,1024]{1,0:T(8,128)(2,1)S(1)}, u32[]{:S(2)}, u32[]{:S(2)}) collective-permute-start(bf16[256,1024]{1,0:T(8,128)(2,1)S(1)} %bitcast.128), channel_id=1, source_target_pairs={{0,16},{16,0},{1,17},{17,1},{2,18},{18,2},{3,19},{19,3},{4,20},{20... | collective-permute-start | bytes 1572872 | tf_op jit(solution)/shard_map/ppermute | solution.py:27
  239.7 37.9 %collective-permute-start.53 = (bf16[512,1024]{1,0:T(8,128)(2,1)S(1)}, bf16[512,1024]{1,0:T(8,128)(2,1)S(1)}, u32[]{:S(2)}, u32[]{:S(2)}) collective-permute-start(bf16[512,1024]{1,0:T(8,128)(2,1)S(1)} %bitcast.127), channel_id=1, source_target_pairs={{0,16},{16,0},{1,17},{17,1},{2,18},{18,2},{3,19},{19,3},{4,20},{20... | collective-permute-start | bytes 3145736 | tf_op jit(solution)/shard_map/ppermute | solution.py:27
  (69 other events, 635.6 us)
Sparse Core Ops, SparseCore 0:
  16.4 68.1 all-gather.2

commit v4 on v3

--- a/solution.py
+++ b/solution.py
@@ -234,21 +234,24 @@
                 kv_ref[:, at - q_cols : at - q_cols + LANES] = turned(tile, cos_k, sin_k).astype(bf16)
 
 
-def visible_keys(meta_q, meta_k):
-    mine = meta_q[...].T
-    theirs = meta_k[...]
-    return (theirs[1:2, :] <= mine[:, 1:2]) & (theirs[0:1, :] == mine[:, 0:1])
-
-
-def attend_body(scale, q_ref, kv_ref, meta_q, meta_k, out_ref, lse_ref):
-    visible = visible_keys(meta_q, meta_k)
-    q = q_ref[...].astype(f32)
+def hide_keys(meta_q, meta_k, bias_ref):
+    @pl.when((pl.program_id(0) == 0) | (pl.num_programs(1) > 1))
+    def _():
+        mine = meta_q[...].T
+        theirs = meta_k[...]
+        visible = (theirs[1:2, :] <= mine[:, 1:2]) & (theirs[0:1, :] == mine[:, 0:1])
+        bias_ref[...] = jnp.where(visible, 0.0, neg_large)
+
+
+def attend_body(scale, q_ref, kv_ref, meta_q, meta_k, out_ref, lse_ref, bias_ref):
+    hide_keys(meta_q, meta_k, bias_ref)
+    q = q_ref[...].astype(f32) * scale
     kv = kv_ref[...]
     low = lane_ids(q.shape) < HEAD_DIM
     outs, lses = [], []
     for half in range(2):
         head = jnp.where(low, pltpu.roll(q, HEAD_DIM, 1) if half else q, 0.0).astype(bf16)
-        scores = jnp.where(visible, nt(head, kv) * scale, neg_large)
+        scores = nt(head, kv) + bias_ref[...]
         most = jnp.max(scores, axis=-1, keepdims=True)
         weights = jnp.exp(scores - most)
         total = jnp.sum(weights, axis=-1, keepdims=True)
@@ -261,9 +264,9 @@
 def attend_back_body(
     scale, q_ref, kv_ref, mixed_ref, grad_ref, lse_ref, meta_q, meta_k, cos, sin, dq_ref, *outs
 ):
-    outs, dkv_ref = outs[:-1], outs[-1]
-    visible = visible_keys(meta_q, meta_k)
-    q = q_ref[...].astype(f32)
+    outs, dkv_ref, bias_ref = outs[:-2], outs[-2], outs[-1]
+    hide_keys(meta_q, meta_k, bias_ref)
+    q = q_ref[...].astype(f32) * scale
     kv = kv_ref[...]
     grad = grad_ref[...].astype(f32)
     low = lane_ids(q.shape) < HEAD_DIM
@@ -276,10 +279,10 @@
         grad_head = jnp.where(low, 0.0, grad if half else pltpu.roll(grad, HEAD_DIM, 1)).astype(bf16)
         delta = jnp.sum(jnp.where(low == (half == 0), product, 0.0), axis=-1, keepdims=True)
         lse_head = lse[:, HEAD_DIM * half : HEAD_DIM * half + 1]
-        probs = jnp.where(visible, jnp.exp(nt(head, kv) * scale - lse_head), 0.0)
+        probs = jnp.exp(nt(head, kv) + (bias_ref[...] - lse_head))
         grad_scores = (probs * (nt(grad_head, kv) - delta)).astype(bf16)
         dqs.append(nn(grad_scores, kv) * scale)
-        term = tn(grad_scores, head) * scale + tn(probs.astype(bf16), grad_head)
+        term = tn(grad_scores, head) + tn(probs.astype(bf16), grad_head)
         dkv = term if dkv is None else dkv + term
     dq = jnp.where(low, dqs[0], pltpu.roll(dqs[1], HEAD_DIM, 1)).astype(bf16).astype(f32)
     dq_ref[...] = turned(dq, cos[...], sin[...], back=True).astype(bf16)
@@ -689,6 +692,7 @@
         grid=grid,
         in_specs=[row_block, key_block, meta_q_block, meta_k_block],
         out_specs=(row_block, row_block),
+        scratch_shapes=[pltpu.VMEM((step, keys), f32)],
     )(q_all, kv_keys, meta, meta)
 
     packs += [swap_with(after(p, mixed), "blk", 1) for p in packs]
@@ -815,7 +819,7 @@
         in_specs=[row_block, key_block, row_block, row_block, row_block, meta_q_block, meta_k_block,
                   table_block, table_block],
         out_specs=(row_block,) + (block_spec,) * (hops + 1),
-        scratch_shapes=[pltpu.VMEM((keys, LANES), f32)],
+        scratch_shapes=[pltpu.VMEM((keys, LANES), f32), pltpu.VMEM((step, keys), f32)],
     )(q_all, kv_keys, mixed, grad_mixed, lse, meta, meta, cos, sin)
     returned = [shifted(grad_kv[hops - n], "blk", -n) for n in range(1, hops + 1)]
     spare = max(1, seqs - 1)
@@ -875,7 +879,7 @@
 
     y_sum = middle + y_near[0].astype(f32)
     for k in range(1, groups):
-        y_sum = y_sum + swap_with(after(y_near[k], *returned), "blk", 4 * k).astype(f32)
+        y_sum = y_sum + swap_with(y_near[k], "blk", 4 * k).astype(f32)
     block_out = y_sum.astype(bf16)[None]
     return (
         block_out, grad_input[None], shard_query, shard_key, shard_value, shard_out.T, shard_router.T,

time: 292 us -> 291 us (level)
  waiting for transfers between devices: 116 us -> 113 us
  transfers between devices with their start and end apart: 56 -> 56, of which waited for: 30 -> 29; matrix products, arithmetic and copies ran while one was open for 5% -> 5% of each run, Pallas kernels for 22% -> 22%
where the time goes in v4:
time: 291 us; the launch traced here: 285 us
  waiting for transfers between devices  113 us (39%)
  starting transfers between devices  70.9 us (24%)
  Pallas kernels  62.9 us (22%)
  between operations  15.2 us (5%)
  local copies, waits for them, and re-layouts  8.77 us (3%)
  other arithmetic  7.96 us (3%)
  matrix products  6.52 us (2%)
    ppermute x51, waiting for transfers between devices, swap_with(): return lax.ppermute(value, axis, [(i, i ^ mask) for i in range(count)])  90.2 us
    ppermute x51, starting transfers between devices, swap_with(): return lax.ppermute(value, axis, [(i, i ^ mask) for i in range(count)])  62.6 us
    pallas_call x4, Pallas kernels, run_experts(): call(functools.partial(expert_body, experts, k, seqs), tuple((pltpu.HBM(d...  26.9 us
    all_gather x1, waiting for transfers between devices, per_device(): lax.all_gather(jnp.concatenate([cot, out_own], axis=0), 'blk', axis=0, ax...  13 us
    pallas_call x2, Pallas kernels, expert_grads(): call(functools.partial(expert_grads_body, e, seqs), outs, limit=10 + 7 *...  12.8 us
    ppermute x4, waiting for transfers between devices, shifted(): lax.ppermute(value, axis, [(i, i + steps) for i in range(leading, last)])  10 us
    ppermute x4, starting transfers between devices, shifted(): lax.ppermute(value, axis, [(i, i + steps) for i in range(leading, last)])  8.21 us
    pallas_call x1, Pallas kernels, per_device(): call(functools.partial(attend_back_body, scale), (shape_of((rows, q_cols)...  7.98 us
  transfers between devices with their start and end apart: 56, of which 29 were waited for; matrix products, arithmetic and copies ran while one was open for 5% of the time, Pallas kernels for 22%

profile of v4, /device:TPU:0, one launch (start us, length us, event | category | flops | bytes accessed | tf_op | source)
XLA Modules:
  0.0 285.4 jit_solution(15051766366097683104)
XLA Ops:
  40.8 4.6 %collective-permute-done.9 = bf16[64,1152]{1,0:T(8,128)(2,1)S(1)} collective-permute-done((bf16[64,1152]{1,0:T(8,128)(2,1)S(1)}, bf16[64,1152]{1,0:T(8,128)(2,1)S(1)}, u32[]{:S(2)}, u32[]{:S(2)}) %collective-permute-start.9) | collective-permute-done | bytes 147488 | tf_op jit(solution)/shard_map/ppermute | solution.py:27
  49.2 3.5 %collective-permute-start.11 = (bf16[256,512]{1,0:T(8,128)(2,1)S(1)}, bf16[256,512]{1,0:T(8,128)(2,1)S(1)}, u32[]{:S(2)}, u32[]{:S(2)}) collective-permute-start(bf16[256,512]{1,0:T(8,128)(2,1)S(1)} %get-tuple-element.109), channel_id=1, source_target_pairs={{0,2},{1,3},{2,4},{3,5},{4,6},{5,7},{6,8},{7,9},{8,10},{9,11},{10,... | collective-permute-start | bytes 786440 | tf_op jit(solution)/shard_map/ppermute | solution.py:33
  55.0 10.0 %collective-permute-done.11 = bf16[256,512]{1,0:T(8,128)(2,1)S(1)} collective-permute-done((bf16[256,512]{1,0:T(8,128)(2,1)S(1)}, bf16[256,512]{1,0:T(8,128)(2,1)S(1)}, u32[]{:S(2)}, u32[]{:S(2)}) %collective-permute-start.11) | collective-permute-done | bytes 262176 | tf_op jit(solution)/shard_map/ppermute | solution.py:33
  65.1 4.8 %shard_map.258 = (bf16[256,512]{1,0:T(8,128)(2,1)S(1)}, f32[256,512]{1,0:T(8,128)S(1)}) custom-call(bf16[256,512]{1,0:T(8,128)(2,1)S(1)} %get-tuple-element.108.q_ref, bf16[768,512]{1,0:T(8,128)(2,1)S(1)} %constant_dynamic-update-slice_fusion.6.kv_ref, f32[8,768]{1,0:T(8,128)S(1)} %maximum_maximum_fusion.1.meta_q.meta_k, ...), custom_call_target="tpu_custom_call" | custom-call | bytes 1572864 | tf_op jit(solution)/shard_map/pallas_call | solution.py:688
  71.6 13.0 %all-gather.3.cloned.1.call-done = bf16[1280,1024]{1,0:T(8,128)(2,1)} async-done(((bf16[160,1024]{1,0:T(8,128)(2,1)}), bf16[1280,1024]{1,0:T(8,128)(2,1)}) %all-gather.3.cloned.1.call-update) | async-done | bytes 2621456 | tf_op jit(solution)/shard_map/all_gather | solution.py:630
  92.4 6.5 %collective-permute-done.14.refs_1_ = bf16[128,1024]{1,0:T(8,128)(2,1)S(1)} collective-permute-done((bf16[128,1024]{1,0:T(8,128)(2,1)S(1)}, bf16[128,1024]{1,0:T(8,128)(2,1)S(1)}, u32[]{:S(2)}, u32[]{:S(2)}) %collective-permute-start.14) | collective-permute-done | bytes 262176 | tf_op jit(solution)/shard_map/ppermute | solution.py:27
  102.7 6.0 %collective-permute-done.17.refs_0_ = bf16[128,1152]{1,0:T(8,128)(2,1)S(1)} collective-permute-done((bf16[128,1152]{1,0:T(8,128)(2,1)S(1)}, bf16[128,1152]{1,0:T(8,128)(2,1)S(1)}, u32[]{:S(2)}, u32[]{:S(2)}) %collective-permute-start.17) | collective-permute-done | bytes 294944 | tf_op jit(solution)/shard_map/ppermute | solution.py:27
  110.7 4.6 %collective-permute-done.15.refs_0_ = bf16[128,1152]{1,0:T(8,128)(2,1)S(1)} collective-permute-done((bf16[128,1152]{1,0:T(8,128)(2,1)S(1)}, bf16[128,1152]{1,0:T(8,128)(2,1)S(1)}, u32[]{:S(2)}, u32[]{:S(2)}) %collective-permute-start.15) | collective-permute-done | bytes 294944 | tf_op jit(solution)/shard_map/ppermute | solution.py:27
  119.3 6.7 %shard_map.262 = (bf16[4,128,1024]{2,1,0:T(8,128)(2,1)}, bf16[4,128,1024]{2,1,0:T(8,128)(2,1)}, bf16[1024,1024]{1,0:T(8,128)(2,1)}, bf16[2,1024,512]{2,1,0:T(8,1...) custom-call(s32[1]{0:T(128)} %bitcast.8.blk_ref.me_ref, ...), custom_call_target="tpu_custom_call" | custom-call | flops 3221225472 | bytes 30539776 | tf_op jit(solution)/shard_map/pallas_call | solution.py:736
  130.2 6.7 %shard_map.263 = (bf16[4,128,1024]{2,1,0:T(8,128)(2,1)}, bf16[4,128,1024]{2,1,0:T(8,128)(2,1)}, bf16[1024,1024]{1,0:T(8,128)(2,1)}, bf16[2,1024,512]{2,1,0:T(8,1...) custom-call(s32[1]{0:T(128)} %bitcast.8.blk_ref.me_ref, ...), custom_call_target="tpu_custom_call", output_to_operand_aliasing={{0}: (9, {}), {1}: (10, {}), {2}: (11, {}), {3}: (12, {}), ... | custom-call | flops 3221225472 | bytes 30539776 | tf_op jit(solution)/shard_map/pallas_call | solution.py:736
  139.4 4.7 %collective-permute-done.25 = bf16[128,1152]{1,0:T(8,128)(2,1)S(1)} collective-permute-done((bf16[128,1152]{1,0:T(8,128)(2,1)S(1)}, bf16[128,1152]{1,0:T(8,128)(2,1)S(1)}, u32[]{:S(2)}, u32[]{:S(2)}) %collective-permute-start.25) | collective-permute-done | bytes 294944 | tf_op jit(solution)/shard_map/ppermute | solution.py:27
  148.0 6.9 %shard_map.264 = (bf16[4,128,1024]{2,1,0:T(8,128)(2,1)}, bf16[4,128,1024]{2,1,0:T(8,128)(2,1)}, bf16[1024,1024]{1,0:T(8,128)(2,1)}, bf16[2,1024,512]{2,1,0:T(8,1...) custom-call(s32[1]{0:T(128)} %bitcast.8.blk_ref.me_ref, ...), custom_call_target="tpu_custom_call", output_to_operand_aliasing={{0}: (9, {}), {1}: (10, {}), {2}: (11, {}), {3}: (12, {}), ... | custom-call | flops 3221225472 | bytes 30539776 | tf_op jit(solution)/shard_map/pallas_call | solution.py:736
  155.6 6.7 %shard_map.265 = (bf16[4,128,1024]{2,1,0:T(8,128)(2,1)}, bf16[4,128,1024]{2,1,0:T(8,128)(2,1)}, bf16[1024,1024]{1,0:T(8,128)(2,1)}, bf16[2,1024,512]{2,1,0:T(8,1...) custom-call(s32[1]{0:T(128)} %bitcast.8.blk_ref.me_ref, ...), custom_call_target="tpu_custom_call", output_to_operand_aliasing={{0}: (9, {}), {1}: (10, {}), {2}: (11, {}), {3}: (12, {}), ... | custom-call | flops 3221225472 | bytes 30539776 | tf_op jit(solution)/shard_map/pallas_call | solution.py:736
  164.5 4.6 %collective-permute-done.31 = bf16[128,1152]{1,0:T(8,128)(2,1)S(1)} collective-permute-done((bf16[128,1152]{1,0:T(8,128)(2,1)S(1)}, bf16[128,1152]{1,0:T(8,128)(2,1)S(1)}, u32[]{:S(2)}, u32[]{:S(2)}) %collective-permute-start.31) | collective-permute-done | bytes 294944 | tf_op jit(solution)/shard_map/ppermute | solution.py:27
  175.3 6.0 %shard_map.267 = bf16[2,768,1024]{2,1,0:T(8,128)(2,1)S(1)} custom-call(s32[1]{0:T(128)} %bitcast.me_ref.seq_ref, bf16[1024,1024]{1,0:T(8,128)(2,1)} %get-tuple-element.155.refs_0_, bf16[2,1024,1024]{2,1,0:T(8,128)(2,1)} %get-tuple-element.156.refs_1_, bf16[2,1024,512]{2,1,0:T(8,128)(2,1)} %get-tuple-element.157.refs_2_, ...), custom_call_target="tpu_custom_call" | custom-call | flops 3221225472 | bytes 6291456 | tf_op jit(solution)/shard_map/pallas_call | solution.py:793
  187.7 3.2 %collective-permute-done.36 = bf16[128,1024]{1,0:T(8,128)(2,1)S(1)} collective-permute-done((bf16[128,1024]{1,0:T(8,128)(2,1)S(1)}, bf16[128,1024]{1,0:T(8,128)(2,1)S(1)}, u32[]{:S(2)}, u32[]{:S(2)}) %collective-permute-start.36) | collective-permute-done | bytes 262176 | tf_op jit(solution)/shard_map/ppermute | solution.py:27
  191.4 8.0 %shard_map.268 = (bf16[256,512]{1,0:T(8,128)(2,1)S(1)}, bf16[256,512]{1,0:T(8,128)(2,1)S(1)}, bf16[256,512]{1,0:T(8,128)(2,1)S(1)}, f32[256,512]{1,0:T(8,128)S(1)}) custom-call(bf16[256,512]{1,0:T(8,128)(2,1)S(1)} %copy-done.8, bf16[768,512]{1,0:T(8,128)(2,1)S(1)} %copy-done.1, bf16[256,512]{1,0:T(8,128)(2,1)S(1)} %get-tuple-element.110.mixed_ref.mixed, ...), custom_call_target="tpu_custom_call" | custom-call | flops 2415919104 | bytes 2621440 | tf_op jit(solution)/shard_map/pallas_call | solution.py:811
  203.9 10.3 %collective-permute-done.32 = bf16[4,128,1024]{2,1,0:T(8,128)(2,1)S(1)} collective-permute-done((bf16[4,128,1024]{2,1,0:T(8,128)(2,1)S(1)}, bf16[4,128,1024]{2,1,0:T(8,128)(2,1)S(1)}, u32[]{:S(2)}, u32[]{:S(2)}) %collective-permute-start.32) | collective-permute-done | bytes 1048608 | tf_op jit(solution)/shard_map/ppermute | solution.py:27
  219.5 6.8 %shard_map.270 = (f32[512,1024]{1,0:T(8,128)S(1)}, f32[256,1024]{1,0:T(8,128)S(1)}, bf16[1,512,1024]{2,1,0:T(8,128)(2,1)S(1)}, bf16[1,256,1024]{2,1,0:T(8,128)(2,1)S(1)}) custom-call(s32[1]{0:T(128)} %bitcast.me_ref.seq_ref, bf16[1024,1024]{1,0:T(8,128)(2,1)} %get-tuple-element.155.refs_0_, bf16[2,1024,1024]{2,1,0:T(8,128)(2,1)} %get-tuple-element.156.refs_1_, ...), custom_call_target="tpu_custom_call" | custom-call | flops 3221225472 | bytes 9437184 | tf_op jit(solution)/shard_map/pallas_call | solution.py:793
  241.4 3.6 %collective-permute-done.42 = bf16[4,64,1152]{2,1,0:T(8,128)(2,1)S(1)} collective-permute-done((bf16[4,64,1152]{2,1,0:T(8,128)(2,1)S(1)}, bf16[4,64,1152]{2,1,0:T(8,128)(2,1)S(1)}, u32[]{:S(2)}, u32[]{:S(2)}) %collective-permute-start.42) | collective-permute-done | bytes 589856 | tf_op jit(solution)/shard_map/ppermute | solution.py:27
  249.7 4.2 %collective-permute-done.43 = bf16[64,1152]{1,0:T(8,128)(2,1)S(1)} collective-permute-done((bf16[64,1152]{1,0:T(8,128)(2,1)S(1)}, bf16[64,1152]{1,0:T(8,128)(2,1)S(1)}, u32[]{:S(2)}, u32[]{:S(2)}) %collective-permute-start.43) | collective-permute-done | bytes 147488 | tf_op jit(solution)/shard_map/ppermute | solution.py:27
  255.7 4.5 %collective-permute-done.44 = bf16[64,1152]{1,0:T(8,128)(2,1)S(1)} collective-permute-done((bf16[64,1152]{1,0:T(8,128)(2,1)S(1)}, bf16[64,1152]{1,0:T(8,128)(2,1)S(1)}, u32[]{:S(2)}, u32[]{:S(2)}) %collective-permute-start.44) | collective-permute-done | bytes 147488 | tf_op jit(solution)/shard_map/ppermute | solution.py:27
  262.6 3.9 %collective-permute-start.50 = (bf16[64,512]{1,0:T(8,128)(2,1)S(1)}, bf16[64,512]{1,0:T(8,128)(2,1)S(1)}, u32[]{:S(2)}, u32[]{:S(2)}) collective-permute-start(bf16[64,512]{1,0:T(8,128)(2,1)S(1)} %get-tuple-element.200), channel_id=1, source_target_pairs={{0,8},{1,9},{2,10},{3,11},{4,12},{5,13},{6,14},{7,15},{8,0},{9,1},... | collective-permute-start | bytes 196616 | tf_op jit(solution)/shard_map/ppermute | solution.py:27
  272.0 3.1 %collective-permute-done.46.refs_1_ = bf16[32,1152]{1,0:T(8,128)(2,1)S(1)} collective-permute-done((bf16[32,1152]{1,0:T(8,128)(2,1)S(1)}, bf16[32,1152]{1,0:T(8,128)(2,1)S(1)}, u32[]{:S(2)}, u32[]{:S(2)}) %collective-permute-start.46) | collective-permute-done | bytes 73760 | tf_op jit(solution)/shard_map/ppermute | solution.py:27
  (250 shorter events, 127.5 us)
Async XLA Ops:
  7.2 77.4 %all-gather.3.cloned.1.call-start = ((), (), s32[]{:S(2)}) async-start(), calls=%async_computation | async-start | bytes 2949120 | tf_op jit(solution)/shard_map/all_gather | solution.py:630
  16.5 17.3 %collective-permute-start.3 = (bf16[64,1152]{1,0:T(8,128)(2,1)S(1)}, bf16[64,1152]{1,0:T(8,128)(2,1)S(1)}, u32[]{:S(2)}, u32[]{:S(2)}) collective-permute-start(bf16[64,1152]{1,0:T(8,128)(2,1)S(1)} %slice.152), channel_id=1, source_target_pairs={{0,4},{1,5},{2,6},{3,7},{4,0},{5,1},{6,2},{7,3},{8,12},{9,13},{10,... | collective-permute-start | bytes 442376 | tf_op jit(solution)/shard_map/ppermute | solution.py:27
  18.3 18.8 %collective-permute-start.2 = (bf16[64,1152]{1,0:T(8,128)(2,1)S(1)}, bf16[64,1152]{1,0:T(8,128)(2,1)S(1)}, u32[]{:S(2)}, u32[]{:S(2)}) collective-permute-start(bf16[64,1152]{1,0:T(8,128)(2,1)S(1)} %slice.152), channel_id=1, source_target_pairs={{0,2},{1,3},{2,0},{3,1},{4,6},{5,7},{6,4},{7,5},{8,10},{9,11},{10,... | collective-permute-start | bytes 442376 | tf_op jit(solution)/shard_map/ppermute | solution.py:27
  35.2 51.0 %collective-permute-start.19 = (bf16[768,1024]{1,0:T(8,128)(2,1)}, bf16[768,1024]{1,0:T(8,128)(2,1)}, u32[]{:S(2)}, u32[]{:S(2)}) collective-permute-start(bf16[768,1024]{1,0:T(8,128)(2,1)} %pad_maximum_fusion.refs_3_), channel_id=1, source_target_pairs={{0,16},{16,0},{1,17},{17,1},{2,18},{18,2},{3,19},{19,3},{4,20},{20... | collective-permute-start | bytes 4718600 | tf_op jit(solution)/shard_map/ppermute | solution.py:27
  49.2 15.7 %collective-permute-start.11 = (bf16[256,512]{1,0:T(8,128)(2,1)S(1)}, bf16[256,512]{1,0:T(8,128)(2,1)S(1)}, u32[]{:S(2)}, u32[]{:S(2)}) collective-permute-start(bf16[256,512]{1,0:T(8,128)(2,1)S(1)} %get-tuple-element.109), channel_id=1, source_target_pairs={{0,2},{1,3},{2,4},{3,5},{4,6},{5,7},{6,8},{7,9},{8,10},{9,11},{10,... | collective-permute-start | bytes 786440 | tf_op jit(solution)/shard_map/ppermute | solution.py:33
  85.8 29.5 %collective-permute-start.20 = (bf16[768,1024]{1,0:T(8,128)(2,1)}, bf16[768,1024]{1,0:T(8,128)(2,1)S(1)}, u32[]{:S(2)}, u32[]{:S(2)}) collective-permute-start(bf16[768,1024]{1,0:T(8,128)(2,1)} %pad_maximum_fusion.refs_3_), channel_id=1, source_target_pairs={{0,1},{1,0},{2,3},{3,2},{4,5},{5,4},{6,7},{7,6},{8,9},{9,8},{10,11... | collective-permute-start | bytes 4718600 | tf_op jit(solution)/shard_map/ppermute | solution.py:27
  86.3 30.4 %collective-permute-start.21 = (bf16[768,1024]{1,0:T(8,128)(2,1)}, bf16[768,1024]{1,0:T(8,128)(2,1)S(1)}, u32[]{:S(2)}, u32[]{:S(2)}) collective-permute-start(bf16[768,1024]{1,0:T(8,128)(2,1)} %collective-permute-done.19.refs_4_), channel_id=1, source_target_pairs={{0,1},{1,0},{2,3},{3,2},{4,5},{5,4},{6,7},{7,6},{8,9},{9,8},{10,11... | collective-permute-start | bytes 4718600 | tf_op jit(solution)/shard_map/ppermute | solution.py:27
  100.8 14.5 %collective-permute-start.15 = (bf16[128,1152]{1,0:T(8,128)(2,1)S(1)}, bf16[128,1152]{1,0:T(8,128)(2,1)S(1)}, u32[]{:S(2)}, u32[]{:S(2)}) collective-permute-start(bf16[128,1152]{1,0:T(8,128)(2,1)S(1)} %get-tuple-element.142.refs_0_), channel_id=1, source_target_pairs={{0,12},{1,13},{2,14},{3,15},{4,8},{5,9},{6,10},{7,11},{8,4},{9,5},... | collective-permute-start | bytes 884744 | tf_op jit(solution)/shard_map/ppermute | solution.py:27
  109.7 45.2 %collective-permute-start.26 = (bf16[128,1152]{1,0:T(8,128)(2,1)S(1)}, bf16[128,1152]{1,0:T(8,128)(2,1)S(1)}, u32[]{:S(2)}, u32[]{:S(2)}) collective-permute-start(bf16[128,1152]{1,0:T(8,128)(2,1)S(1)} %get-tuple-element.142.refs_0_), channel_id=1, source_target_pairs={{0,2},{1,3},{2,0},{3,1},{4,6},{5,7},{6,4},{7,5},{8,10},{9,11},{10,... | collective-permute-start | bytes 884744 | tf_op jit(solution)/shard_map/ppermute | solution.py:27
  115.3 23.0 %collective-permute-start.16 = (bf16[128,1152]{1,0:T(8,128)(2,1)S(1)}, bf16[128,1152]{1,0:T(8,128)(2,1)S(1)}, u32[]{:S(2)}, u32[]{:S(2)}) collective-permute-start(bf16[128,1152]{1,0:T(8,128)(2,1)S(1)} %get-tuple-element.142.refs_0_), channel_id=1, source_target_pairs={{0,8},{1,9},{2,10},{3,11},{4,12},{5,13},{6,14},{7,15},{8,0},{9,1},... | collective-permute-start | bytes 884744 | tf_op jit(solution)/shard_map/ppermute | solution.py:27
  115.3 14.2 %collective-permute-start.22 = (bf16[128,1152]{1,0:T(8,128)(2,1)S(1)}, bf16[128,1152]{1,0:T(8,128)(2,1)S(1)}, u32[]{:S(2)}, u32[]{:S(2)}) collective-permute-start(bf16[128,1152]{1,0:T(8,128)(2,1)S(1)} %collective-permute-done.15.refs_0_), channel_id=1, source_target_pairs={{0,2},{1,3},{2,0},{3,1},{4,6},{5,7},{6,4},{7,5},{8,10},{9,11},{10,... | collective-permute-start | bytes 884744 | tf_op jit(solution)/shard_map/ppermute | solution.py:27
  139.1 42.3 %collective-permute-start.27 = (bf16[128,1152]{1,0:T(8,128)(2,1)S(1)}, bf16[128,1152]{1,0:T(8,128)(2,1)S(1)}, u32[]{:S(2)}, u32[]{:S(2)}) collective-permute-start(bf16[128,1152]{1,0:T(8,128)(2,1)S(1)} %fusion.21), channel_id=1, source_target_pairs={{0,4},{1,5},{2,6},{3,7},{4,0},{5,1},{6,2},{7,3},{8,12},{9,13},{10,... | collective-permute-start | bytes 884744 | tf_op jit(solution)/shard_map/ppermute | solution.py:27
  144.2 37.2 %collective-permute-start.28 = (bf16[128,1152]{1,0:T(8,128)(2,1)S(1)}, bf16[128,1152]{1,0:T(8,128)(2,1)S(1)}, u32[]{:S(2)}, u32[]{:S(2)}) collective-permute-start(bf16[128,1152]{1,0:T(8,128)(2,1)S(1)} %fusion.20), channel_id=1, source_target_pairs={{0,12},{1,13},{2,14},{3,15},{4,8},{5,9},{6,10},{7,11},{8,4},{9,5},... | collective-permute-start | bytes 884744 | tf_op jit(solution)/shard_map/ppermute | solution.py:27
  181.3 35.6 %collective-permute-start.38 = (bf16[2,768,1024]{2,1,0:T(8,128)(2,1)S(1)}, bf16[2,768,1024]{2,1,0:T(8,128)(2,1)S(1)}, u32[]{:S(2)}, u32[]{:S(2)}) collective-permute-start(bf16[2,768,1024]{2,1,0:T(8,128)(2,1)S(1)} %shard_map.267), channel_id=1, source_target_pairs={{0,1},{1,0},{2,3},{3,2},{4,5},{5,4},{6,7},{7,6},{8,9},{9,8},{10,11... | collective-permute-start | bytes 9437192 | tf_op jit(solution)/shard_map/ppermute | solution.py:27
  185.7 28.4 %collective-permute-start.32 = (bf16[4,128,1024]{2,1,0:T(8,128)(2,1)S(1)}, bf16[4,128,1024]{2,1,0:T(8,128)(2,1)S(1)}, u32[]{:S(2)}, u32[]{:S(2)}) collective-permute-start(bf16[4,128,1024]{2,1,0:T(8,128)(2,1)S(1)} %copy-done.18), channel_id=1, source_target_pairs={{0,2},{1,3},{2,0},{3,1},{4,6},{5,7},{6,4},{7,5},{8,10},{9,11},{10,... | collective-permute-start | bytes 3145736 | tf_op jit(solution)/shard_map/ppermute | solution.py:27
  201.2 14.5 %collective-permute-start.37 = (bf16[512,1152]{1,0:T(8,128)(2,1)S(1)}, bf16[512,1152]{1,0:T(8,128)(2,1)S(1)}, u32[]{:S(2)}, u32[]{:S(2)}) collective-permute-start(bf16[512,1152]{1,0:T(8,128)(2,1)S(1)} %get-tuple-element.166), channel_id=1, source_target_pairs={{0,1},{1,0},{2,3},{3,2},{4,5},{5,4},{6,7},{7,6},{8,9},{9,8},{10,11... | collective-permute-start | bytes 3538952 | tf_op jit(solution)/shard_map/ppermute | solution.py:27
  201.3 25.0 %collective-permute-start.39 = (bf16[256,512]{1,0:T(8,128)(2,1)S(1)}, bf16[256,512]{1,0:T(8,128)(2,1)S(1)}, u32[]{:S(2)}, u32[]{:S(2)}) collective-permute-start(bf16[256,512]{1,0:T(8,128)(2,1)S(1)} %get-tuple-element.170), channel_id=1, source_target_pairs={{1,0},{2,1},{3,2},{4,3},{5,4},{6,5},{7,6},{8,7},{9,8},{10,9},{11,1... | collective-permute-start | bytes 786440 | tf_op jit(solution)/shard_map/ppermute | solution.py:33
  202.6 23.7 %collective-permute-start.40 = (bf16[256,512]{1,0:T(8,128)(2,1)S(1)}, bf16[256,512]{1,0:T(8,128)(2,1)S(1)}, u32[]{:S(2)}, u32[]{:S(2)}) collective-permute-start(bf16[256,512]{1,0:T(8,128)(2,1)S(1)} %get-tuple-element.171), channel_id=1, source_target_pairs={{2,0},{3,1},{4,2},{5,3},{6,4},{7,5},{8,6},{9,7},{10,8},{11,9},{12,... | collective-permute-start | bytes 786440 | tf_op jit(solution)/shard_map/ppermute | solution.py:33
  214.6 16.4 %collective-permute-start.33 = (bf16[128,1024]{1,0:T(8,128)(2,1)S(1)}, bf16[128,1024]{1,0:T(8,128)(2,1)S(1)}, u32[]{:S(2)}, u32[]{:S(2)}) collective-permute-start(bf16[128,1024]{1,0:T(8,128)(2,1)S(1)} %get-tuple-element.192), channel_id=1, source_target_pairs={{0,4},{1,5},{2,6},{3,7},{4,0},{5,1},{6,2},{7,3},{8,12},{9,13},{10,... | collective-permute-start | bytes 786440 | tf_op jit(solution)/shard_map/ppermute | solution.py:27
  215.7 18.5 %collective-permute-start.34 = (bf16[128,1024]{1,0:T(8,128)(2,1)S(1)}, bf16[128,1024]{1,0:T(8,128)(2,1)S(1)}, u32[]{:S(2)}, u32[]{:S(2)}) collective-permute-start(bf16[128,1024]{1,0:T(8,128)(2,1)S(1)} %get-tuple-element.194), channel_id=1, source_target_pairs={{0,8},{1,9},{2,10},{3,11},{4,12},{5,13},{6,14},{7,15},{8,0},{9,1},... | collective-permute-start | bytes 786440 | tf_op jit(solution)/shard_map/ppermute | solution.py:27
  216.9 17.3 %collective-permute-start.35 = (bf16[128,1024]{1,0:T(8,128)(2,1)S(1)}, bf16[128,1024]{1,0:T(8,128)(2,1)S(1)}, u32[]{:S(2)}, u32[]{:S(2)}) collective-permute-start(bf16[128,1024]{1,0:T(8,128)(2,1)S(1)} %get-tuple-element.193), channel_id=1, source_target_pairs={{0,12},{1,13},{2,14},{3,15},{4,8},{5,9},{6,10},{7,11},{8,4},{9,5},... | collective-permute-start | bytes 786440 | tf_op jit(solution)/shard_map/ppermute | solution.py:27
  228.5 16.6 %collective-permute-start.42 = (bf16[4,64,1152]{2,1,0:T(8,128)(2,1)S(1)}, bf16[4,64,1152]{2,1,0:T(8,128)(2,1)S(1)}, u32[]{:S(2)}, u32[]{:S(2)}) collective-permute-start(bf16[4,64,1152]{2,1,0:T(8,128)(2,1)S(1)} %slice_bitcast_fusion.2), channel_id=1, source_target_pairs={{0,2},{1,3},{2,0},{3,1},{4,6},{5,7},{6,4},{7,5},{8,10},{9,11},{10,... | collective-permute-start | bytes 1769480 | tf_op jit(solution)/shard_map/ppermute | solution.py:27
  235.1 35.7 %collective-permute-start.54 = (bf16[256,1024]{1,0:T(8,128)(2,1)S(1)}, bf16[256,1024]{1,0:T(8,128)(2,1)S(1)}, u32[]{:S(2)}, u32[]{:S(2)}) collective-permute-start(bf16[256,1024]{1,0:T(8,128)(2,1)S(1)} %bitcast.128), channel_id=1, source_target_pairs={{0,16},{16,0},{1,17},{17,1},{2,18},{18,2},{3,19},{19,3},{4,20},{20... | collective-permute-start | bytes 1572872 | tf_op jit(solution)/shard_map/ppermute | solution.py:27
  236.7 39.7 %collective-permute-start.53 = (bf16[512,1024]{1,0:T(8,128)(2,1)S(1)}, bf16[512,1024]{1,0:T(8,128)(2,1)S(1)}, u32[]{:S(2)}, u32[]{:S(2)}) collective-permute-start(bf16[512,1024]{1,0:T(8,128)(2,1)S(1)} %bitcast.127), channel_id=1, source_target_pairs={{0,16},{16,0},{1,17},{17,1},{2,18},{18,2},{3,19},{19,3},{4,20},{20... | collective-permute-start | bytes 3145736 | tf_op jit(solution)/shard_map/ppermute | solution.py:27
  (69 other events, 635.2 us)
Sparse Core Ops, SparseCore 0:
  16.4 68.1 all-gather.2

commit v5 on v4

--- a/solution.py
+++ b/solution.py
@@ -755,10 +755,10 @@
             ],
         )(blk_scalar, seq_scalar, *[in_hbm(a) for a in operands])
 
-    turns = [1] + list(range(groups - 1, 1, -1)) + [0]
+    turns = [1, 3, 0] + [k for k in range(2, groups) if k != 3]
     far = {0: wide}
     last = wide
-    for k in turns[:-1]:
+    for k in [t for t in turns if t]:
         far[k] = swap_with(after(wide, last), "blk", 4 * k)
         last = far[k] if k > 1 else last
     across = {k: swap_with(far[k], "blk", 2) for k in far}

time: 291 us -> 286 us (0.983)
  waiting for transfers between devices: 113 us -> 110 us
    ppermute x51, waiting for transfers between devices: 90.2 us -> 86.8 us  [swap_with(): return lax.ppermute(value, axis, [(i, i ^ mask) for i in range(count)])]
  transfers between devices with their start and end apart: 56 -> 56, of which waited for: 29 -> 27; matrix products, arithmetic and copies ran while one was open for 5% -> 5% of each run, Pallas kernels for 22% -> 22%
where the time goes in v5:
time: 286 us; the launch traced here: 281 us
  waiting for transfers between devices  110 us (38%)
  starting transfers between devices  69.5 us (24%)
  Pallas kernels  62.9 us (22%)
  between operations  15.2 us (5%)
  local copies, waits for them, and re-layouts  8.77 us (3%)
  other arithmetic  7.97 us (3%)
  matrix products  6.52 us (2%)
    ppermute x51, waiting for transfers between devices, swap_with(): return lax.ppermute(value, axis, [(i, i ^ mask) for i in range(count)])  86.8 us
    ppermute x51, starting transfers between devices, swap_with(): return lax.ppermute(value, axis, [(i, i ^ mask) for i in range(count)])  61.3 us
    pallas_call x4, Pallas kernels, run_experts(): call(functools.partial(expert_body, experts, k, seqs), tuple((pltpu.HBM(d...  26.9 us
    all_gather x1, waiting for transfers between devices, per_device(): lax.all_gather(jnp.concatenate([cot, out_own], axis=0), 'blk', axis=0, ax...  13 us
    pallas_call x2, Pallas kernels, expert_grads(): call(functools.partial(expert_grads_body, e, seqs), outs, limit=10 + 7 *...  12.8 us
    ppermute x4, waiting for transfers between devices, shifted(): lax.ppermute(value, axis, [(i, i + steps) for i in range(leading, last)])  10 us
    ppermute x4, starting transfers between devices, shifted(): lax.ppermute(value, axis, [(i, i + steps) for i in range(leading, last)])  8.21 us
    pallas_call x1, Pallas kernels, per_device(): call(functools.partial(attend_back_body, scale), (shape_of((rows, q_cols)...  7.98 us
  transfers between devices with their start and end apart: 56, of which 27 were waited for; matrix products, arithmetic and copies ran while one was open for 5% of the time, Pallas kernels for 22%

profile of v5, /device:TPU:0, one launch (start us, length us, event | category | flops | bytes accessed | tf_op | source)
XLA Modules:
  0.0 280.7 jit_solution(3203876110617627858)
XLA Ops:
  40.8 4.6 %collective-permute-done.9 = bf16[64,1152]{1,0:T(8,128)(2,1)S(1)} collective-permute-done((bf16[64,1152]{1,0:T(8,128)(2,1)S(1)}, bf16[64,1152]{1,0:T(8,128)(2,1)S(1)}, u32[]{:S(2)}, u32[]{:S(2)}) %collective-permute-start.9) | collective-permute-done | bytes 147488 | tf_op jit(solution)/shard_map/ppermute | solution.py:27
  49.2 3.5 %collective-permute-start.11 = (bf16[256,512]{1,0:T(8,128)(2,1)S(1)}, bf16[256,512]{1,0:T(8,128)(2,1)S(1)}, u32[]{:S(2)}, u32[]{:S(2)}) collective-permute-start(bf16[256,512]{1,0:T(8,128)(2,1)S(1)} %get-tuple-element.109), channel_id=1, source_target_pairs={{0,2},{1,3},{2,4},{3,5},{4,6},{5,7},{6,8},{7,9},{8,10},{9,11},{10,... | collective-permute-start | bytes 786440 | tf_op jit(solution)/shard_map/ppermute | solution.py:33
  55.0 10.0 %collective-permute-done.11 = bf16[256,512]{1,0:T(8,128)(2,1)S(1)} collective-permute-done((bf16[256,512]{1,0:T(8,128)(2,1)S(1)}, bf16[256,512]{1,0:T(8,128)(2,1)S(1)}, u32[]{:S(2)}, u32[]{:S(2)}) %collective-permute-start.11) | collective-permute-done | bytes 262176 | tf_op jit(solution)/shard_map/ppermute | solution.py:33
  65.1 4.8 %shard_map.258 = (bf16[256,512]{1,0:T(8,128)(2,1)S(1)}, f32[256,512]{1,0:T(8,128)S(1)}) custom-call(bf16[256,512]{1,0:T(8,128)(2,1)S(1)} %get-tuple-element.108.q_ref, bf16[768,512]{1,0:T(8,128)(2,1)S(1)} %constant_dynamic-update-slice_fusion.6.kv_ref, f32[8,768]{1,0:T(8,128)S(1)} %maximum_maximum_fusion.1.meta_q.meta_k, ...), custom_call_target="tpu_custom_call" | custom-call | bytes 1572864 | tf_op jit(solution)/shard_map/pallas_call | solution.py:688
  71.6 13.0 %all-gather.3.cloned.1.call-done = bf16[1280,1024]{1,0:T(8,128)(2,1)} async-done(((bf16[160,1024]{1,0:T(8,128)(2,1)}), bf16[1280,1024]{1,0:T(8,128)(2,1)}) %all-gather.3.cloned.1.call-update) | async-done | bytes 2621456 | tf_op jit(solution)/shard_map/all_gather | solution.py:630
  92.4 6.5 %collective-permute-done.14.refs_1_ = bf16[128,1024]{1,0:T(8,128)(2,1)S(1)} collective-permute-done((bf16[128,1024]{1,0:T(8,128)(2,1)S(1)}, bf16[128,1024]{1,0:T(8,128)(2,1)S(1)}, u32[]{:S(2)}, u32[]{:S(2)}) %collective-permute-start.14) | collective-permute-done | bytes 262176 | tf_op jit(solution)/shard_map/ppermute | solution.py:27
  102.7 6.0 %collective-permute-done.17.refs_0_ = bf16[128,1152]{1,0:T(8,128)(2,1)S(1)} collective-permute-done((bf16[128,1152]{1,0:T(8,128)(2,1)S(1)}, bf16[128,1152]{1,0:T(8,128)(2,1)S(1)}, u32[]{:S(2)}, u32[]{:S(2)}) %collective-permute-start.17) | collective-permute-done | bytes 294944 | tf_op jit(solution)/shard_map/ppermute | solution.py:27
  110.7 4.6 %collective-permute-done.15.refs_0_ = bf16[128,1152]{1,0:T(8,128)(2,1)S(1)} collective-permute-done((bf16[128,1152]{1,0:T(8,128)(2,1)S(1)}, bf16[128,1152]{1,0:T(8,128)(2,1)S(1)}, u32[]{:S(2)}, u32[]{:S(2)}) %collective-permute-start.15) | collective-permute-done | bytes 294944 | tf_op jit(solution)/shard_map/ppermute | solution.py:27
  119.3 6.7 %shard_map.262 = (bf16[4,128,1024]{2,1,0:T(8,128)(2,1)}, bf16[4,128,1024]{2,1,0:T(8,128)(2,1)}, bf16[1024,1024]{1,0:T(8,128)(2,1)}, bf16[2,1024,512]{2,1,0:T(8,1...) custom-call(s32[1]{0:T(128)} %bitcast.8.blk_ref.me_ref, ...), custom_call_target="tpu_custom_call" | custom-call | flops 3221225472 | bytes 30539776 | tf_op jit(solution)/shard_map/pallas_call | solution.py:736
  130.2 6.7 %shard_map.263 = (bf16[4,128,1024]{2,1,0:T(8,128)(2,1)}, bf16[4,128,1024]{2,1,0:T(8,128)(2,1)}, bf16[1024,1024]{1,0:T(8,128)(2,1)}, bf16[2,1024,512]{2,1,0:T(8,1...) custom-call(s32[1]{0:T(128)} %bitcast.8.blk_ref.me_ref, ...), custom_call_target="tpu_custom_call", output_to_operand_aliasing={{0}: (9, {}), {1}: (10, {}), {2}: (11, {}), {3}: (12, {}), ... | custom-call | flops 3221225472 | bytes 30539776 | tf_op jit(solution)/shard_map/pallas_call | solution.py:736
  139.4 4.7 %collective-permute-done.25 = bf16[128,1152]{1,0:T(8,128)(2,1)S(1)} collective-permute-done((bf16[128,1152]{1,0:T(8,128)(2,1)S(1)}, bf16[128,1152]{1,0:T(8,128)(2,1)S(1)}, u32[]{:S(2)}, u32[]{:S(2)}) %collective-permute-start.25) | collective-permute-done | bytes 294944 | tf_op jit(solution)/shard_map/ppermute | solution.py:27
  146.9 6.9 %shard_map.264 = (bf16[4,128,1024]{2,1,0:T(8,128)(2,1)}, bf16[4,128,1024]{2,1,0:T(8,128)(2,1)}, bf16[1024,1024]{1,0:T(8,128)(2,1)}, bf16[2,1024,512]{2,1,0:T(8,1...) custom-call(s32[1]{0:T(128)} %bitcast.8.blk_ref.me_ref, ...), custom_call_target="tpu_custom_call", output_to_operand_aliasing={{0}: (9, {}), {1}: (10, {}), {2}: (11, {}), {3}: (12, {}), ... | custom-call | flops 3221225472 | bytes 30539776 | tf_op jit(solution)/shard_map/pallas_call | solution.py:736
  154.6 6.7 %shard_map.265 = (bf16[4,128,1024]{2,1,0:T(8,128)(2,1)}, bf16[4,128,1024]{2,1,0:T(8,128)(2,1)}, bf16[1024,1024]{1,0:T(8,128)(2,1)}, bf16[2,1024,512]{2,1,0:T(8,1...) custom-call(s32[1]{0:T(128)} %bitcast.8.blk_ref.me_ref, ...), custom_call_target="tpu_custom_call", output_to_operand_aliasing={{0}: (9, {}), {1}: (10, {}), {2}: (11, {}), {3}: (12, {}), ... | custom-call | flops 3221225472 | bytes 30539776 | tf_op jit(solution)/shard_map/pallas_call | solution.py:736
  163.5 4.6 %collective-permute-done.30 = bf16[128,1152]{1,0:T(8,128)(2,1)S(1)} collective-permute-done((bf16[128,1152]{1,0:T(8,128)(2,1)S(1)}, bf16[128,1152]{1,0:T(8,128)(2,1)S(1)}, u32[]{:S(2)}, u32[]{:S(2)}) %collective-permute-start.30) | collective-permute-done | bytes 294944 | tf_op jit(solution)/shard_map/ppermute | solution.py:27
  169.3 6.0 %shard_map.267 = bf16[2,768,1024]{2,1,0:T(8,128)(2,1)S(1)} custom-call(s32[1]{0:T(128)} %bitcast.me_ref.seq_ref, bf16[1024,1024]{1,0:T(8,128)(2,1)} %get-tuple-element.155.refs_0_, bf16[2,1024,1024]{2,1,0:T(8,128)(2,1)} %get-tuple-element.156.refs_1_, bf16[2,1024,512]{2,1,0:T(8,128)(2,1)} %get-tuple-element.157.refs_2_, ...), custom_call_target="tpu_custom_call" | custom-call | flops 3221225472 | bytes 6291456 | tf_op jit(solution)/shard_map/pallas_call | solution.py:793
  175.5 3.5 %collective-permute-done.31.refs_3_ = bf16[128,1152]{1,0:T(8,128)(2,1)S(1)} collective-permute-done((bf16[128,1152]{1,0:T(8,128)(2,1)S(1)}, bf16[128,1152]{1,0:T(8,128)(2,1)S(1)}, u32[]{:S(2)}, u32[]{:S(2)}) %collective-permute-start.31) | collective-permute-done | bytes 294944 | tf_op jit(solution)/shard_map/ppermute | solution.py:27
  186.6 8.0 %shard_map.268 = (bf16[256,512]{1,0:T(8,128)(2,1)S(1)}, bf16[256,512]{1,0:T(8,128)(2,1)S(1)}, bf16[256,512]{1,0:T(8,128)(2,1)S(1)}, f32[256,512]{1,0:T(8,128)S(1)}) custom-call(bf16[256,512]{1,0:T(8,128)(2,1)S(1)} %copy-done.8, bf16[768,512]{1,0:T(8,128)(2,1)S(1)} %copy-done.1, bf16[256,512]{1,0:T(8,128)(2,1)S(1)} %get-tuple-element.110.mixed_ref.mixed, ...), custom_call_target="tpu_custom_call" | custom-call | flops 2415919104 | bytes 2621440 | tf_op jit(solution)/shard_map/pallas_call | solution.py:811
  199.1 9.9 %collective-permute-done.32 = bf16[4,128,1024]{2,1,0:T(8,128)(2,1)S(1)} collective-permute-done((bf16[4,128,1024]{2,1,0:T(8,128)(2,1)S(1)}, bf16[4,128,1024]{2,1,0:T(8,128)(2,1)S(1)}, u32[]{:S(2)}, u32[]{:S(2)}) %collective-permute-start.32) | collective-permute-done | bytes 1048608 | tf_op jit(solution)/shard_map/ppermute | solution.py:27
  214.4 6.8 %shard_map.270 = (f32[512,1024]{1,0:T(8,128)S(1)}, f32[256,1024]{1,0:T(8,128)S(1)}, bf16[1,512,1024]{2,1,0:T(8,128)(2,1)S(1)}, bf16[1,256,1024]{2,1,0:T(8,128)(2,1)S(1)}) custom-call(s32[1]{0:T(128)} %bitcast.me_ref.seq_ref, bf16[1024,1024]{1,0:T(8,128)(2,1)} %get-tuple-element.155.refs_0_, bf16[2,1024,1024]{2,1,0:T(8,128)(2,1)} %get-tuple-element.156.refs_1_, ...), custom_call_target="tpu_custom_call" | custom-call | flops 3221225472 | bytes 9437184 | tf_op jit(solution)/shard_map/pallas_call | solution.py:793
  226.1 4.2 %collective-permute-done.34 = bf16[128,1024]{1,0:T(8,128)(2,1)S(1)} collective-permute-done((bf16[128,1024]{1,0:T(8,128)(2,1)S(1)}, bf16[128,1024]{1,0:T(8,128)(2,1)S(1)}, u32[]{:S(2)}, u32[]{:S(2)}) %collective-permute-start.34) | collective-permute-done | bytes 262176 | tf_op jit(solution)/shard_map/ppermute | solution.py:27
  236.4 3.6 %collective-permute-done.42 = bf16[4,64,1152]{2,1,0:T(8,128)(2,1)S(1)} collective-permute-done((bf16[4,64,1152]{2,1,0:T(8,128)(2,1)S(1)}, bf16[4,64,1152]{2,1,0:T(8,128)(2,1)S(1)}, u32[]{:S(2)}, u32[]{:S(2)}) %collective-permute-start.42) | collective-permute-done | bytes 589856 | tf_op jit(solution)/shard_map/ppermute | solution.py:27
  244.8 4.2 %collective-permute-done.43 = bf16[64,1152]{1,0:T(8,128)(2,1)S(1)} collective-permute-done((bf16[64,1152]{1,0:T(8,128)(2,1)S(1)}, bf16[64,1152]{1,0:T(8,128)(2,1)S(1)}, u32[]{:S(2)}, u32[]{:S(2)}) %collective-permute-start.43) | collective-permute-done | bytes 147488 | tf_op jit(solution)/shard_map/ppermute | solution.py:27
  250.7 5.2 %collective-permute-done.44 = bf16[64,1152]{1,0:T(8,128)(2,1)S(1)} collective-permute-done((bf16[64,1152]{1,0:T(8,128)(2,1)S(1)}, bf16[64,1152]{1,0:T(8,128)(2,1)S(1)}, u32[]{:S(2)}, u32[]{:S(2)}) %collective-permute-start.44) | collective-permute-done | bytes 147488 | tf_op jit(solution)/shard_map/ppermute | solution.py:27
  258.2 4.2 %collective-permute-start.50 = (bf16[64,512]{1,0:T(8,128)(2,1)S(1)}, bf16[64,512]{1,0:T(8,128)(2,1)S(1)}, u32[]{:S(2)}, u32[]{:S(2)}) collective-permute-start(bf16[64,512]{1,0:T(8,128)(2,1)S(1)} %get-tuple-element.200), channel_id=1, source_target_pairs={{0,8},{1,9},{2,10},{3,11},{4,12},{5,13},{6,14},{7,15},{8,0},{9,1},... | collective-permute-start | bytes 196616 | tf_op jit(solution)/shard_map/ppermute | solution.py:27
  (250 shorter events, 120.7 us)
Async XLA Ops:
  7.2 77.4 %all-gather.3.cloned.1.call-start = ((), (), s32[]{:S(2)}) async-start(), calls=%async_computation | async-start | bytes 2949120 | tf_op jit(solution)/shard_map/all_gather | solution.py:630
  16.5 17.3 %collective-permute-start.3 = (bf16[64,1152]{1,0:T(8,128)(2,1)S(1)}, bf16[64,1152]{1,0:T(8,128)(2,1)S(1)}, u32[]{:S(2)}, u32[]{:S(2)}) collective-permute-start(bf16[64,1152]{1,0:T(8,128)(2,1)S(1)} %slice.152), channel_id=1, source_target_pairs={{0,4},{1,5},{2,6},{3,7},{4,0},{5,1},{6,2},{7,3},{8,12},{9,13},{10,... | collective-permute-start | bytes 442376 | tf_op jit(solution)/shard_map/ppermute | solution.py:27
  18.3 18.8 %collective-permute-start.2 = (bf16[64,1152]{1,0:T(8,128)(2,1)S(1)}, bf16[64,1152]{1,0:T(8,128)(2,1)S(1)}, u32[]{:S(2)}, u32[]{:S(2)}) collective-permute-start(bf16[64,1152]{1,0:T(8,128)(2,1)S(1)} %slice.152), channel_id=1, source_target_pairs={{0,2},{1,3},{2,0},{3,1},{4,6},{5,7},{6,4},{7,5},{8,10},{9,11},{10,... | collective-permute-start | bytes 442376 | tf_op jit(solution)/shard_map/ppermute | solution.py:27
  35.2 51.0 %collective-permute-start.19 = (bf16[768,1024]{1,0:T(8,128)(2,1)}, bf16[768,1024]{1,0:T(8,128)(2,1)}, u32[]{:S(2)}, u32[]{:S(2)}) collective-permute-start(bf16[768,1024]{1,0:T(8,128)(2,1)} %pad_maximum_fusion.refs_3_), channel_id=1, source_target_pairs={{0,16},{16,0},{1,17},{17,1},{2,18},{18,2},{3,19},{19,3},{4,20},{20... | collective-permute-start | bytes 4718600 | tf_op jit(solution)/shard_map/ppermute | solution.py:27
  49.2 15.7 %collective-permute-start.11 = (bf16[256,512]{1,0:T(8,128)(2,1)S(1)}, bf16[256,512]{1,0:T(8,128)(2,1)S(1)}, u32[]{:S(2)}, u32[]{:S(2)}) collective-permute-start(bf16[256,512]{1,0:T(8,128)(2,1)S(1)} %get-tuple-element.109), channel_id=1, source_target_pairs={{0,2},{1,3},{2,4},{3,5},{4,6},{5,7},{6,8},{7,9},{8,10},{9,11},{10,... | collective-permute-start | bytes 786440 | tf_op jit(solution)/shard_map/ppermute | solution.py:33
  85.8 29.5 %collective-permute-start.20 = (bf16[768,1024]{1,0:T(8,128)(2,1)}, bf16[768,1024]{1,0:T(8,128)(2,1)S(1)}, u32[]{:S(2)}, u32[]{:S(2)}) collective-permute-start(bf16[768,1024]{1,0:T(8,128)(2,1)} %pad_maximum_fusion.refs_3_), channel_id=1, source_target_pairs={{0,1},{1,0},{2,3},{3,2},{4,5},{5,4},{6,7},{7,6},{8,9},{9,8},{10,11... | collective-permute-start | bytes 4718600 | tf_op jit(solution)/shard_map/ppermute | solution.py:27
  86.3 30.4 %collective-permute-start.21 = (bf16[768,1024]{1,0:T(8,128)(2,1)}, bf16[768,1024]{1,0:T(8,128)(2,1)S(1)}, u32[]{:S(2)}, u32[]{:S(2)}) collective-permute-start(bf16[768,1024]{1,0:T(8,128)(2,1)} %collective-permute-done.19.refs_4_), channel_id=1, source_target_pairs={{0,1},{1,0},{2,3},{3,2},{4,5},{5,4},{6,7},{7,6},{8,9},{9,8},{10,11... | collective-permute-start | bytes 4718600 | tf_op jit(solution)/shard_map/ppermute | solution.py:27
  100.8 14.5 %collective-permute-start.15 = (bf16[128,1152]{1,0:T(8,128)(2,1)S(1)}, bf16[128,1152]{1,0:T(8,128)(2,1)S(1)}, u32[]{:S(2)}, u32[]{:S(2)}) collective-permute-start(bf16[128,1152]{1,0:T(8,128)(2,1)S(1)} %get-tuple-element.134.refs_0_), channel_id=1, source_target_pairs={{0,12},{1,13},{2,14},{3,15},{4,8},{5,9},{6,10},{7,11},{8,4},{9,5},... | collective-permute-start | bytes 884744 | tf_op jit(solution)/shard_map/ppermute | solution.py:27
  109.7 36.5 %collective-permute-start.24 = (bf16[128,1152]{1,0:T(8,128)(2,1)S(1)}, bf16[128,1152]{1,0:T(8,128)(2,1)S(1)}, u32[]{:S(2)}, u32[]{:S(2)}) collective-permute-start(bf16[128,1152]{1,0:T(8,128)(2,1)S(1)} %get-tuple-element.134.refs_0_), channel_id=1, source_target_pairs={{0,2},{1,3},{2,0},{3,1},{4,6},{5,7},{6,4},{7,5},{8,10},{9,11},{10,... | collective-permute-start | bytes 884744 | tf_op jit(solution)/shard_map/ppermute | solution.py:27
  115.3 22.9 %collective-permute-start.16 = (bf16[128,1152]{1,0:T(8,128)(2,1)S(1)}, bf16[128,1152]{1,0:T(8,128)(2,1)S(1)}, u32[]{:S(2)}, u32[]{:S(2)}) collective-permute-start(bf16[128,1152]{1,0:T(8,128)(2,1)S(1)} %get-tuple-element.134.refs_0_), channel_id=1, source_target_pairs={{0,8},{1,9},{2,10},{3,11},{4,12},{5,13},{6,14},{7,15},{8,0},{9,1},... | collective-permute-start | bytes 884744 | tf_op jit(solution)/shard_map/ppermute | solution.py:27
  138.2 15.6 %collective-permute-start.26 = (bf16[128,1152]{1,0:T(8,128)(2,1)S(1)}, bf16[128,1152]{1,0:T(8,128)(2,1)S(1)}, u32[]{:S(2)}, u32[]{:S(2)}) collective-permute-start(bf16[128,1152]{1,0:T(8,128)(2,1)S(1)} %collective-permute-done.16.refs_0_), channel_id=1, source_target_pairs={{0,2},{1,3},{2,0},{3,1},{4,6},{5,7},{6,4},{7,5},{8,10},{9,11},{10,... | collective-permute-start | bytes 884744 | tf_op jit(solution)/shard_map/ppermute | solution.py:27
  139.1 36.4 %collective-permute-start.27 = (bf16[128,1152]{1,0:T(8,128)(2,1)S(1)}, bf16[128,1152]{1,0:T(8,128)(2,1)S(1)}, u32[]{:S(2)}, u32[]{:S(2)}) collective-permute-start(bf16[128,1152]{1,0:T(8,128)(2,1)S(1)} %fusion.21), channel_id=1, source_target_pairs={{0,4},{1,5},{2,6},{3,7},{4,0},{5,1},{6,2},{7,3},{8,12},{9,13},{10,... | collective-permute-start | bytes 884744 | tf_op jit(solution)/shard_map/ppermute | solution.py:27
  144.2 31.3 %collective-permute-start.28 = (bf16[128,1152]{1,0:T(8,128)(2,1)S(1)}, bf16[128,1152]{1,0:T(8,128)(2,1)S(1)}, u32[]{:S(2)}, u32[]{:S(2)}) collective-permute-start(bf16[128,1152]{1,0:T(8,128)(2,1)S(1)} %fusion.20), channel_id=1, source_target_pairs={{0,12},{1,13},{2,14},{3,15},{4,8},{5,9},{6,10},{7,11},{8,4},{9,5},... | collective-permute-start | bytes 884744 | tf_op jit(solution)/shard_map/ppermute | solution.py:27
  175.3 37.2 %collective-permute-start.38 = (bf16[2,768,1024]{2,1,0:T(8,128)(2,1)S(1)}, bf16[2,768,1024]{2,1,0:T(8,128)(2,1)S(1)}, u32[]{:S(2)}, u32[]{:S(2)}) collective-permute-start(bf16[2,768,1024]{2,1,0:T(8,128)(2,1)S(1)} %shard_map.267), channel_id=1, source_target_pairs={{0,1},{1,0},{2,3},{3,2},{4,5},{5,4},{6,7},{7,6},{8,9},{9,8},{10,11... | collective-permute-start | bytes 9437192 | tf_op jit(solution)/shard_map/ppermute | solution.py:27
  181.2 27.8 %collective-permute-start.32 = (bf16[4,128,1024]{2,1,0:T(8,128)(2,1)S(1)}, bf16[4,128,1024]{2,1,0:T(8,128)(2,1)S(1)}, u32[]{:S(2)}, u32[]{:S(2)}) collective-permute-start(bf16[4,128,1024]{2,1,0:T(8,128)(2,1)S(1)} %copy-done.18), channel_id=1, source_target_pairs={{0,2},{1,3},{2,0},{3,1},{4,6},{5,7},{6,4},{7,5},{8,10},{9,11},{10,... | collective-permute-start | bytes 3145736 | tf_op jit(solution)/shard_map/ppermute | solution.py:27
  196.4 15.1 %collective-permute-start.37 = (bf16[512,1152]{1,0:T(8,128)(2,1)S(1)}, bf16[512,1152]{1,0:T(8,128)(2,1)S(1)}, u32[]{:S(2)}, u32[]{:S(2)}) collective-permute-start(bf16[512,1152]{1,0:T(8,128)(2,1)S(1)} %get-tuple-element.166), channel_id=1, source_target_pairs={{0,1},{1,0},{2,3},{3,2},{4,5},{5,4},{6,7},{7,6},{8,9},{9,8},{10,11... | collective-permute-start | bytes 3538952 | tf_op jit(solution)/shard_map/ppermute | solution.py:27
  196.5 24.7 %collective-permute-start.39 = (bf16[256,512]{1,0:T(8,128)(2,1)S(1)}, bf16[256,512]{1,0:T(8,128)(2,1)S(1)}, u32[]{:S(2)}, u32[]{:S(2)}) collective-permute-start(bf16[256,512]{1,0:T(8,128)(2,1)S(1)} %get-tuple-element.170), channel_id=1, source_target_pairs={{1,0},{2,1},{3,2},{4,3},{5,4},{6,5},{7,6},{8,7},{9,8},{10,9},{11,1... | collective-permute-start | bytes 786440 | tf_op jit(solution)/shard_map/ppermute | solution.py:33
  197.8 23.4 %collective-permute-start.40 = (bf16[256,512]{1,0:T(8,128)(2,1)S(1)}, bf16[256,512]{1,0:T(8,128)(2,1)S(1)}, u32[]{:S(2)}, u32[]{:S(2)}) collective-permute-start(bf16[256,512]{1,0:T(8,128)(2,1)S(1)} %get-tuple-element.171), channel_id=1, source_target_pairs={{2,0},{3,1},{4,2},{5,3},{6,4},{7,5},{8,6},{9,7},{10,8},{11,9},{12,... | collective-permute-start | bytes 786440 | tf_op jit(solution)/shard_map/ppermute | solution.py:33
  209.4 16.7 %collective-permute-start.33 = (bf16[128,1024]{1,0:T(8,128)(2,1)S(1)}, bf16[128,1024]{1,0:T(8,128)(2,1)S(1)}, u32[]{:S(2)}, u32[]{:S(2)}) collective-permute-start(bf16[128,1024]{1,0:T(8,128)(2,1)S(1)} %get-tuple-element.192), channel_id=1, source_target_pairs={{0,4},{1,5},{2,6},{3,7},{4,0},{5,1},{6,2},{7,3},{8,12},{9,13},{10,... | collective-permute-start | bytes 786440 | tf_op jit(solution)/shard_map/ppermute | solution.py:27
  211.5 18.7 %collective-permute-start.34 = (bf16[128,1024]{1,0:T(8,128)(2,1)S(1)}, bf16[128,1024]{1,0:T(8,128)(2,1)S(1)}, u32[]{:S(2)}, u32[]{:S(2)}) collective-permute-start(bf16[128,1024]{1,0:T(8,128)(2,1)S(1)} %get-tuple-element.194), channel_id=1, source_target_pairs={{0,8},{1,9},{2,10},{3,11},{4,12},{5,13},{6,14},{7,15},{8,0},{9,1},... | collective-permute-start | bytes 786440 | tf_op jit(solution)/shard_map/ppermute | solution.py:27
  212.5 17.8 %collective-permute-start.35 = (bf16[128,1024]{1,0:T(8,128)(2,1)S(1)}, bf16[128,1024]{1,0:T(8,128)(2,1)S(1)}, u32[]{:S(2)}, u32[]{:S(2)}) collective-permute-start(bf16[128,1024]{1,0:T(8,128)(2,1)S(1)} %get-tuple-element.193), channel_id=1, source_target_pairs={{0,12},{1,13},{2,14},{3,15},{4,8},{5,9},{6,10},{7,11},{8,4},{9,5},... | collective-permute-start | bytes 786440 | tf_op jit(solution)/shard_map/ppermute | solution.py:27
  223.4 16.7 %collective-permute-start.42 = (bf16[4,64,1152]{2,1,0:T(8,128)(2,1)S(1)}, bf16[4,64,1152]{2,1,0:T(8,128)(2,1)S(1)}, u32[]{:S(2)}, u32[]{:S(2)}) collective-permute-start(bf16[4,64,1152]{2,1,0:T(8,128)(2,1)S(1)} %slice_bitcast_fusion.2), channel_id=1, source_target_pairs={{0,2},{1,3},{2,0},{3,1},{4,6},{5,7},{6,4},{7,5},{8,10},{9,11},{10,... | collective-permute-start | bytes 1769480 | tf_op jit(solution)/shard_map/ppermute | solution.py:27
  231.2 35.7 %collective-permute-start.54 = (bf16[256,1024]{1,0:T(8,128)(2,1)S(1)}, bf16[256,1024]{1,0:T(8,128)(2,1)S(1)}, u32[]{:S(2)}, u32[]{:S(2)}) collective-permute-start(bf16[256,1024]{1,0:T(8,128)(2,1)S(1)} %bitcast.128), channel_id=1, source_target_pairs={{0,16},{16,0},{1,17},{17,1},{2,18},{18,2},{3,19},{19,3},{4,20},{20... | collective-permute-start | bytes 1572872 | tf_op jit(solution)/shard_map/ppermute | solution.py:27
  232.7 39.0 %collective-permute-start.53 = (bf16[512,1024]{1,0:T(8,128)(2,1)S(1)}, bf16[512,1024]{1,0:T(8,128)(2,1)S(1)}, u32[]{:S(2)}, u32[]{:S(2)}) collective-permute-start(bf16[512,1024]{1,0:T(8,128)(2,1)S(1)} %bitcast.127), channel_id=1, source_target_pairs={{0,16},{16,0},{1,17},{17,1},{2,18},{18,2},{3,19},{19,3},{4,20},{20... | collective-permute-start | bytes 3145736 | tf_op jit(solution)/shard_map/ppermute | solution.py:27
  (69 other events, 649.9 us)
Sparse Core Ops, SparseCore 0:
  16.4 68.1 all-gather.2
